TPU v7x, 32 devices: a whole 2x2x4 slice. The times are simulated.
32 devices in a mesh: groups: 2 (over y), dp: 4 (over x, core), ctx: 4 (over z).
Axes of the slice: x: 2, y: 2, z: 4, core: 2. Of those that a mesh axis runs over, the one named last changes fastest.
Arguments:
- normed_input: bfloat16 [8, 1024, 4096], P(('groups', 'dp'), 'ctx'), parts along dimension 0, may hold values from -6 to 6
- query_weight: bfloat16 [4096, 1024], P(('dp', 'ctx')), may hold values from -0.09375 to 0.09375
- key_vectors: bfloat16 [8, 1024, 1024], P(('groups', 'dp'), 'ctx'), parts along dimension 0, may hold values from -6 to 6
- value_vectors: bfloat16 [8, 1024, 1024], P(('groups', 'dp'), 'ctx'), parts along dimension 0, may hold values from -6 to 6
- input_gate: float32 [8, 4, 1024], P(('groups', 'dp'), None, 'ctx'), parts along dimension 0, may hold values from -16 to 210
- forget_gate: float32 [8, 4, 1024], P(('groups', 'dp'), None, 'ctx'), parts along dimension 0
- resets: int32 [8, 1024], P(('groups', 'dp'), 'ctx'), parts along dimension 0, may hold values 0 or 1
Outputs:
- hidden: bfloat16 [8, 1024, 1024], P(('groups', 'dp'), 'ctx'), parts along dimension 0
There are 2 independent parts, one for each index of `groups`. A program takes and returns all parts, laid end to end along the dimension named above; an argument that names none is the same for every part. Nothing has to cross between parts.
Inputs may be any that keep to these rules, and one draw needn't show every extreme that they name: `resets`: 1 where a new document begins at that position.
All inputs are finite; a program needn't handle non-finite values. No bound on the sum of `resets` on one device may be relied on, other than what follows from the above.
Results may differ from a plain program's by a relative error of at most 0.009.
Values may be sent and summed in bfloat16 or wider, within the bound.
No kernel may reach another device: no remote copies, remote signals or barrier semaphores. Data moves between devices by JAX's collectives and lax.ppermute only.
A program may use at most 128 MiB of HBM per device.

v0:
```python
import functools

import jax
import jax.numpy as jnp
from jax import lax
from jax.experimental import pallas as pl
from jax.experimental.pallas import tpu as pltpu
from jax.sharding import PartitionSpec as P


very_low = -1e30
AXES = ("groups", "dp", "ctx")
CORES = 2
EXTRA = 16
f32 = jnp.float32
bf16 = jnp.bfloat16


def moves(mesh, where):
    ng, nd, nz = (mesh.shape[a] for a in AXES)
    pairs = []
    for g in range(ng):
        for x in range(nd // CORES):
            for k in range(CORES):
                for z in range(nz):
                    to = where(g, x, k, z)
                    if to is not None:
                        g2, x2, k2, z2 = to
                        source = (g * nd + x * CORES + k) * nz + z
                        pairs.append((source, (g2 * nd + x2 * CORES + k2) * nz + z2))
    return pairs


def lane_scan(values):
    length = values.shape[1]
    lane = lax.broadcasted_iota(jnp.int32, values.shape, 1)
    step = 1
    while step < length:
        moved = pltpu.roll(values, step, 1)
        values = values + jnp.where(lane >= step, moved, jnp.zeros_like(values))
        step *= 2
    return values


def log_sigmoid(x):
    return jnp.minimum(x, 0.0) - jnp.log1p(jnp.exp(-jnp.abs(x)))


def padded(values):
    rows = values.shape[0]
    if rows % 8 == 0:
        return values
    fill = jnp.zeros((8 - rows % 8, values.shape[1]), values.dtype)
    return jnp.concatenate([values, fill], axis=0)


def split_rows(value):
    high = value.astype(bf16)
    rest = value - high.astype(f32)
    mid = rest.astype(bf16)
    low = (rest - mid.astype(f32)).astype(bf16)
    return high, mid, low


def store_message(out_ref, base, size, memory, normer, top):
    out_ref[base : base + size, :] = memory.astype(bf16)
    n_parts = split_rows(normer)
    t_parts = split_rows(jnp.broadcast_to(top, normer.shape))
    row = lax.broadcasted_iota(jnp.int32, (EXTRA, normer.shape[1]), 0)
    block = jnp.zeros((EXTRA, normer.shape[1]), f32)
    for i, part in enumerate(n_parts + t_parts):
        block = jnp.where(row == i, part.astype(f32), block)
    out_ref[base + size : base + size + EXTRA, :] = block.astype(bf16)


def load_message(ref, base, size):
    extra = ref[base + size : base + size + EXTRA, :].astype(f32)
    normer = extra[0:1] + extra[1:2] + extra[2:3]
    top = extra[3:4, 0:1] + extra[4:5, 0:1] + extra[5:6, 0:1]
    return ref[base : base + size, :], normer, top


def prepare_kernel(heads, ng, nx, *refs):
    k_ref, v_ref, x_ref, w_ref, gate_ref, forget_ref, reset_ref = refs[:7]
    wsend_ref, xown_ref = refs[7:9]
    xaway = refs[9 : 8 + nx]
    chunks = refs[8 + nx : 8 + nx + 3 * ng]
    kbuf, vbuf, sems = refs[8 + nx + 3 * ng :]
    length = k_ref.shape[0]
    size, vsize = k_ref.shape[1] // heads, v_ref.shape[1] // heads
    group, dp = lax.axis_index("groups"), lax.axis_index("dp")
    core, x = lax.rem(dp, CORES), lax.div(dp, CORES)
    half = wsend_ref.shape[1]
    depth = xown_ref.shape[1]

    def block(ref, at, count):
        return ref.at[:, pl.ds(pl.multiple_of(at * count, count), count)]

    moved = [
        (k_ref, kbuf),
        (v_ref, vbuf),
        (block(w_ref, 1 - core, half), wsend_ref),
    ]
    for rel in range(1, nx):
        moved.append((block(x_ref, lax.rem(x + rel, nx), depth), xaway[rel - 1]))
    moved.append((block(x_ref, x, depth), xown_ref))
    copies = []
    for i, (source, target) in enumerate(moved):
        copy = pltpu.make_async_copy(source, target, sems.at[i])
        copy.start()
        copies.append(copy)
    count = lane_scan(padded(reset_ref[...].astype(f32)))[0:1]
    cumulative = lane_scan(padded(log_sigmoid(forget_ref[...])))[0:heads]
    total = cumulative[:, length - 1 : length]
    final = count[:, length - 1 : length]
    expo = jnp.where(count == final, total - cumulative + gate_ref[...], very_low)
    top = jnp.max(expo, axis=1, keepdims=True)
    weight = padded(jnp.exp(expo - top)).T
    gap = jnp.where(final > 0, very_low, total)
    copies[0].wait()
    copies[1].wait()
    for r in range(ng):
        own_ref, msg_ref, side_ref = chunks[3 * r : 3 * r + 3]
        for j in range(heads // ng):
            within = lax.rem(group + r, ng)
            head = j * ng + within

            def pick(values):
                chosen = values[j * ng]
                for i in range(1, ng):
                    chosen = jnp.where(within == i, values[j * ng + i], chosen)
                return chosen

            keys = kbuf[:, pl.ds(pl.multiple_of(head * size, size), size)].astype(f32)
            values = vbuf[:, pl.ds(pl.multiple_of(head * vsize, vsize), vsize)]
            scale = pick([weight[:, h : h + 1] for h in range(heads)])
            this_top = pick([top[h : h + 1] for h in range(heads)])
            this_gap = pick([gap[h : h + 1] for h in range(heads)])
            weighted = (keys * scale).astype(bf16)
            memory = lax.dot_general(
                weighted, values, (((0,), (0,)), ((), ())), preferred_element_type=f32
            )
            normer = jnp.sum(weighted.astype(f32), axis=0, keepdims=True)
            own_ref[j * size : (j + 1) * size, :] = memory
            side_ref[j * 8 : j * 8 + 1, :] = normer
            side_ref[j * 8 + 1 : j * 8 + 2, :] = jnp.broadcast_to(this_top, normer.shape)
            side_ref[j * 8 + 2 : j * 8 + 3, :] = jnp.broadcast_to(this_gap, normer.shape)
            store_message(msg_ref, j * (size + EXTRA), size, memory, normer, this_top)
    for copy in copies[2:]:
        copy.wait()


def combine_kernel(heads, prev_ref, own_ref, side_ref, msg_ref):
    size = own_ref.shape[0] // heads
    stride = size + EXTRA
    for h in range(heads):
        memory, normer, top = load_message(prev_ref, h * stride, size)
        own_normer = side_ref[h * 8 : h * 8 + 1, :]
        own_top = side_ref[h * 8 + 1 : h * 8 + 2, 0:1]
        gap = side_ref[h * 8 + 2 : h * 8 + 3, 0:1]
        shifted = top + gap
        both = jnp.maximum(shifted, own_top)
        early = jnp.exp(shifted - both)
        late = jnp.exp(own_top - both)
        joined = early * memory.astype(f32) + late * own_ref[h * size : (h + 1) * size, :]
        store_message(msg_ref, h * stride, size, joined, early * normer + late * own_normer, both)


def project_kernel(nz, nx, *refs):
    count = CORES * nx
    blocks, parts = refs[:count], refs[count : count + nz]
    outs = refs[count + nz : 2 * count + nz]
    tokens, whole, sems = refs[2 * count + nz :]
    rows = parts[0].shape[1]
    place = lax.axis_index("ctx")
    core = lax.rem(lax.axis_index("dp"), CORES)
    copies = []
    for s in range(nz):
        source = place ^ s
        for j in range(CORES):
            owner = lax.rem(core + j, CORES)
            row = pl.multiple_of((owner * nz + source) * rows, rows)
            copies.append((parts[s].at[j], whole.at[pl.ds(row, rows)]))
    sequence = list(range(CORES, count)) + list(range(CORES))
    for i in sequence:
        copies.append((blocks[i], tokens.at[i]))
    started = []
    for i, (source, target) in enumerate(copies):
        copy = pltpu.make_async_copy(source, target, sems.at[i])
        copy.start()
        started.append(copy)
    for copy in started[: nz * CORES]:
        copy.wait()
    for at, i in enumerate(sequence):
        started[nz * CORES + at].wait()
        value = jnp.dot(tokens[i], whole[...], preferred_element_type=f32)
        outs[i][...] = value.astype(outs[i].dtype)


def read_kernel(heads, ng, nx, hops, phase, *refs):
    partials = [refs[j * nx : (j + 1) * nx] for j in range(CORES)]
    k_ref, v_ref, gate_ref, forget_ref, reset_ref = refs[CORES * nx : CORES * nx + 5]
    at = CORES * nx + 5
    done = phase if phase == ng - 1 else 0
    states, earlier = refs[at : at + hops], refs[at + hops : at + hops + done]
    out_ref, kbuf, vbuf, state, sems = refs[at + hops + done :]
    length = k_ref.shape[0]
    size, vsize = k_ref.shape[1] // heads, v_ref.shape[1] // heads
    factor = size ** (-0.5)
    stride = size + EXTRA
    group, dp, place = (lax.axis_index(a) for a in AXES)
    core = lax.rem(dp, CORES)

    def slot_of(j):
        return lax.rem(core + j, CORES)

    def head_of(j, r):
        return slot_of(j) * ng + lax.rem(group + r, ng)

    copies = []
    for j in range(CORES):
        head = head_of(j, phase)
        for i, (ref, buffer, wide) in enumerate(((k_ref, kbuf, size), (v_ref, vbuf, vsize))):
            source = ref.at[:, pl.ds(pl.multiple_of(head * wide, wide), wide)]
            copy = pltpu.make_async_copy(source, buffer.at[j], sems.at[2 * j + i])
            copy.start()
            copies.append(copy)
    for h in range(hops):

        @pl.when(place == h + 1)
        def _():
            pltpu.make_async_copy(states[h], state, sems.at[2 * CORES]).start()

    @pl.when(place == 0)
    def _():
        state[...] = jnp.zeros_like(state)

    t_at = lax.broadcasted_iota(jnp.int32, (length, length), 0)
    s_at = lax.broadcasted_iota(jnp.int32, (length, length), 1)
    forget = [log_sigmoid(forget_ref[pl.ds(head_of(j, phase), 1), :]) for j in range(CORES)]
    running = lane_scan(padded(jnp.concatenate([reset_ref[...].astype(f32)] + forget, axis=0)))
    running_rows = running.T
    count, count_rows = running[0:1], running_rows[:, 0:1]
    linked = jnp.logical_and(count_rows == count, t_at >= s_at)
    exponents = []
    for j in range(CORES):
        exponents.append(
            jnp.where(
                linked,
                running_rows[:, 1 + j : 2 + j]
                - running[1 + j : 2 + j]
                + gate_ref[pl.ds(head_of(j, phase), 1), :],
                very_low,
            )
        )

    @pl.when(place > 0)
    def _():
        pltpu.make_async_copy(states[0], state, sems.at[2 * CORES]).wait()

    for copy in copies:
        copy.wait()
    for j in range(CORES):
        total = partials[j][0][...]
        for other in partials[j][1:]:
            total = total + other[...].astype(f32)
        query = total.astype(bf16)
        keys, values = kbuf[j], vbuf[j]
        base = pl.multiple_of(slot_of(j) * stride, EXTRA)
        memory = state[pl.ds(base, size), :]
        extra = state[pl.ds(pl.multiple_of(base + size, EXTRA), EXTRA), :].astype(f32)
        normer = (extra[0:1] + extra[1:2] + extra[2:3]).astype(bf16).astype(f32)
        top = extra[3:4, 0:1] + extra[4:5, 0:1] + extra[5:6, 0:1]
        top = jnp.where(place == 0, very_low, top)
        exponent = exponents[j]
        carried = jnp.where(count_rows == 0.0, running_rows[:, 1 + j : 2 + j] + top, very_low)
        row_max = jnp.maximum(jnp.max(exponent, axis=1, keepdims=True), carried)
        scores = lax.dot_general(
            query, keys, (((1,), (1,)), ((), ())), preferred_element_type=f32
        )
        weighted = (jnp.exp(exponent - row_max) * (scores * factor)).astype(bf16)
        scale = jnp.exp(carried - row_max) * factor
        cross = jnp.dot(query, memory, preferred_element_type=f32)
        inter = jnp.sum(query.astype(f32) * normer, axis=1, keepdims=True)
        numerator = jnp.dot(weighted, values, preferred_element_type=f32) + scale * cross
        denominator = jnp.sum(weighted.astype(f32), axis=1, keepdims=True) + scale * inter
        floor = jnp.exp(jnp.maximum(-row_max, 0.0))
        hidden = (numerator / jnp.maximum(jnp.abs(denominator), floor)).astype(bf16)
        if phase < ng - 1:
            out_ref[:, j * vsize : (j + 1) * vsize] = hidden
        else:
            target = pl.multiple_of(head_of(j, phase) * vsize, vsize)
            out_ref[:, pl.ds(target, vsize)] = hidden
    if phase == ng - 1:
        for r in range(phase):
            for j in range(CORES):
                target = pl.multiple_of(head_of(j, r) * vsize, vsize)
                out_ref[:, pl.ds(target, vsize)] = earlier[r][:, j * vsize : (j + 1) * vsize]


VMEM = pl.BlockSpec(memory_space=pltpu.VMEM)
ANY = pl.BlockSpec(memory_space=pl.ANY)


def make_body(mesh):
    ng, nd, nz = (mesh.shape[a] for a in AXES)
    nx = nd // CORES

    def send(value, where):
        return lax.ppermute(value, AXES, moves(mesh, where))

    def over_core(value):
        return send(value, lambda g, x, k, z: (g, x, 1 - k, z))

    def call(kernel, *args, **options):
        return pl.pallas_call(kernel, **options)(*args)

    def body(normed_input, query_weight, key_vectors, value_vectors, input_gate, forget_gate, resets):
        _, length, features = normed_input.shape
        heads = input_gate.shape[1]
        columns = query_weight.shape[1]
        width = columns // (ng * CORES)
        size = columns // heads
        keys, values = key_vectors[0], value_vectors[0]
        gate, forget = input_gate[0], forget_gate[0]
        vwidth = values.shape[1]
        group = lax.axis_index("groups")
        dp = lax.axis_index("dp")
        core = dp % CORES
        half = columns // CORES
        depth = features // nx
        flat = normed_input[0]

        def columns_of(value, at, count):
            return lax.dynamic_slice_in_dim(value, at * count, count, 1)

        stride = size + EXTRA
        vsize = vwidth // heads
        slots = heads // ng
        message = jax.ShapeDtypeStruct((slots * stride, vsize), bf16)
        block = jax.ShapeDtypeStruct((length, depth), flat.dtype)
        prepared = call(
            functools.partial(prepare_kernel, heads, ng, nx),
            keys, values, flat, query_weight, gate, forget, resets,
            out_shape=(
                jax.ShapeDtypeStruct((query_weight.shape[0], half), query_weight.dtype),
                *[block] * nx,
                *[
                    jax.ShapeDtypeStruct((slots * size, vsize), f32),
                    message,
                    jax.ShapeDtypeStruct((slots * 8, vsize), f32),
                ]
                * ng,
            ),
            in_specs=[ANY] * 4 + [VMEM] * 3,
            out_specs=(ANY,) * (1 + nx) + (VMEM,) * (3 * ng),
            scratch_shapes=[
                pltpu.VMEM(keys.shape, bf16),
                pltpu.VMEM(values.shape, bf16),
                pltpu.SemaphoreType.DMA((3 + nx,)),
            ],
        )
        swapped = over_core(prepared[0])
        kept = columns_of(query_weight, core, half)
        parts = [
            jnp.stack([columns_of(v, (group + r) % ng, width) for v in (kept, swapped)])
            for r in range(ng)
        ]
        tokens = [prepared[1]]
        arrived = [
            send(prepared[1 + rel], lambda g, x, k, z: (g, (x + rel) % nx, k, z))
            for rel in range(1, nx)
        ]
        tokens.append(over_core(tokens[0]))
        for rel, value in enumerate(arrived):
            tokens.extend([value, over_core(value)])
        pieces = [[parts[r]] for r in range(ng)]
        for s in range(1, nz):
            mine = send(parts[0], lambda g, x, k, z: (g, x, k, z ^ s))
            pieces[0].append(mine)
            for r in range(1, ng):
                pieces[r].append(send(mine, lambda g, x, k, z: ((g - r) % ng, x, k, z)))
        states = [[] for _ in range(ng)]
        for r in range(ng):
            own, current, side = prepared[1 + nx + 3 * r : 4 + nx + 3 * r]
            for hop in range(1, nz):
                state = send(current, lambda g, x, k, z: (g, x, k, z + 1) if z == hop - 1 else None)
                states[r].append(state)
                if hop < nz - 1:
                    current = call(
                        functools.partial(combine_kernel, slots),
                        state, own, side,
                        out_shape=message,
                        in_specs=[VMEM] * 3,
                        out_specs=VMEM,
                    )
        results = []
        for r in range(ng):
            piece = jax.ShapeDtypeStruct((length, width), f32)
            small = jax.ShapeDtypeStruct((length, width), bf16)
            sums = call(
                functools.partial(project_kernel, nz, nx),
                *tokens, *pieces[r],
                out_shape=(piece,) * CORES + (small,) * (CORES * (nx - 1)),
                in_specs=[ANY] * (CORES * nx + nz),
                out_specs=(VMEM,) * (CORES * nx),
                scratch_shapes=[
                    pltpu.VMEM((CORES * nx, length, depth), bf16),
                    pltpu.VMEM((depth, width), bf16),
                    pltpu.SemaphoreType.DMA((CORES * (nx + nz),)),
                ],
            )
            partials = [[sums[0]], [over_core(sums[1])]]
            for rel in range(1, nx):
                for j in range(CORES):
                    partials[j].append(
                        send(
                            sums[CORES * rel + j], lambda g, x, k, z: (g, (x - rel) % nx, k ^ j, z)
                        )
                    )
            last = r == ng - 1
            results.append(
                call(
                    functools.partial(read_kernel, heads, ng, nx, nz - 1, r),
                    *partials[0], *partials[1], keys, values, gate, forget, resets,
                    *states[r], *(results if last else []),
                    out_shape=jax.ShapeDtypeStruct(
                        (length, vwidth if last else CORES * vsize), bf16
                    ),
                    in_specs=[VMEM] * (CORES * nx) + [ANY] * 2 + [VMEM] * 3
                    + [ANY] * (nz - 1) + [VMEM] * (r if last else 0),
                    out_specs=VMEM,
                    scratch_shapes=[
                        pltpu.VMEM((CORES, length, size), bf16),
                        pltpu.VMEM((CORES, length, vsize), bf16),
                        pltpu.VMEM(message.shape, bf16),
                        pltpu.SemaphoreType.DMA((2 * CORES + 1,)),
                    ],
                )
            )
        hidden = results[-1]
        return hidden[None]

    return body


def solution(mesh):
    return jax.shard_map(
        make_body(mesh),
        mesh=mesh,
        in_specs=(
            P(("groups", "dp"), "ctx", None),
            P(("dp", "ctx"), None),
            P(("groups", "dp"), "ctx", None),
            P(("groups", "dp"), "ctx", None),
            P(("groups", "dp"), None, "ctx"),
            P(("groups", "dp"), None, "ctx"),
            P(("groups", "dp"), "ctx"),
        ),
        out_specs=P(("groups", "dp"), "ctx", None),
        check_vma=False,
    )
```

profile of v0, /device:TPU:17, one launch (start us, length us, event | category | flops | bytes accessed | tf_op | source)
XLA Modules:
  0.0 186.4 jit_solution(4897449737893222698)
XLA Ops:
  0.0 74.5 %shard_map.73 = (bf16[256,512]{1,0:T(8,128)(2,1)}, bf16[256,2048]{1,0:T(8,128)(2,1)}, bf16[256,2048]{1,0:T(8,128)(2,1)}, f32[512,256]{1,0:T(8,128)}, bf16[544,25...) custom-call(bf16[256,1024]{1,0:T(8,128)(2,1)} %bitcast.14, ...), custom_call_target="tpu_custom_call" | custom-call | tf_op jit(solution)/shard_map/pallas_call | solution.py:316
  78.1 20.7 %collective-permute-done.1.refs_2_ = bf16[256,2048]{1,0:T(8,128)(2,1)S(1)} collective-permute-done((bf16[256,2048]{1,0:T(8,128)(2,1)}, bf16[256,2048]{1,0:T(8,128)(2,1)S(1)}, u32[]{:S(2)}, u32[]{:S(2)}) %collective-permute-start.1) | collective-permute-done | bytes 1048608 | tf_op jit(solution)/shard_map/ppermute | solution.py:310
  98.8 1.5 collective-permute-start.2
  101.1 1.8 dynamic-slice_bitcast_fusion.1
  102.9 1.7 dynamic-slice_bitcast_fusion
  104.6 2.0 %shard_map.78 = bf16[544,256]{1,0:T(8,128)(2,1)} custom-call(bf16[544,256]{1,0:T(8,128)(2,1)} %collective-permute-done.19.prev_ref.refs_9_, f32[512,256]{1,0:T(8,128)} %get-tuple-element.37.own_ref, f32[16,256]{1,0:T(8,128)} %get-tuple-element.38.side_ref), custom_call_target="tpu_custom_call" | custom-call | tf_op jit(solution)/shard_map/pallas_call | solution.py:316
  107.8 1.7 pad_maximum_fusion.1.refs_4_
  111.6 2.0 %shard_map.75 = bf16[544,256]{1,0:T(8,128)(2,1)} custom-call(bf16[544,256]{1,0:T(8,128)(2,1)} %copy-done.3, f32[512,256]{1,0:T(8,128)} %get-tuple-element.30.own_ref, f32[16,256]{1,0:T(8,128)} %get-tuple-element.31.side_ref), custom_call_target="tpu_custom_call" | custom-call | tf_op jit(solution)/shard_map/pallas_call | solution.py:316
  114.9 2.8 %collective-permute-done.4.refs_5_ = bf16[2,256,256]{2,1,0:T(8,128)(2,1)} collective-permute-done((bf16[2,256,256]{2,1,0:T(8,128)(2,1)}, bf16[2,256,256]{2,1,0:T(8,128)(2,1)}, u32[]{:S(2)}, u32[]{:S(2)}) %collective-permute-start.4) | collective-permute-done | bytes 262176 | tf_op jit(solution)/shard_map/ppermute | solution.py:310
  117.7 2.4 %collective-permute-start.6 = (bf16[2,256,256]{2,1,0:T(8,128)(2,1)}, bf16[2,256,256]{2,1,0:T(8,128)(2,1)}, u32[]{:S(2)}, u32[]{:S(2)}) collective-permute-start(bf16[2,256,256]{2,1,0:T(8,128)(2,1)} %pad_maximum_fusion.1.refs_4_), channel_id=1, source_target_pairs={{0,2},{1,3},{2,0},{3,1},{4,6},{5,7},{6,4},{7,5},{8,10},{9,11},{10,... | collective-permute-start | bytes 786440 | tf_op jit(solution)/shard_map/ppermute | solution.py:310
  120.3 2.0 %shard_map.79 = bf16[544,256]{1,0:T(8,128)(2,1)} custom-call(bf16[544,256]{1,0:T(8,128)(2,1)} %collective-permute-done.20.prev_ref.refs_10_, f32[512,256]{1,0:T(8,128)} %get-tuple-element.37.own_ref, f32[16,256]{1,0:T(8,128)} %get-tuple-element.38.side_ref), custom_call_target="tpu_custom_call" | custom-call | tf_op jit(solution)/shard_map/pallas_call | solution.py:316
  122.2 14.4 %collective-permute-done.6.refs_6_ = bf16[2,256,256]{2,1,0:T(8,128)(2,1)} collective-permute-done((bf16[2,256,256]{2,1,0:T(8,128)(2,1)}, bf16[2,256,256]{2,1,0:T(8,128)(2,1)}, u32[]{:S(2)}, u32[]{:S(2)}) %collective-permute-start.6) | collective-permute-done | bytes 262176 | tf_op jit(solution)/shard_map/ppermute | solution.py:310
  136.7 7.7 %collective-permute-start.21 = (bf16[544,256]{1,0:T(8,128)(2,1)}, bf16[544,256]{1,0:T(8,128)(2,1)}, u32[]{:S(2)}, u32[]{:S(2)}) collective-permute-start(bf16[544,256]{1,0:T(8,128)(2,1)} %shard_map.79), channel_id=1, source_target_pairs={{2,3},{6,7},{10,11},{14,15},{18,19},{22,23},{26,27},{30,31}} | collective-permute-start | bytes 835592 | tf_op jit(solution)/shard_map/ppermute | solution.py:310
  144.4 1.8 collective-permute-done.8.refs_7_
  148.9 2.0 %shard_map.76 = bf16[544,256]{1,0:T(8,128)(2,1)} custom-call(bf16[544,256]{1,0:T(8,128)(2,1)} %copy-done.4, f32[512,256]{1,0:T(8,128)} %get-tuple-element.30.own_ref, f32[16,256]{1,0:T(8,128)} %get-tuple-element.31.side_ref), custom_call_target="tpu_custom_call" | custom-call | tf_op jit(solution)/shard_map/pallas_call | solution.py:316
  152.2 1.7 pad_maximum_fusion.refs_4_
  153.9 5.3 %shard_map.77 = (f32[256,256]{1,0:T(8,128)}, f32[256,256]{1,0:T(8,128)}, bf16[256,256]{1,0:T(8,128)(2,1)}, bf16[256,256]{1,0:T(8,128)(2,1)}) custom-call(bf16[256,2048]{1,0:T(8,128)(2,1)} %get-tuple-element.22.refs_0_, bf16[256,2048]{1,0:T(8,128)(2,1)} %copy-done.1, bf16[256,2048]{1,0:T(8,128)(2,1)} %copy-done, bf16[256,2048]{1,0:T(8,128)(2,1)} %copy-done.2, ...), custom_call_target="tpu_custom_call" | custom-call | tf_op jit(solution)/shard_map/pallas_call | solution.py:316
  159.2 2.1 %collective-permute-start.17 = (f32[256,256]{1,0:T(8,128)}, f32[256,256]{1,0:T(8,128)S(1)}, u32[]{:S(2)}, u32[]{:S(2)}) collective-permute-start(f32[256,256]{1,0:T(8,128)} %get-tuple-element.34), channel_id=1, source_target_pairs={{0,4},{1,5},{2,6},{3,7},{4,0},{5,1},{6,2},{7,3},{8,12},{9,13},{10,... | collective-permute-start | bytes 786440 | tf_op jit(solution)/shard_map/ppermute | solution.py:310
  162.5 2.0 %collective-permute-done.9.refs_7_ = bf16[2,256,256]{2,1,0:T(8,128)(2,1)} collective-permute-done((bf16[2,256,256]{2,1,0:T(8,128)(2,1)}, bf16[2,256,256]{2,1,0:T(8,128)(2,1)}, u32[]{:S(2)}, u32[]{:S(2)}) %collective-permute-start.9) | collective-permute-done | bytes 262176 | tf_op jit(solution)/shard_map/ppermute | solution.py:310
  164.5 3.1 %collective-permute-start.18 = (bf16[256,256]{1,0:T(8,128)(2,1)}, bf16[256,256]{1,0:T(8,128)(2,1)S(1)}, u32[]{:S(2)}, u32[]{:S(2)}) collective-permute-start(bf16[256,256]{1,0:T(8,128)(2,1)} %get-tuple-element.35), channel_id=1, source_target_pairs={{0,12},{1,13},{2,14},{3,15},{4,8},{5,9},{6,10},{7,11},{8,4},{9,5},... | collective-permute-start | bytes 393224 | tf_op jit(solution)/shard_map/ppermute | solution.py:310
  167.6 5.2 %shard_map.74 = (f32[256,256]{1,0:T(8,128)}, f32[256,256]{1,0:T(8,128)}, bf16[256,256]{1,0:T(8,128)(2,1)}, bf16[256,256]{1,0:T(8,128)(2,1)}) custom-call(bf16[256,2048]{1,0:T(8,128)(2,1)} %get-tuple-element.22.refs_0_, bf16[256,2048]{1,0:T(8,128)(2,1)} %copy-done.1, bf16[256,2048]{1,0:T(8,128)(2,1)} %copy-done, bf16[256,2048]{1,0:T(8,128)(2,1)} %copy-done.2, ...), custom_call_target="tpu_custom_call" | custom-call | tf_op jit(solution)/shard_map/pallas_call | solution.py:316
  173.3 1.8 collective-permute-start.12
  175.8 4.1 %shard_map.80.refs_12_ = bf16[256,512]{1,0:T(8,128)(2,1)} custom-call(f32[256,256]{1,0:T(8,128)} %get-tuple-element.32.refs_0_, bf16[256,256]{1,0:T(8,128)(2,1)} %copy-done.10, f32[256,256]{1,0:T(8,128)} %copy-done.7, bf16[256,256]{1,0:T(8,128)(2,1)} %copy-done.11, bf16[256,1024]{1,0:T(8,128)(2,1)} %bitcast.15, bf16[256,1024]{1,0:T(8,128)(2,1)} %bitcast.18, ...), custom_call_target="tpu_custom_call" | custom-call | tf_op jit(solution)/shard_map/pallas_call | solution.py:316
  182.0 4.4 %shard_map.81 = bf16[256,1024]{1,0:T(8,128)(2,1)} custom-call(f32[256,256]{1,0:T(8,128)} %get-tuple-element.25.refs_0_, bf16[256,256]{1,0:T(8,128)(2,1)} %copy-done.8, f32[256,256]{1,0:T(8,128)} %copy-done.6, bf16[256,256]{1,0:T(8,128)(2,1)} %copy-done.9, bf16[256,1024]{1,0:T(8,128)(2,1)} %bitcast.16, bf16[256,1024]{1,0:T(8,128)(2,1)} %bitcast.19, ...), custom_call_target="tpu_custom_call" | custom-call | tf_op jit(solution)/shard_map/pallas_call | solution.py:316
  (57 shorter events, 17.5 us)
Async XLA Ops:
  74.5 24.3 %collective-permute-start.1 = (bf16[256,2048]{1,0:T(8,128)(2,1)}, bf16[256,2048]{1,0:T(8,128)(2,1)S(1)}, u32[]{:S(2)}, u32[]{:S(2)}) collective-permute-start(bf16[256,2048]{1,0:T(8,128)(2,1)} %get-tuple-element.23), channel_id=1, source_target_pairs={{0,8},{1,9},{2,10},{3,11},{4,12},{5,13},{6,14},{7,15},{8,0},{9,1},... | collective-permute-start | bytes 3145736 | tf_op jit(solution)/shard_map/ppermute | solution.py:310
  75.8 71.9 %collective-permute-start = (bf16[256,2048]{1,0:T(8,128)(2,1)}, bf16[256,2048]{1,0:T(8,128)(2,1)S(1)}, u32[]{:S(2)}, u32[]{:S(2)}) collective-permute-start(bf16[256,2048]{1,0:T(8,128)(2,1)} %get-tuple-element.22.refs_0_), channel_id=1, source_target_pairs={{0,4},{1,5},{2,6},{3,7},{4,0},{5,1},{6,2},{7,3},{8,12},{9,13},{10,... | collective-permute-start | bytes 3145736 | tf_op jit(solution)/shard_map/ppermute | solution.py:310
  76.7 26.1 %collective-permute-start.3 = (bf16[256,512]{1,0:T(8,128)(2,1)}, bf16[256,512]{1,0:T(8,128)(2,1)}, u32[]{:S(2)}, u32[]{:S(2)}) collective-permute-start(bf16[256,512]{1,0:T(8,128)(2,1)} %get-tuple-element.24), channel_id=1, source_target_pairs={{0,4},{1,5},{2,6},{3,7},{4,0},{5,1},{6,2},{7,3},{8,12},{9,13},{10,... | collective-permute-start | bytes 786440 | tf_op jit(solution)/shard_map/ppermute | solution.py:310
  76.7 27.8 %collective-permute-start.19 = (bf16[544,256]{1,0:T(8,128)(2,1)}, bf16[544,256]{1,0:T(8,128)(2,1)}, u32[]{:S(2)}, u32[]{:S(2)}) collective-permute-start(bf16[544,256]{1,0:T(8,128)(2,1)} %get-tuple-element.36), channel_id=1, source_target_pairs={{0,1},{4,5},{8,9},{12,13},{16,17},{20,21},{24,25},{28,29}} | collective-permute-start | bytes 835592 | tf_op jit(solution)/shard_map/ppermute | solution.py:310
  98.8 23.4 %copy-start = (bf16[256,2048]{1,0:T(8,128)(2,1)}, bf16[256,2048]{1,0:T(8,128)(2,1)S(1)}, u32[]{:S(2)}) copy-start(bf16[256,2048]{1,0:T(8,128)(2,1)S(1)} %collective-permute-done.1.refs_2_) | copy-start | bytes 3145732
  98.8 52.1 %collective-permute-start.2 = (bf16[256,2048]{1,0:T(8,128)(2,1)S(1)}, bf16[256,2048]{1,0:T(8,128)(2,1)S(1)}, u32[]{:S(2)}, u32[]{:S(2)}) collective-permute-start(bf16[256,2048]{1,0:T(8,128)(2,1)S(1)} %collective-permute-done.1.refs_2_), channel_id=1, source_target_pairs={{0,4},{1,5},{2,6},{3,7},{4,0},{5,1},{6,2},{7,3},{8,12},{9,13},{10,... | collective-permute-start | bytes 3145736 | tf_op jit(solution)/shard_map/ppermute | solution.py:310
  100.3 10.6 %collective-permute-start.13 = (bf16[544,256]{1,0:T(8,128)(2,1)}, bf16[544,256]{1,0:T(8,128)(2,1)S(1)}, u32[]{:S(2)}, u32[]{:S(2)}) collective-permute-start(bf16[544,256]{1,0:T(8,128)(2,1)} %get-tuple-element.29), channel_id=1, source_target_pairs={{0,1},{4,5},{8,9},{12,13},{16,17},{20,21},{24,25},{28,29}} | collective-permute-start | bytes 835592 | tf_op jit(solution)/shard_map/ppermute | solution.py:310
  106.5 13.6 %collective-permute-start.20 = (bf16[544,256]{1,0:T(8,128)(2,1)}, bf16[544,256]{1,0:T(8,128)(2,1)}, u32[]{:S(2)}, u32[]{:S(2)}) collective-permute-start(bf16[544,256]{1,0:T(8,128)(2,1)} %shard_map.78), channel_id=1, source_target_pairs={{1,2},{5,6},{9,10},{13,14},{17,18},{21,22},{25,26},{29,30}} | collective-permute-start | bytes 835592 | tf_op jit(solution)/shard_map/ppermute | solution.py:310
  109.5 8.2 %collective-permute-start.4 = (bf16[2,256,256]{2,1,0:T(8,128)(2,1)}, bf16[2,256,256]{2,1,0:T(8,128)(2,1)}, u32[]{:S(2)}, u32[]{:S(2)}) collective-permute-start(bf16[2,256,256]{2,1,0:T(8,128)(2,1)} %pad_maximum_fusion.1.refs_4_), channel_id=1, source_target_pairs={{0,1},{1,0},{2,3},{3,2},{4,5},{5,4},{6,7},{7,6},{8,9},{9,8},{10,11... | collective-permute-start | bytes 786440 | tf_op jit(solution)/shard_map/ppermute | solution.py:310
  113.6 33.8 %collective-permute-start.14 = (bf16[544,256]{1,0:T(8,128)(2,1)}, bf16[544,256]{1,0:T(8,128)(2,1)S(1)}, u32[]{:S(2)}, u32[]{:S(2)}) collective-permute-start(bf16[544,256]{1,0:T(8,128)(2,1)} %shard_map.75), channel_id=1, source_target_pairs={{1,2},{5,6},{9,10},{13,14},{17,18},{21,22},{25,26},{29,30}} | collective-permute-start | bytes 835592 | tf_op jit(solution)/shard_map/ppermute | solution.py:310
  117.7 19.0 %collective-permute-start.6 = (bf16[2,256,256]{2,1,0:T(8,128)(2,1)}, bf16[2,256,256]{2,1,0:T(8,128)(2,1)}, u32[]{:S(2)}, u32[]{:S(2)}) collective-permute-start(bf16[2,256,256]{2,1,0:T(8,128)(2,1)} %pad_maximum_fusion.1.refs_4_), channel_id=1, source_target_pairs={{0,2},{1,3},{2,0},{3,1},{4,6},{5,7},{6,4},{7,5},{8,10},{9,11},{10,... | collective-permute-start | bytes 786440 | tf_op jit(solution)/shard_map/ppermute | solution.py:310
  120.1 26.1 %collective-permute-start.8 = (bf16[2,256,256]{2,1,0:T(8,128)(2,1)}, bf16[2,256,256]{2,1,0:T(8,128)(2,1)}, u32[]{:S(2)}, u32[]{:S(2)}) collective-permute-start(bf16[2,256,256]{2,1,0:T(8,128)(2,1)} %pad_maximum_fusion.1.refs_4_), channel_id=1, source_target_pairs={{0,3},{1,2},{2,1},{3,0},{4,7},{5,6},{6,5},{7,4},{8,11},{9,10},{10,... | collective-permute-start | bytes 786440 | tf_op jit(solution)/shard_map/ppermute | solution.py:310
  136.7 36.2 %collective-permute-start.21 = (bf16[544,256]{1,0:T(8,128)(2,1)}, bf16[544,256]{1,0:T(8,128)(2,1)}, u32[]{:S(2)}, u32[]{:S(2)}) collective-permute-start(bf16[544,256]{1,0:T(8,128)(2,1)} %shard_map.79), channel_id=1, source_target_pairs={{2,3},{6,7},{10,11},{14,15},{18,19},{22,23},{26,27},{30,31}} | collective-permute-start | bytes 835592 | tf_op jit(solution)/shard_map/ppermute | solution.py:310
  146.2 13.0 %collective-permute-start.5 = (bf16[2,256,256]{2,1,0:T(8,128)(2,1)}, bf16[2,256,256]{2,1,0:T(8,128)(2,1)}, u32[]{:S(2)}, u32[]{:S(2)}) collective-permute-start(bf16[2,256,256]{2,1,0:T(8,128)(2,1)} %collective-permute-done.4.refs_5_), channel_id=1, source_target_pairs={{0,16},{1,17},{2,18},{3,19},{4,20},{5,21},{6,22},{7,23},{8,24},{9,... | collective-permute-start | bytes 786440 | tf_op jit(solution)/shard_map/ppermute | solution.py:310
  147.4 13.8 %collective-permute-start.7 = (bf16[2,256,256]{2,1,0:T(8,128)(2,1)}, bf16[2,256,256]{2,1,0:T(8,128)(2,1)}, u32[]{:S(2)}, u32[]{:S(2)}) collective-permute-start(bf16[2,256,256]{2,1,0:T(8,128)(2,1)} %collective-permute-done.6.refs_6_), channel_id=1, source_target_pairs={{0,16},{1,17},{2,18},{3,19},{4,20},{5,21},{6,22},{7,23},{8,24},{9,... | collective-permute-start | bytes 786440 | tf_op jit(solution)/shard_map/ppermute | solution.py:310
  147.7 6.2 %copy-start.1 = (bf16[256,2048]{1,0:T(8,128)(2,1)}, bf16[256,2048]{1,0:T(8,128)(2,1)S(1)}, u32[]{:S(2)}) copy-start(bf16[256,2048]{1,0:T(8,128)(2,1)S(1)} %collective-permute-done.refs_1_) | copy-start | bytes 3145732
  147.7 16.8 %collective-permute-start.9 = (bf16[2,256,256]{2,1,0:T(8,128)(2,1)}, bf16[2,256,256]{2,1,0:T(8,128)(2,1)}, u32[]{:S(2)}, u32[]{:S(2)}) collective-permute-start(bf16[2,256,256]{2,1,0:T(8,128)(2,1)} %collective-permute-done.8.refs_7_), channel_id=1, source_target_pairs={{0,16},{1,17},{2,18},{3,19},{4,20},{5,21},{6,22},{7,23},{8,24},{9,... | collective-permute-start | bytes 786440 | tf_op jit(solution)/shard_map/ppermute | solution.py:310
  150.9 29.0 %collective-permute-start.15 = (bf16[544,256]{1,0:T(8,128)(2,1)}, bf16[544,256]{1,0:T(8,128)(2,1)S(1)}, u32[]{:S(2)}, u32[]{:S(2)}) collective-permute-start(bf16[544,256]{1,0:T(8,128)(2,1)} %shard_map.76), channel_id=1, source_target_pairs={{2,3},{6,7},{10,11},{14,15},{18,19},{22,23},{26,27},{30,31}} | collective-permute-start | bytes 835592 | tf_op jit(solution)/shard_map/ppermute | solution.py:310
  159.2 15.9 %collective-permute-start.17 = (f32[256,256]{1,0:T(8,128)}, f32[256,256]{1,0:T(8,128)S(1)}, u32[]{:S(2)}, u32[]{:S(2)}) collective-permute-start(f32[256,256]{1,0:T(8,128)} %get-tuple-element.34), channel_id=1, source_target_pairs={{0,4},{1,5},{2,6},{3,7},{4,0},{5,1},{6,2},{7,3},{8,12},{9,13},{10,... | collective-permute-start | bytes 786440 | tf_op jit(solution)/shard_map/ppermute | solution.py:310
  161.3 11.6 %collective-permute-start.16 = (bf16[256,256]{1,0:T(8,128)(2,1)}, bf16[256,256]{1,0:T(8,128)(2,1)S(1)}, u32[]{:S(2)}, u32[]{:S(2)}) collective-permute-start(bf16[256,256]{1,0:T(8,128)(2,1)} %get-tuple-element.33), channel_id=1, source_target_pairs={{0,8},{1,9},{2,10},{3,11},{4,12},{5,13},{6,14},{7,15},{8,0},{9,1},... | collective-permute-start | bytes 393224 | tf_op jit(solution)/shard_map/ppermute | solution.py:310
  164.5 8.8 %collective-permute-start.18 = (bf16[256,256]{1,0:T(8,128)(2,1)}, bf16[256,256]{1,0:T(8,128)(2,1)S(1)}, u32[]{:S(2)}, u32[]{:S(2)}) collective-permute-start(bf16[256,256]{1,0:T(8,128)(2,1)} %get-tuple-element.35), channel_id=1, source_target_pairs={{0,12},{1,13},{2,14},{3,15},{4,8},{5,9},{6,10},{7,11},{8,4},{9,5},... | collective-permute-start | bytes 393224 | tf_op jit(solution)/shard_map/ppermute | solution.py:310
  172.8 8.4 %collective-permute-start.11 = (f32[256,256]{1,0:T(8,128)}, f32[256,256]{1,0:T(8,128)S(1)}, u32[]{:S(2)}, u32[]{:S(2)}) collective-permute-start(f32[256,256]{1,0:T(8,128)} %get-tuple-element.27), channel_id=1, source_target_pairs={{0,4},{1,5},{2,6},{3,7},{4,0},{5,1},{6,2},{7,3},{8,12},{9,13},{10,... | collective-permute-start | bytes 786440 | tf_op jit(solution)/shard_map/ppermute | solution.py:310
  172.9 7.0 %collective-permute-start.10 = (bf16[256,256]{1,0:T(8,128)(2,1)}, bf16[256,256]{1,0:T(8,128)(2,1)S(1)}, u32[]{:S(2)}, u32[]{:S(2)}) collective-permute-start(bf16[256,256]{1,0:T(8,128)(2,1)} %get-tuple-element.26), channel_id=1, source_target_pairs={{0,8},{1,9},{2,10},{3,11},{4,12},{5,13},{6,14},{7,15},{8,0},{9,1},... | collective-permute-start | bytes 393224 | tf_op jit(solution)/shard_map/ppermute | solution.py:310
  173.3 8.0 %collective-permute-start.12 = (bf16[256,256]{1,0:T(8,128)(2,1)}, bf16[256,256]{1,0:T(8,128)(2,1)S(1)}, u32[]{:S(2)}, u32[]{:S(2)}) collective-permute-start(bf16[256,256]{1,0:T(8,128)(2,1)} %get-tuple-element.28), channel_id=1, source_target_pairs={{0,12},{1,13},{2,14},{3,15},{4,8},{5,9},{6,10},{7,11},{8,4},{9,5},... | collective-permute-start | bytes 393224 | tf_op jit(solution)/shard_map/ppermute | solution.py:310
  (10 other events, 13.8 us)
where the time goes:
time: 187 us; the launch traced here: 186 us
  Pallas kernels  101 us (54%)
  waiting for transfers between devices  43 us (23%)
  starting transfers between devices  32.6 us (17%)
  local copies, waits for them, and re-layouts  5.65 us (3%)
  other arithmetic  3.37 us (2%)
    pallas_call x9, Pallas kernels, call(): return pl.pallas_call(kernel, **options)(*args)  101 us
    ppermute x22, waiting for transfers between devices, send(): return lax.ppermute(value, AXES, moves(mesh, where))  43 us
    ppermute x22, starting transfers between devices, send(): return lax.ppermute(value, AXES, moves(mesh, where))  32.6 us
  transfers between devices with their start and end apart: 22, of which 6 were waited for; matrix products, arithmetic and copies ran while one was open for 4% of the time, Pallas kernels for 12%

commit v1 on v0

--- a/solution.py
+++ b/solution.py
@@ -85,7 +85,7 @@
     wsend_ref, xown_ref = refs[7:9]
     xaway = refs[9 : 8 + nx]
     chunks = refs[8 + nx : 8 + nx + 3 * ng]
-    kbuf, vbuf, sems = refs[8 + nx + 3 * ng :]
+    kbuf, vbuf, wbuf, xbuf, sems, out_sems = refs[8 + nx + 3 * ng :]
     length = k_ref.shape[0]
     size, vsize = k_ref.shape[1] // heads, v_ref.shape[1] // heads
     group, dp = lax.axis_index("groups"), lax.axis_index("dp")
@@ -99,11 +99,10 @@
     moved = [
         (k_ref, kbuf),
         (v_ref, vbuf),
-        (block(w_ref, 1 - core, half), wsend_ref),
+        (block(w_ref, 1 - core, half), wbuf),
     ]
-    for rel in range(1, nx):
-        moved.append((block(x_ref, lax.rem(x + rel, nx), depth), xaway[rel - 1]))
-    moved.append((block(x_ref, x, depth), xown_ref))
+    for rel in range(nx):
+        moved.append((block(x_ref, lax.rem(x + rel, nx), depth), xbuf.at[rel]))
     copies = []
     for i, (source, target) in enumerate(moved):
         copy = pltpu.make_async_copy(source, target, sems.at[i])
@@ -117,8 +116,15 @@
     top = jnp.max(expo, axis=1, keepdims=True)
     weight = padded(jnp.exp(expo - top)).T
     gap = jnp.where(final > 0, very_low, total)
-    copies[0].wait()
-    copies[1].wait()
+    leaving = [(wbuf, wsend_ref), (xbuf.at[0], xown_ref)]
+    leaving += [(xbuf.at[rel], xaway[rel - 1]) for rel in range(1, nx)]
+    for copy in copies:
+        copy.wait()
+    copies = []
+    for i, (source, target) in enumerate(leaving):
+        copy = pltpu.make_async_copy(source, target, out_sems.at[i])
+        copy.start()
+        copies.append(copy)
     for r in range(ng):
         own_ref, msg_ref, side_ref = chunks[3 * r : 3 * r + 3]
         for j in range(heads // ng):
@@ -146,7 +152,7 @@
             side_ref[j * 8 + 1 : j * 8 + 2, :] = jnp.broadcast_to(this_top, normer.shape)
             side_ref[j * 8 + 2 : j * 8 + 3, :] = jnp.broadcast_to(this_gap, normer.shape)
             store_message(msg_ref, j * (size + EXTRA), size, memory, normer, this_top)
-    for copy in copies[2:]:
+    for copy in copies:
         copy.wait()
 
 
@@ -313,7 +319,8 @@
         return send(value, lambda g, x, k, z: (g, x, 1 - k, z))
 
     def call(kernel, *args, **options):
-        return pl.pallas_call(kernel, **options)(*args)
+        params = pltpu.CompilerParams(vmem_limit_bytes=20 * 2**20)
+        return pl.pallas_call(kernel, compiler_params=params, **options)(*args)
 
     def body(normed_input, query_weight, key_vectors, value_vectors, input_gate, forget_gate, resets):
         _, length, features = normed_input.shape
@@ -357,7 +364,10 @@
             scratch_shapes=[
                 pltpu.VMEM(keys.shape, bf16),
                 pltpu.VMEM(values.shape, bf16),
+                pltpu.VMEM((query_weight.shape[0], half), bf16),
+                pltpu.VMEM((nx, length, depth), bf16),
                 pltpu.SemaphoreType.DMA((3 + nx,)),
+                pltpu.SemaphoreType.DMA((1 + nx,)),
             ],
         )
         swapped = over_core(prepared[0])

time: 187 us -> 118 us (0.63)
  Pallas kernels: 101 us -> 18.8 us
  waiting for transfers between devices: 43 us -> 54.7 us
  local copies, waits for them, and re-layouts: 5.65 us -> 11.6 us
  other arithmetic: 3.37 us -> 0.05 us
    pallas_call x9, Pallas kernels: 101 us -> 18.8 us  [call(): return pl.pallas_call(kernel, compiler_params=params, **options)(*args)]
    ppermute x22, waiting for transfers between devices: 43 us -> 54.7 us  [send(): return lax.ppermute(value, AXES, moves(mesh, where))]
    unnamed x24 -> x32, local copies, waits for them, and re-layouts: 2.16 us -> 9.41 us
    another operation x2, other arithmetic: 3.37 us -> 0.05 us  [body(): jnp.stack([columns_of(v, (group + r) % ng, width) for v in (kept, swapped)])]
  transfers between devices with their start and end apart: 22 -> 22, of which waited for: 6 -> 8; matrix products, arithmetic and copies ran while one was open for 4% -> 2% of each run, Pallas kernels for 12% -> 11%
where the time goes in v1:
time: 118 us; the launch traced here: 117 us
  waiting for transfers between devices  54.7 us (46%)
  starting transfers between devices  31.9 us (27%)
  Pallas kernels  18.8 us (16%)
  local copies, waits for them, and re-layouts  11.6 us (10%)
    ppermute x22, waiting for transfers between devices, send(): return lax.ppermute(value, AXES, moves(mesh, where))  54.7 us
    ppermute x22, starting transfers between devices, send(): return lax.ppermute(value, AXES, moves(mesh, where))  31.9 us
    pallas_call x9, Pallas kernels, call(): return pl.pallas_call(kernel, compiler_params=params, **options)(*args)  18.8 us
    unnamed x32, local copies, waits for them, and re-layouts  9.41 us
  transfers between devices with their start and end apart: 22, of which 8 were waited for; matrix products, arithmetic and copies ran while one was open for 2% of the time, Pallas kernels for 11%

profile of v1, /device:TPU:17, one launch (start us, length us, event | category | flops | bytes accessed | tf_op | source)
XLA Modules:
  0.0 117.4 jit_solution(5284802126683427279)
XLA Ops:
  2.1 1.6 %copy-done.4 = bf16[1,256,4096]{2,1,0:T(8,128)(2,1)S(1)} copy-done((bf16[1,256,4096]{2,1,0:T(8,128)(2,1)S(1)}, bf16[1,256,4096]{2,1,0:T(8,128)(2,1)}, u32[]{:S(2)}) %copy-start.4) | copy-done | bytes 2097176
  6.8 2.9 %shard_map.73 = (bf16[256,512]{1,0:T(8,128)(2,1)}, bf16[256,2048]{1,0:T(8,128)(2,1)S(1)}, bf16[256,2048]{1,0:T(8,128)(2,1)S(1)}, f32[512,256]{1,0:T(8,128)S(1)},...) custom-call(bf16[256,1024]{1,0:T(8,128)(2,1)S(1)} %bitcast.14, ...), custom_call_target="tpu_custom_call" | custom-call | tf_op jit(solution)/shard_map/pallas_call | solution.py:323
  13.4 1.4 %collective-permute-start.19 = (bf16[544,256]{1,0:T(8,128)(2,1)}, bf16[544,256]{1,0:T(8,128)(2,1)}, u32[]{:S(2)}, u32[]{:S(2)}) collective-permute-start(bf16[544,256]{1,0:T(8,128)(2,1)} %get-tuple-element.36), channel_id=1, source_target_pairs={{0,1},{4,5},{8,9},{12,13},{16,17},{20,21},{24,25},{28,29}} | collective-permute-start | bytes 835592 | tf_op jit(solution)/shard_map/ppermute | solution.py:316
  14.8 20.5 %collective-permute-done.1.refs_2_ = bf16[256,2048]{1,0:T(8,128)(2,1)S(1)} collective-permute-done((bf16[256,2048]{1,0:T(8,128)(2,1)S(1)}, bf16[256,2048]{1,0:T(8,128)(2,1)S(1)}, u32[]{:S(2)}, u32[]{:S(2)}) %collective-permute-start.1) | collective-permute-done | bytes 1048608 | tf_op jit(solution)/shard_map/ppermute | solution.py:316
  35.3 1.5 %collective-permute-start.2 = (bf16[256,2048]{1,0:T(8,128)(2,1)S(1)}, bf16[256,2048]{1,0:T(8,128)(2,1)}, u32[]{:S(2)}, u32[]{:S(2)}) collective-permute-start(bf16[256,2048]{1,0:T(8,128)(2,1)S(1)} %collective-permute-done.1.refs_2_), channel_id=1, source_target_pairs={{0,4},{1,5},{2,6},{3,7},{4,0},{5,1},{6,2},{7,3},{8,12},{9,13},{10,... | collective-permute-start | bytes 3145736 | tf_op jit(solution)/shard_map/ppermute | solution.py:316
  42.0 1.3 %collective-permute-start.20 = (bf16[544,256]{1,0:T(8,128)(2,1)S(1)}, bf16[544,256]{1,0:T(8,128)(2,1)S(1)}, u32[]{:S(2)}, u32[]{:S(2)}) collective-permute-start(bf16[544,256]{1,0:T(8,128)(2,1)S(1)} %shard_map.78), channel_id=1, source_target_pairs={{1,2},{5,6},{9,10},{13,14},{17,18},{21,22},{25,26},{29,30}} | collective-permute-start | bytes 835592 | tf_op jit(solution)/shard_map/ppermute | solution.py:316
  44.2 1.3 %collective-permute-start.14 = (bf16[544,256]{1,0:T(8,128)(2,1)S(1)}, bf16[544,256]{1,0:T(8,128)(2,1)S(1)}, u32[]{:S(2)}, u32[]{:S(2)}) collective-permute-start(bf16[544,256]{1,0:T(8,128)(2,1)S(1)} %shard_map.75), channel_id=1, source_target_pairs={{1,2},{5,6},{9,10},{13,14},{17,18},{21,22},{25,26},{29,30}} | collective-permute-start | bytes 835592 | tf_op jit(solution)/shard_map/ppermute | solution.py:316
  45.5 5.7 %collective-permute-done.4.refs_5_ = bf16[2,256,256]{2,1,0:T(8,128)(2,1)S(1)} collective-permute-done((bf16[2,256,256]{2,1,0:T(8,128)(2,1)S(1)}, bf16[2,256,256]{2,1,0:T(8,128)(2,1)S(1)}, u32[]{:S(2)}, u32[]{:S(2)}) %collective-permute-start.4) | collective-permute-done | bytes 262176 | tf_op jit(solution)/shard_map/ppermute | solution.py:316
  51.2 1.7 %collective-permute-start.6 = (bf16[2,256,256]{2,1,0:T(8,128)(2,1)S(1)}, bf16[2,256,256]{2,1,0:T(8,128)(2,1)S(1)}, u32[]{:S(2)}, u32[]{:S(2)}) collective-permute-start(bf16[2,256,256]{2,1,0:T(8,128)(2,1)S(1)} %pad_maximum_fusion.1.refs_4_), channel_id=1, source_target_pairs={{0,2},{1,3},{2,0},{3,1},{4,6},{5,7},{6,4},{7,5},{8,10},{9,11},{10,... | collective-permute-start | bytes 786440 | tf_op jit(solution)/shard_map/ppermute | solution.py:316
  53.2 15.9 %collective-permute-done.6.refs_6_ = bf16[2,256,256]{2,1,0:T(8,128)(2,1)S(1)} collective-permute-done((bf16[2,256,256]{2,1,0:T(8,128)(2,1)S(1)}, bf16[2,256,256]{2,1,0:T(8,128)(2,1)S(1)}, u32[]{:S(2)}, u32[]{:S(2)}) %collective-permute-start.6) | collective-permute-done | bytes 262176 | tf_op jit(solution)/shard_map/ppermute | solution.py:316
  69.2 8.8 %collective-permute-start.21 = (bf16[544,256]{1,0:T(8,128)(2,1)S(1)}, bf16[544,256]{1,0:T(8,128)(2,1)S(1)}, u32[]{:S(2)}, u32[]{:S(2)}) collective-permute-start(bf16[544,256]{1,0:T(8,128)(2,1)S(1)} %shard_map.79), channel_id=1, source_target_pairs={{2,3},{6,7},{10,11},{14,15},{18,19},{22,23},{26,27},{30,31}} | collective-permute-start | bytes 835592 | tf_op jit(solution)/shard_map/ppermute | solution.py:316
  78.0 2.5 %collective-permute-done.8.refs_7_ = bf16[2,256,256]{2,1,0:T(8,128)(2,1)S(1)} collective-permute-done((bf16[2,256,256]{2,1,0:T(8,128)(2,1)S(1)}, bf16[2,256,256]{2,1,0:T(8,128)(2,1)S(1)}, u32[]{:S(2)}, u32[]{:S(2)}) %collective-permute-start.8) | collective-permute-done | bytes 262176 | tf_op jit(solution)/shard_map/ppermute | solution.py:316
  82.0 1.2 %collective-permute-start.9 = (bf16[2,256,256]{2,1,0:T(8,128)(2,1)S(1)}, bf16[2,256,256]{2,1,0:T(8,128)(2,1)S(1)}, u32[]{:S(2)}, u32[]{:S(2)}) collective-permute-start(bf16[2,256,256]{2,1,0:T(8,128)(2,1)S(1)} %collective-permute-done.8.refs_7_), channel_id=1, source_target_pairs={{0,16},{1,17},{2,18},{3,19},{4,20},{5,21},{6,22},{7,23},{8,24},{9,... | collective-permute-start | bytes 786440 | tf_op jit(solution)/shard_map/ppermute | solution.py:316
  83.4 1.3 %collective-permute-start.15 = (bf16[544,256]{1,0:T(8,128)(2,1)S(1)}, bf16[544,256]{1,0:T(8,128)(2,1)S(1)}, u32[]{:S(2)}, u32[]{:S(2)}) collective-permute-start(bf16[544,256]{1,0:T(8,128)(2,1)S(1)} %shard_map.76), channel_id=1, source_target_pairs={{2,3},{6,7},{10,11},{14,15},{18,19},{22,23},{26,27},{30,31}} | collective-permute-start | bytes 835592 | tf_op jit(solution)/shard_map/ppermute | solution.py:316
  84.7 4.8 %shard_map.77 = (f32[256,256]{1,0:T(8,128)S(1)}, f32[256,256]{1,0:T(8,128)S(1)}, bf16[256,256]{1,0:T(8,128)(2,1)S(1)}, bf16[256,256]{1,0:T(8,128)(2,1)S(1)}) custom-call(bf16[256,2048]{1,0:T(8,128)(2,1)S(1)} %get-tuple-element.22.refs_0_, bf16[256,2048]{1,0:T(8,128)(2,1)S(1)} %collective-permute-done.refs_1_, ...), custom_call_target="tpu_custom_call" | custom-call | tf_op jit(solution)/shard_map/pallas_call | solution.py:323
  89.6 1.8 %collective-permute-start.17 = (f32[256,256]{1,0:T(8,128)S(1)}, f32[256,256]{1,0:T(8,128)S(1)}, u32[]{:S(2)}, u32[]{:S(2)}) collective-permute-start(f32[256,256]{1,0:T(8,128)S(1)} %get-tuple-element.34), channel_id=1, source_target_pairs={{0,4},{1,5},{2,6},{3,7},{4,0},{5,1},{6,2},{7,3},{8,12},{9,13},{10,... | collective-permute-start | bytes 786440 | tf_op jit(solution)/shard_map/ppermute | solution.py:316
  91.4 1.7 %collective-permute-done.7.refs_6_ = bf16[2,256,256]{2,1,0:T(8,128)(2,1)S(1)} collective-permute-done((bf16[2,256,256]{2,1,0:T(8,128)(2,1)S(1)}, bf16[2,256,256]{2,1,0:T(8,128)(2,1)S(1)}, u32[]{:S(2)}, u32[]{:S(2)}) %collective-permute-start.7) | collective-permute-done | bytes 262176 | tf_op jit(solution)/shard_map/ppermute | solution.py:316
  94.3 4.4 %collective-permute-done.9.refs_7_ = bf16[2,256,256]{2,1,0:T(8,128)(2,1)S(1)} collective-permute-done((bf16[2,256,256]{2,1,0:T(8,128)(2,1)S(1)}, bf16[2,256,256]{2,1,0:T(8,128)(2,1)S(1)}, u32[]{:S(2)}, u32[]{:S(2)}) %collective-permute-start.9) | collective-permute-done | bytes 262176 | tf_op jit(solution)/shard_map/ppermute | solution.py:316
  98.7 2.9 %collective-permute-start.18 = (bf16[256,256]{1,0:T(8,128)(2,1)S(1)}, bf16[256,256]{1,0:T(8,128)(2,1)S(1)}, u32[]{:S(2)}, u32[]{:S(2)}) collective-permute-start(bf16[256,256]{1,0:T(8,128)(2,1)S(1)} %get-tuple-element.35), channel_id=1, source_target_pairs={{0,12},{1,13},{2,14},{3,15},{4,8},{5,9},{6,10},{7,11},{8,4},{9,5},... | collective-permute-start | bytes 393224 | tf_op jit(solution)/shard_map/ppermute | solution.py:316
  101.6 4.8 %shard_map.74 = (f32[256,256]{1,0:T(8,128)S(1)}, f32[256,256]{1,0:T(8,128)S(1)}, bf16[256,256]{1,0:T(8,128)(2,1)S(1)}, bf16[256,256]{1,0:T(8,128)(2,1)S(1)}) custom-call(bf16[256,2048]{1,0:T(8,128)(2,1)S(1)} %get-tuple-element.22.refs_0_, bf16[256,2048]{1,0:T(8,128)(2,1)S(1)} %collective-permute-done.refs_1_, ...), custom_call_target="tpu_custom_call" | custom-call | tf_op jit(solution)/shard_map/pallas_call | solution.py:323
  106.8 1.8 %collective-permute-start.12 = (bf16[256,256]{1,0:T(8,128)(2,1)S(1)}, bf16[256,256]{1,0:T(8,128)(2,1)S(1)}, u32[]{:S(2)}, u32[]{:S(2)}) collective-permute-start(bf16[256,256]{1,0:T(8,128)(2,1)S(1)} %get-tuple-element.28), channel_id=1, source_target_pairs={{0,12},{1,13},{2,14},{3,15},{4,8},{5,9},{6,10},{7,11},{8,4},{9,5},... | collective-permute-start | bytes 393224 | tf_op jit(solution)/shard_map/ppermute | solution.py:316
  108.7 2.0 %shard_map.80.refs_12_ = bf16[256,512]{1,0:T(8,128)(2,1)S(1)} custom-call(f32[256,256]{1,0:T(8,128)S(1)} %get-tuple-element.32.refs_0_, bf16[256,256]{1,0:T(8,128)(2,1)S(1)} %collective-permute-done.16.refs_1_, f32[256,256]{1,0:T(8,128)S(1)} %collective-permute-done.17.refs_2_, bf16[256,256]{1,0:T(8,128)(2,1)S(1)} %collective-permute-done.18.refs_3_, ...), custom_call_target="tpu_custom_call" | custom-call | tf_op jit(solution)/shard_map/pallas_call | solution.py:323
  111.2 3.4 %collective-permute-done.12.refs_3_ = bf16[256,256]{1,0:T(8,128)(2,1)S(1)} collective-permute-done((bf16[256,256]{1,0:T(8,128)(2,1)S(1)}, bf16[256,256]{1,0:T(8,128)(2,1)S(1)}, u32[]{:S(2)}, u32[]{:S(2)}) %collective-permute-start.12) | collective-permute-done | bytes 131104 | tf_op jit(solution)/shard_map/ppermute | solution.py:316
  114.6 2.7 %shard_map.81 = bf16[256,1024]{1,0:T(8,128)(2,1)} custom-call(f32[256,256]{1,0:T(8,128)S(1)} %get-tuple-element.25.refs_0_, bf16[256,256]{1,0:T(8,128)(2,1)S(1)} %collective-permute-done.10.refs_1_, f32[256,256]{1,0:T(8,128)S(1)} %collective-permute-done.11.refs_2_, bf16[256,256]{1,0:T(8,128)(2,1)S(1)} %collective-permute-done.12.refs_3_, ...), custom_call_target="tpu_custom_call" | custom-call | tf_op jit(solution)/shard_map/pallas_call | solution.py:323
  (65 shorter events, 19.1 us)
Async XLA Ops:
  11.3 24.0 %collective-permute-start.1 = (bf16[256,2048]{1,0:T(8,128)(2,1)S(1)}, bf16[256,2048]{1,0:T(8,128)(2,1)S(1)}, u32[]{:S(2)}, u32[]{:S(2)}) collective-permute-start(bf16[256,2048]{1,0:T(8,128)(2,1)S(1)} %get-tuple-element.23), channel_id=1, source_target_pairs={{0,8},{1,9},{2,10},{3,11},{4,12},{5,13},{6,14},{7,15},{8,0},{9,1},... | collective-permute-start | bytes 3145736 | tf_op jit(solution)/shard_map/ppermute | solution.py:316
  12.5 69.5 %collective-permute-start = (bf16[256,2048]{1,0:T(8,128)(2,1)S(1)}, bf16[256,2048]{1,0:T(8,128)(2,1)S(1)}, u32[]{:S(2)}, u32[]{:S(2)}) collective-permute-start(bf16[256,2048]{1,0:T(8,128)(2,1)S(1)} %get-tuple-element.22.refs_0_), channel_id=1, source_target_pairs={{0,4},{1,5},{2,6},{3,7},{4,0},{5,1},{6,2},{7,3},{8,12},{9,13},{10,... | collective-permute-start | bytes 3145736 | tf_op jit(solution)/shard_map/ppermute | solution.py:316
  13.4 25.4 %collective-permute-start.3 = (bf16[256,512]{1,0:T(8,128)(2,1)}, bf16[256,512]{1,0:T(8,128)(2,1)}, u32[]{:S(2)}, u32[]{:S(2)}) collective-permute-start(bf16[256,512]{1,0:T(8,128)(2,1)} %get-tuple-element.24), channel_id=1, source_target_pairs={{0,4},{1,5},{2,6},{3,7},{4,0},{5,1},{6,2},{7,3},{8,12},{9,13},{10,... | collective-permute-start | bytes 786440 | tf_op jit(solution)/shard_map/ppermute | solution.py:316
  13.4 26.4 %collective-permute-start.19 = (bf16[544,256]{1,0:T(8,128)(2,1)}, bf16[544,256]{1,0:T(8,128)(2,1)}, u32[]{:S(2)}, u32[]{:S(2)}) collective-permute-start(bf16[544,256]{1,0:T(8,128)(2,1)} %get-tuple-element.36), channel_id=1, source_target_pairs={{0,1},{4,5},{8,9},{12,13},{16,17},{20,21},{24,25},{28,29}} | collective-permute-start | bytes 835592 | tf_op jit(solution)/shard_map/ppermute | solution.py:316
  35.3 48.1 %collective-permute-start.2 = (bf16[256,2048]{1,0:T(8,128)(2,1)S(1)}, bf16[256,2048]{1,0:T(8,128)(2,1)}, u32[]{:S(2)}, u32[]{:S(2)}) collective-permute-start(bf16[256,2048]{1,0:T(8,128)(2,1)S(1)} %collective-permute-done.1.refs_2_), channel_id=1, source_target_pairs={{0,4},{1,5},{2,6},{3,7},{4,0},{5,1},{6,2},{7,3},{8,12},{9,13},{10,... | collective-permute-start | bytes 3145736 | tf_op jit(solution)/shard_map/ppermute | solution.py:316
  36.8 7.2 %collective-permute-start.13 = (bf16[544,256]{1,0:T(8,128)(2,1)}, bf16[544,256]{1,0:T(8,128)(2,1)S(1)}, u32[]{:S(2)}, u32[]{:S(2)}) collective-permute-start(bf16[544,256]{1,0:T(8,128)(2,1)} %get-tuple-element.29), channel_id=1, source_target_pairs={{0,1},{4,5},{8,9},{12,13},{16,17},{20,21},{24,25},{28,29}} | collective-permute-start | bytes 835592 | tf_op jit(solution)/shard_map/ppermute | solution.py:316
  42.0 10.9 %collective-permute-start.20 = (bf16[544,256]{1,0:T(8,128)(2,1)S(1)}, bf16[544,256]{1,0:T(8,128)(2,1)S(1)}, u32[]{:S(2)}, u32[]{:S(2)}) collective-permute-start(bf16[544,256]{1,0:T(8,128)(2,1)S(1)} %shard_map.78), channel_id=1, source_target_pairs={{1,2},{5,6},{9,10},{13,14},{17,18},{21,22},{25,26},{29,30}} | collective-permute-start | bytes 835592 | tf_op jit(solution)/shard_map/ppermute | solution.py:316
  43.3 7.9 %collective-permute-start.4 = (bf16[2,256,256]{2,1,0:T(8,128)(2,1)S(1)}, bf16[2,256,256]{2,1,0:T(8,128)(2,1)S(1)}, u32[]{:S(2)}, u32[]{:S(2)}) collective-permute-start(bf16[2,256,256]{2,1,0:T(8,128)(2,1)S(1)} %pad_maximum_fusion.1.refs_4_), channel_id=1, source_target_pairs={{0,1},{1,0},{2,3},{3,2},{4,5},{5,4},{6,7},{7,6},{8,9},{9,8},{10,11... | collective-permute-start | bytes 786440 | tf_op jit(solution)/shard_map/ppermute | solution.py:316
  44.2 37.5 %collective-permute-start.14 = (bf16[544,256]{1,0:T(8,128)(2,1)S(1)}, bf16[544,256]{1,0:T(8,128)(2,1)S(1)}, u32[]{:S(2)}, u32[]{:S(2)}) collective-permute-start(bf16[544,256]{1,0:T(8,128)(2,1)S(1)} %shard_map.75), channel_id=1, source_target_pairs={{1,2},{5,6},{9,10},{13,14},{17,18},{21,22},{25,26},{29,30}} | collective-permute-start | bytes 835592 | tf_op jit(solution)/shard_map/ppermute | solution.py:316
  51.2 18.0 %collective-permute-start.6 = (bf16[2,256,256]{2,1,0:T(8,128)(2,1)S(1)}, bf16[2,256,256]{2,1,0:T(8,128)(2,1)S(1)}, u32[]{:S(2)}, u32[]{:S(2)}) collective-permute-start(bf16[2,256,256]{2,1,0:T(8,128)(2,1)S(1)} %pad_maximum_fusion.1.refs_4_), channel_id=1, source_target_pairs={{0,2},{1,3},{2,0},{3,1},{4,6},{5,7},{6,4},{7,5},{8,10},{9,11},{10,... | collective-permute-start | bytes 786440 | tf_op jit(solution)/shard_map/ppermute | solution.py:316
  52.9 27.6 %collective-permute-start.8 = (bf16[2,256,256]{2,1,0:T(8,128)(2,1)S(1)}, bf16[2,256,256]{2,1,0:T(8,128)(2,1)S(1)}, u32[]{:S(2)}, u32[]{:S(2)}) collective-permute-start(bf16[2,256,256]{2,1,0:T(8,128)(2,1)S(1)} %pad_maximum_fusion.1.refs_4_), channel_id=1, source_target_pairs={{0,3},{1,2},{2,1},{3,0},{4,7},{5,6},{6,5},{7,4},{8,11},{9,10},{10,... | collective-permute-start | bytes 786440 | tf_op jit(solution)/shard_map/ppermute | solution.py:316
  69.2 37.3 %collective-permute-start.21 = (bf16[544,256]{1,0:T(8,128)(2,1)S(1)}, bf16[544,256]{1,0:T(8,128)(2,1)S(1)}, u32[]{:S(2)}, u32[]{:S(2)}) collective-permute-start(bf16[544,256]{1,0:T(8,128)(2,1)S(1)} %shard_map.79), channel_id=1, source_target_pairs={{2,3},{6,7},{10,11},{14,15},{18,19},{22,23},{26,27},{30,31}} | collective-permute-start | bytes 835592 | tf_op jit(solution)/shard_map/ppermute | solution.py:316
  80.5 9.1 %collective-permute-start.5 = (bf16[2,256,256]{2,1,0:T(8,128)(2,1)S(1)}, bf16[2,256,256]{2,1,0:T(8,128)(2,1)S(1)}, u32[]{:S(2)}, u32[]{:S(2)}) collective-permute-start(bf16[2,256,256]{2,1,0:T(8,128)(2,1)S(1)} %collective-permute-done.4.refs_5_), channel_id=1, source_target_pairs={{0,16},{1,17},{2,18},{3,19},{4,20},{5,21},{6,22},{7,23},{8,24},{9,... | collective-permute-start | bytes 786440 | tf_op jit(solution)/shard_map/ppermute | solution.py:316
  81.7 11.4 %collective-permute-start.7 = (bf16[2,256,256]{2,1,0:T(8,128)(2,1)S(1)}, bf16[2,256,256]{2,1,0:T(8,128)(2,1)S(1)}, u32[]{:S(2)}, u32[]{:S(2)}) collective-permute-start(bf16[2,256,256]{2,1,0:T(8,128)(2,1)S(1)} %collective-permute-done.6.refs_6_), channel_id=1, source_target_pairs={{0,16},{1,17},{2,18},{3,19},{4,20},{5,21},{6,22},{7,23},{8,24},{9,... | collective-permute-start | bytes 786440 | tf_op jit(solution)/shard_map/ppermute | solution.py:316
  82.0 16.7 %collective-permute-start.9 = (bf16[2,256,256]{2,1,0:T(8,128)(2,1)S(1)}, bf16[2,256,256]{2,1,0:T(8,128)(2,1)S(1)}, u32[]{:S(2)}, u32[]{:S(2)}) collective-permute-start(bf16[2,256,256]{2,1,0:T(8,128)(2,1)S(1)} %collective-permute-done.8.refs_7_), channel_id=1, source_target_pairs={{0,16},{1,17},{2,18},{3,19},{4,20},{5,21},{6,22},{7,23},{8,24},{9,... | collective-permute-start | bytes 786440 | tf_op jit(solution)/shard_map/ppermute | solution.py:316
  83.4 27.3 %collective-permute-start.15 = (bf16[544,256]{1,0:T(8,128)(2,1)S(1)}, bf16[544,256]{1,0:T(8,128)(2,1)S(1)}, u32[]{:S(2)}, u32[]{:S(2)}) collective-permute-start(bf16[544,256]{1,0:T(8,128)(2,1)S(1)} %shard_map.76), channel_id=1, source_target_pairs={{2,3},{6,7},{10,11},{14,15},{18,19},{22,23},{26,27},{30,31}} | collective-permute-start | bytes 835592 | tf_op jit(solution)/shard_map/ppermute | solution.py:316
  89.6 19.1 %collective-permute-start.17 = (f32[256,256]{1,0:T(8,128)S(1)}, f32[256,256]{1,0:T(8,128)S(1)}, u32[]{:S(2)}, u32[]{:S(2)}) collective-permute-start(f32[256,256]{1,0:T(8,128)S(1)} %get-tuple-element.34), channel_id=1, source_target_pairs={{0,4},{1,5},{2,6},{3,7},{4,0},{5,1},{6,2},{7,3},{8,12},{9,13},{10,... | collective-permute-start | bytes 786440 | tf_op jit(solution)/shard_map/ppermute | solution.py:316
  93.1 13.4 %collective-permute-start.16 = (bf16[256,256]{1,0:T(8,128)(2,1)S(1)}, bf16[256,256]{1,0:T(8,128)(2,1)S(1)}, u32[]{:S(2)}, u32[]{:S(2)}) collective-permute-start(bf16[256,256]{1,0:T(8,128)(2,1)S(1)} %get-tuple-element.33), channel_id=1, source_target_pairs={{0,8},{1,9},{2,10},{3,11},{4,12},{5,13},{6,14},{7,15},{8,0},{9,1},... | collective-permute-start | bytes 393224 | tf_op jit(solution)/shard_map/ppermute | solution.py:316
  98.7 10.0 %copy-start.13 = (f32[1,4,256]{2,1,0:T(4,128)S(1)}, f32[1,4,256]{2,1,0:T(4,128)}, u32[]{:S(2)}) copy-start(f32[1,4,256]{2,1,0:T(4,128)} %param.12) | copy-start | bytes 12292
  98.7 10.0 %copy-start.15 = (s32[1,256]{1,0:T(1,128)S(1)}, s32[1,256]{1,0:T(1,128)}, u32[]{:S(2)}) copy-start(s32[1,256]{1,0:T(1,128)} %refs_8_.3) | copy-start | bytes 3076
  98.7 8.1 %collective-permute-start.18 = (bf16[256,256]{1,0:T(8,128)(2,1)S(1)}, bf16[256,256]{1,0:T(8,128)(2,1)S(1)}, u32[]{:S(2)}, u32[]{:S(2)}) collective-permute-start(bf16[256,256]{1,0:T(8,128)(2,1)S(1)} %get-tuple-element.35), channel_id=1, source_target_pairs={{0,12},{1,13},{2,14},{3,15},{4,8},{5,9},{6,10},{7,11},{8,4},{9,5},... | collective-permute-start | bytes 393224 | tf_op jit(solution)/shard_map/ppermute | solution.py:316
  106.4 8.2 %collective-permute-start.11 = (f32[256,256]{1,0:T(8,128)S(1)}, f32[256,256]{1,0:T(8,128)S(1)}, u32[]{:S(2)}, u32[]{:S(2)}) collective-permute-start(f32[256,256]{1,0:T(8,128)S(1)} %get-tuple-element.27), channel_id=1, source_target_pairs={{0,4},{1,5},{2,6},{3,7},{4,0},{5,1},{6,2},{7,3},{8,12},{9,13},{10,... | collective-permute-start | bytes 786440 | tf_op jit(solution)/shard_map/ppermute | solution.py:316
  106.5 4.7 %collective-permute-start.10 = (bf16[256,256]{1,0:T(8,128)(2,1)S(1)}, bf16[256,256]{1,0:T(8,128)(2,1)S(1)}, u32[]{:S(2)}, u32[]{:S(2)}) collective-permute-start(bf16[256,256]{1,0:T(8,128)(2,1)S(1)} %get-tuple-element.26), channel_id=1, source_target_pairs={{0,8},{1,9},{2,10},{3,11},{4,12},{5,13},{6,14},{7,15},{8,0},{9,1},... | collective-permute-start | bytes 393224 | tf_op jit(solution)/shard_map/ppermute | solution.py:316
  106.8 7.8 %collective-permute-start.12 = (bf16[256,256]{1,0:T(8,128)(2,1)S(1)}, bf16[256,256]{1,0:T(8,128)(2,1)S(1)}, u32[]{:S(2)}, u32[]{:S(2)}) collective-permute-start(bf16[256,256]{1,0:T(8,128)(2,1)S(1)} %get-tuple-element.28), channel_id=1, source_target_pairs={{0,12},{1,13},{2,14},{3,15},{4,8},{5,9},{6,10},{7,11},{8,4},{9,5},... | collective-permute-start | bytes 393224 | tf_op jit(solution)/shard_map/ppermute | solution.py:316
  (14 other events, 45.8 us)

commit v2 on v0

--- a/solution.py
+++ b/solution.py
@@ -80,35 +80,44 @@
     return ref[base : base + size, :], normer, top
 
 
-def prepare_kernel(heads, ng, nx, *refs):
-    k_ref, v_ref, x_ref, w_ref, gate_ref, forget_ref, reset_ref = refs[:7]
-    wsend_ref, xown_ref = refs[7:9]
-    xaway = refs[9 : 8 + nx]
-    chunks = refs[8 + nx : 8 + nx + 3 * ng]
-    kbuf, vbuf, sems = refs[8 + nx + 3 * ng :]
+def slice_kernel(ng, nx, x_ref, w_ref, send_ref, *refs):
+    own, away, sems = refs[:ng], refs[ng : ng + nx - 1], refs[ng + nx - 1]
+    group, dp = lax.axis_index("groups"), lax.axis_index("dp")
+    core, x = lax.rem(dp, CORES), lax.div(dp, CORES)
+    half, width, depth = send_ref.shape[1], own[0].shape[1], away[0].shape[1]
+    copies = []
+
+    def copy(ref, column, target):
+        source = ref.at[:, pl.ds(pl.multiple_of(column, width), target.shape[1])]
+        copies.append(pltpu.make_async_copy(source, target, sems.at[len(copies)]))
+        copies[-1].start()
+
+    copy(w_ref, (1 - core) * half, send_ref)
+    for r in range(ng):
+        copy(w_ref, core * half + lax.rem(group + r, ng) * width, own[r])
+    for rel in range(1, nx):
+        copy(x_ref, lax.rem(x + rel, nx) * depth, away[rel - 1])
+    for each in copies:
+        each.wait()
+
+
+def pack_kernel(own_ref, swapped_ref, out_ref):
+    _, width = own_ref.shape
+    column = pl.multiple_of(lax.axis_index("groups") * width, width)
+    out_ref[0] = own_ref[...]
+    out_ref[1] = swapped_ref[:, pl.ds(column, width)]
+
+
+def state_kernel(heads, ng, *refs):
+    k_ref, v_ref, x_ref, gate_ref, forget_ref, reset_ref, xown_ref = refs[:7]
+    chunks, sem = refs[7 : 7 + 3 * ng], refs[7 + 3 * ng]
     length = k_ref.shape[0]
     size, vsize = k_ref.shape[1] // heads, v_ref.shape[1] // heads
     group, dp = lax.axis_index("groups"), lax.axis_index("dp")
-    core, x = lax.rem(dp, CORES), lax.div(dp, CORES)
-    half = wsend_ref.shape[1]
     depth = xown_ref.shape[1]
-
-    def block(ref, at, count):
-        return ref.at[:, pl.ds(pl.multiple_of(at * count, count), count)]
-
-    moved = [
-        (k_ref, kbuf),
-        (v_ref, vbuf),
-        (block(w_ref, 1 - core, half), wsend_ref),
-    ]
-    for rel in range(1, nx):
-        moved.append((block(x_ref, lax.rem(x + rel, nx), depth), xaway[rel - 1]))
-    moved.append((block(x_ref, x, depth), xown_ref))
-    copies = []
-    for i, (source, target) in enumerate(moved):
-        copy = pltpu.make_async_copy(source, target, sems.at[i])
-        copy.start()
-        copies.append(copy)
+    column = pl.multiple_of(lax.div(dp, CORES) * depth, depth)
+    copy = pltpu.make_async_copy(x_ref.at[:, pl.ds(column, depth)], xown_ref, sem)
+    copy.start()
     count = lane_scan(padded(reset_ref[...].astype(f32)))[0:1]
     cumulative = lane_scan(padded(log_sigmoid(forget_ref[...])))[0:heads]
     total = cumulative[:, length - 1 : length]
@@ -117,8 +126,6 @@
     top = jnp.max(expo, axis=1, keepdims=True)
     weight = padded(jnp.exp(expo - top)).T
     gap = jnp.where(final > 0, very_low, total)
-    copies[0].wait()
-    copies[1].wait()
     for r in range(ng):
         own_ref, msg_ref, side_ref = chunks[3 * r : 3 * r + 3]
         for j in range(heads // ng):
@@ -131,8 +138,8 @@
                     chosen = jnp.where(within == i, values[j * ng + i], chosen)
                 return chosen
 
-            keys = kbuf[:, pl.ds(pl.multiple_of(head * size, size), size)].astype(f32)
-            values = vbuf[:, pl.ds(pl.multiple_of(head * vsize, vsize), vsize)]
+            keys = k_ref[:, pl.ds(pl.multiple_of(head * size, size), size)].astype(f32)
+            values = v_ref[:, pl.ds(pl.multiple_of(head * vsize, vsize), vsize)]
             scale = pick([weight[:, h : h + 1] for h in range(heads)])
             this_top = pick([top[h : h + 1] for h in range(heads)])
             this_gap = pick([gap[h : h + 1] for h in range(heads)])
@@ -146,8 +153,7 @@
             side_ref[j * 8 + 1 : j * 8 + 2, :] = jnp.broadcast_to(this_top, normer.shape)
             side_ref[j * 8 + 2 : j * 8 + 3, :] = jnp.broadcast_to(this_gap, normer.shape)
             store_message(msg_ref, j * (size + EXTRA), size, memory, normer, this_top)
-    for copy in copies[2:]:
-        copy.wait()
+    copy.wait()
 
 
 def combine_kernel(heads, prev_ref, own_ref, side_ref, msg_ref):
@@ -166,35 +172,41 @@
         store_message(msg_ref, h * stride, size, joined, early * normer + late * own_normer, both)
 
 
-def project_kernel(nz, nx, *refs):
-    count = CORES * nx
-    blocks, parts = refs[:count], refs[count : count + nz]
-    outs = refs[count + nz : 2 * count + nz]
-    tokens, whole, sems = refs[2 * count + nz :]
-    rows = parts[0].shape[1]
-    place = lax.axis_index("ctx")
+def away_kernel(nz, ng, phase, count, *refs):
+    split = nz == 4
+    first = 2 if phase else 1
+    tokens, parts = refs[:count], refs[count : count + first + nz - 1 + split]
+    outs, whole = refs[count + len(parts) : -1], refs[-1]
+    rows, width = parts[-1].shape[1:]
+    place, group = lax.axis_index("ctx"), lax.axis_index("groups")
     core = lax.rem(lax.axis_index("dp"), CORES)
-    copies = []
-    for s in range(nz):
-        source = place ^ s
+    if phase:
+        column = pl.multiple_of(lax.rem(group + phase, ng) * width, width)
+        values = [(parts[0][...], parts[1][:, pl.ds(column, width)])]
+    else:
+        values = [(parts[0][0], parts[0][1])]
+    steps = list(range(nz))
+    for part in parts[first:]:
+        values.append((part[0], part[1]))
+    if split:
+        inner = jnp.logical_or(place == 1, place == 2)
+        outer = values.pop()
+        values[-1] = tuple(jnp.where(inner, a, b) for a, b in zip(values[-1], outer))
+        steps = [0, 2, 1, 3]
+    for at, s in enumerate(steps):
         for j in range(CORES):
             owner = lax.rem(core + j, CORES)
-            row = pl.multiple_of((owner * nz + source) * rows, rows)
-            copies.append((parts[s].at[j], whole.at[pl.ds(row, rows)]))
-    sequence = list(range(CORES, count)) + list(range(CORES))
-    for i in sequence:
-        copies.append((blocks[i], tokens.at[i]))
-    started = []
-    for i, (source, target) in enumerate(copies):
-        copy = pltpu.make_async_copy(source, target, sems.at[i])
-        copy.start()
-        started.append(copy)
-    for copy in started[: nz * CORES]:
-        copy.wait()
-    for at, i in enumerate(sequence):
-        started[nz * CORES + at].wait()
-        value = jnp.dot(tokens[i], whole[...], preferred_element_type=f32)
-        outs[i][...] = value.astype(outs[i].dtype)
+            row = pl.multiple_of((owner * nz + (place ^ s)) * rows, rows)
+            whole[pl.ds(row, rows), :] = values[at][j]
+    for token, out in zip(tokens, outs):
+        value = jnp.dot(token[...], whole[...], preferred_element_type=f32)
+        out[...] = value.astype(out.dtype)
+
+
+def keep_kernel(*refs):
+    tokens, whole, outs = refs[:CORES], refs[CORES], refs[CORES + 1 :]
+    for token, out in zip(tokens, outs):
+        out[...] = jnp.dot(token[...], whole[...], preferred_element_type=f32)
 
 
 def read_kernel(heads, ng, nx, hops, phase, *refs):
@@ -203,7 +215,7 @@
     at = CORES * nx + 5
     done = phase if phase == ng - 1 else 0
     states, earlier = refs[at : at + hops], refs[at + hops : at + hops + done]
-    out_ref, kbuf, vbuf, state, sems = refs[at + hops + done :]
+    out_ref, state, sem = refs[at + hops + done :]
     length = k_ref.shape[0]
     size, vsize = k_ref.shape[1] // heads, v_ref.shape[1] // heads
     factor = size ** (-0.5)
@@ -217,19 +229,11 @@
     def head_of(j, r):
         return slot_of(j) * ng + lax.rem(group + r, ng)
 
-    copies = []
-    for j in range(CORES):
-        head = head_of(j, phase)
-        for i, (ref, buffer, wide) in enumerate(((k_ref, kbuf, size), (v_ref, vbuf, vsize))):
-            source = ref.at[:, pl.ds(pl.multiple_of(head * wide, wide), wide)]
-            copy = pltpu.make_async_copy(source, buffer.at[j], sems.at[2 * j + i])
-            copy.start()
-            copies.append(copy)
     for h in range(hops):
 
         @pl.when(place == h + 1)
         def _():
-            pltpu.make_async_copy(states[h], state, sems.at[2 * CORES]).start()
+            pltpu.make_async_copy(states[h], state, sem).start()
 
     @pl.when(place == 0)
     def _():
@@ -256,16 +260,16 @@
 
     @pl.when(place > 0)
     def _():
-        pltpu.make_async_copy(states[0], state, sems.at[2 * CORES]).wait()
-
-    for copy in copies:
-        copy.wait()
+        pltpu.make_async_copy(states[0], state, sem).wait()
+
     for j in range(CORES):
         total = partials[j][0][...]
         for other in partials[j][1:]:
             total = total + other[...].astype(f32)
         query = total.astype(bf16)
-        keys, values = kbuf[j], vbuf[j]
+        head = head_of(j, phase)
+        keys = k_ref[:, pl.ds(pl.multiple_of(head * size, size), size)]
+        values = v_ref[:, pl.ds(pl.multiple_of(head * vsize, vsize), vsize)]
         base = pl.multiple_of(slot_of(j) * stride, EXTRA)
         memory = state[pl.ds(base, size), :]
         extra = state[pl.ds(pl.multiple_of(base + size, EXTRA), EXTRA), :].astype(f32)
@@ -302,6 +306,17 @@
 ANY = pl.BlockSpec(memory_space=pl.ANY)
 
 
+def gather_plan(nz):
+    if nz != 4:
+        return [(s, None, lambda z, s=s: z ^ s) for s in range(1, nz)]
+    return [
+        ("2", None, lambda z: z ^ 2),
+        ("1", None, lambda z: z ^ 1),
+        ("in", None, lambda z: z ^ 3 if z in (1, 2) else None),
+        ("out", "2", lambda z: {1: 0, 2: 3}.get(z)),
+    ]
+
+
 def make_body(mesh):
     ng, nd, nz = (mesh.shape[a] for a in AXES)
     nx = nd // CORES
@@ -313,7 +328,8 @@
         return send(value, lambda g, x, k, z: (g, x, 1 - k, z))
 
     def call(kernel, *args, **options):
-        return pl.pallas_call(kernel, **options)(*args)
+        params = pltpu.CompilerParams(vmem_limit_bytes=20 * 2**20)
+        return pl.pallas_call(kernel, compiler_params=params, **options)(*args)
 
     def body(normed_input, query_weight, key_vectors, value_vectors, input_gate, forget_gate, resets):
         _, length, features = normed_input.shape
@@ -324,27 +340,49 @@
         keys, values = key_vectors[0], value_vectors[0]
         gate, forget = input_gate[0], forget_gate[0]
         vwidth = values.shape[1]
-        group = lax.axis_index("groups")
-        dp = lax.axis_index("dp")
-        core = dp % CORES
         half = columns // CORES
         depth = features // nx
         flat = normed_input[0]
-
-        def columns_of(value, at, count):
-            return lax.dynamic_slice_in_dim(value, at * count, count, 1)
 
         stride = size + EXTRA
         vsize = vwidth // heads
         slots = heads // ng
         message = jax.ShapeDtypeStruct((slots * stride, vsize), bf16)
         block = jax.ShapeDtypeStruct((length, depth), flat.dtype)
+        hbm_tokens = pltpu.with_memory_space_constraint(flat, pltpu.HBM)
+        hbm_weight = pltpu.with_memory_space_constraint(query_weight, pltpu.HBM)
+        rows = query_weight.shape[0]
+        quarter = jax.ShapeDtypeStruct((rows, width), query_weight.dtype)
+        sliced = call(
+            functools.partial(slice_kernel, ng, nx),
+            hbm_tokens, hbm_weight,
+            out_shape=(
+                jax.ShapeDtypeStruct((rows, half), query_weight.dtype),
+                *[quarter] * ng,
+                *[block] * (nx - 1),
+            ),
+            in_specs=[ANY] * 2,
+            out_specs=(VMEM,) * (ng + nx),
+            scratch_shapes=[pltpu.SemaphoreType.DMA((ng + nx,))],
+        )
+        swapped = over_core(sliced[0])
+        own_parts = sliced[1 : 1 + ng]
+        arrived = [
+            send(sliced[ng + rel], lambda g, x, k, z: (g, (x + rel) % nx, k, z))
+            for rel in range(1, nx)
+        ]
+        packed = call(
+            pack_kernel,
+            own_parts[0], swapped,
+            out_shape=jax.ShapeDtypeStruct((CORES, rows, width), bf16),
+            in_specs=[VMEM] * 2,
+            out_specs=VMEM,
+        )
         prepared = call(
-            functools.partial(prepare_kernel, heads, ng, nx),
-            keys, values, flat, query_weight, gate, forget, resets,
+            functools.partial(state_kernel, heads, ng),
+            keys, values, hbm_tokens, gate, forget, resets,
             out_shape=(
-                jax.ShapeDtypeStruct((query_weight.shape[0], half), query_weight.dtype),
-                *[block] * nx,
+                block,
                 *[
                     jax.ShapeDtypeStruct((slots * size, vsize), f32),
                     message,
@@ -352,37 +390,33 @@
                 ]
                 * ng,
             ),
-            in_specs=[ANY] * 4 + [VMEM] * 3,
-            out_specs=(ANY,) * (1 + nx) + (VMEM,) * (3 * ng),
-            scratch_shapes=[
-                pltpu.VMEM(keys.shape, bf16),
-                pltpu.VMEM(values.shape, bf16),
-                pltpu.SemaphoreType.DMA((3 + nx,)),
-            ],
+            in_specs=[VMEM] * 2 + [ANY] + [VMEM] * 3,
+            out_specs=(VMEM,) * (1 + 3 * ng),
+            scratch_shapes=[pltpu.SemaphoreType.DMA(())],
         )
-        swapped = over_core(prepared[0])
-        kept = columns_of(query_weight, core, half)
-        parts = [
-            jnp.stack([columns_of(v, (group + r) % ng, width) for v in (kept, swapped)])
-            for r in range(ng)
-        ]
-        tokens = [prepared[1]]
-        arrived = [
-            send(prepared[1 + rel], lambda g, x, k, z: (g, (x + rel) % nx, k, z))
-            for rel in range(1, nx)
-        ]
+        tokens = [prepared[0]]
         tokens.append(over_core(tokens[0]))
         for rel, value in enumerate(arrived):
             tokens.extend([value, over_core(value)])
-        pieces = [[parts[r]] for r in range(ng)]
-        for s in range(1, nz):
-            mine = send(parts[0], lambda g, x, k, z: (g, x, k, z ^ s))
+        pieces = [[packed]] + [[own_parts[r], swapped] for r in range(1, ng)]
+        gathered = {}
+        for name, origin, where in gather_plan(nz):
+            value = packed if origin is None else gathered[origin]
+            mine = send(value, lambda g, x, k, z: None if where(z) is None else (g, x, k, where(z)))
+            gathered[name] = mine
             pieces[0].append(mine)
             for r in range(1, ng):
-                pieces[r].append(send(mine, lambda g, x, k, z: ((g - r) % ng, x, k, z)))
+                pieces[r].append(
+                    send(
+                        mine,
+                        lambda g, x, k, z: (
+                            ((g - r) % ng, x, k, z) if z in map(where, range(nz)) else None
+                        ),
+                    )
+                )
         states = [[] for _ in range(ng)]
         for r in range(ng):
-            own, current, side = prepared[1 + nx + 3 * r : 4 + nx + 3 * r]
+            own, current, side = prepared[1 + 3 * r : 4 + 3 * r]
             for hop in range(1, nz):
                 state = send(current, lambda g, x, k, z: (g, x, k, z + 1) if z == hop - 1 else None)
                 states[r].append(state)
@@ -398,18 +432,22 @@
         for r in range(ng):
             piece = jax.ShapeDtypeStruct((length, width), f32)
             small = jax.ShapeDtypeStruct((length, width), bf16)
-            sums = call(
-                functools.partial(project_kernel, nz, nx),
-                *tokens, *pieces[r],
-                out_shape=(piece,) * CORES + (small,) * (CORES * (nx - 1)),
-                in_specs=[ANY] * (CORES * nx + nz),
-                out_specs=(VMEM,) * (CORES * nx),
-                scratch_shapes=[
-                    pltpu.VMEM((CORES * nx, length, depth), bf16),
-                    pltpu.VMEM((depth, width), bf16),
-                    pltpu.SemaphoreType.DMA((CORES * (nx + nz),)),
-                ],
+            count = CORES * (nx - 1)
+            sent = call(
+                functools.partial(away_kernel, nz, ng, r, count),
+                *tokens[CORES:], *pieces[r],
+                out_shape=(small,) * count + (jax.ShapeDtypeStruct((depth, width), bf16),),
+                in_specs=[VMEM] * (count + len(pieces[r])),
+                out_specs=(VMEM,) * (count + 1),
             )
+            kept = call(
+                keep_kernel,
+                *tokens[:CORES], sent[-1],
+                out_shape=(piece,) * CORES,
+                in_specs=[VMEM] * (CORES + 1),
+                out_specs=(VMEM,) * CORES,
+            )
+            sums = [*kept, *sent[:-1]]
             partials = [[sums[0]], [over_core(sums[1])]]
             for rel in range(1, nx):
                 for j in range(CORES):
@@ -427,14 +465,12 @@
                     out_shape=jax.ShapeDtypeStruct(
                         (length, vwidth if last else CORES * vsize), bf16
                     ),
-                    in_specs=[VMEM] * (CORES * nx) + [ANY] * 2 + [VMEM] * 3
+                    in_specs=[VMEM] * (CORES * nx + 5)
                     + [ANY] * (nz - 1) + [VMEM] * (r if last else 0),
                     out_specs=VMEM,
                     scratch_shapes=[
-                        pltpu.VMEM((CORES, length, size), bf16),
-                        pltpu.VMEM((CORES, length, vsize), bf16),
                         pltpu.VMEM(message.shape, bf16),
-                        pltpu.SemaphoreType.DMA((2 * CORES + 1,)),
+                        pltpu.SemaphoreType.DMA(()),
                     ],
                 )
             )

time: 187 us -> 92.4 us (0.49)
  the two profiles are of different devices: /device:TPU:17 before, /device:TPU:0 now
where the time goes in v2:
time: 92.4 us; the launch traced here: 91.4 us
  waiting for transfers between devices  43.5 us (47%)
  starting transfers between devices  35.2 us (38%)
  Pallas kernels  12.3 us (13%)
    ppermute x24, waiting for transfers between devices, send(): return lax.ppermute(value, AXES, moves(mesh, where))  43.5 us
    ppermute x24, starting transfers between devices, send(): return lax.ppermute(value, AXES, moves(mesh, where))  35.2 us
    pallas_call x13, Pallas kernels, call(): return pl.pallas_call(kernel, compiler_params=params, **options)(*args)  12.3 us
  transfers between devices with their start and end apart: 24, of which 7 were waited for; matrix products, arithmetic and copies ran while one was open for 0% of the time, Pallas kernels for 9%

profile of v2, /device:TPU:0, one launch (start us, length us, event | category | flops | bytes accessed | tf_op | source)
XLA Modules:
  0.0 91.4 jit_solution(1775882596718340099)
XLA Ops:
  0.0 1.6 %shard_map.74 = (bf16[256,512]{1,0:T(8,128)(2,1)S(1)}, bf16[256,256]{1,0:T(8,128)(2,1)S(1)}, bf16[256,256]{1,0:T(8,128)(2,1)S(1)}, bf16[256,2048]{1,0:T(8,128)(2,1)S(1)}) custom-call(bf16[256,4096]{1,0:T(8,128)(2,1)} %bitcast.18, bf16[256,1024]{1,0:T(8,128)(2,1)} %w_ref.1), custom_call_target="tpu_custom_call" | custom-call | tf_op jit(solution)/shard_map/pallas_call | solution.py:332
  1.6 3.0 %collective-permute-start.1 = (bf16[256,2048]{1,0:T(8,128)(2,1)S(1)}, bf16[256,2048]{1,0:T(8,128)(2,1)S(1)}, u32[]{:S(2)}, u32[]{:S(2)}) collective-permute-start(bf16[256,2048]{1,0:T(8,128)(2,1)S(1)} %get-tuple-element.27), channel_id=1, source_target_pairs={{0,8},{1,9},{2,10},{3,11},{4,12},{5,13},{6,14},{7,15},{8,0},{9,1},... | collective-permute-start | bytes 3145736 | tf_op jit(solution)/shard_map/ppermute | solution.py:325
  4.7 2.6 %shard_map.73 = (bf16[256,2048]{1,0:T(8,128)(2,1)S(1)}, f32[512,256]{1,0:T(8,128)S(1)}, bf16[544,256]{1,0:T(8,128)(2,1)S(1)}, f32[16,256]{1,0:T(8,128)S(1)}, f32...) custom-call(bf16[256,1024]{1,0:T(8,128)(2,1)S(1)} %bitcast.6, ...), custom_call_target="tpu_custom_call" | custom-call | tf_op jit(solution)/shard_map/pallas_call | solution.py:332
  7.9 3.5 %collective-permute-start.21 = (bf16[544,256]{1,0:T(8,128)(2,1)S(1)}, bf16[544,256]{1,0:T(8,128)(2,1)S(1)}, u32[]{:S(2)}, u32[]{:S(2)}) collective-permute-start(bf16[544,256]{1,0:T(8,128)(2,1)S(1)} %get-tuple-element.44), channel_id=1, source_target_pairs={{0,1},{4,5},{8,9},{12,13},{16,17},{20,21},{24,25},{28,29}} | collective-permute-start | bytes 835592 | tf_op jit(solution)/shard_map/ppermute | solution.py:325
  11.4 1.3 %collective-permute-start.15 = (bf16[544,256]{1,0:T(8,128)(2,1)S(1)}, bf16[544,256]{1,0:T(8,128)(2,1)S(1)}, u32[]{:S(2)}, u32[]{:S(2)}) collective-permute-start(bf16[544,256]{1,0:T(8,128)(2,1)S(1)} %get-tuple-element.36), channel_id=1, source_target_pairs={{0,1},{4,5},{8,9},{12,13},{16,17},{20,21},{24,25},{28,29}} | collective-permute-start | bytes 835592 | tf_op jit(solution)/shard_map/ppermute | solution.py:325
  12.7 15.1 %collective-permute-done.1.refs_0_ = bf16[256,2048]{1,0:T(8,128)(2,1)S(1)} collective-permute-done((bf16[256,2048]{1,0:T(8,128)(2,1)S(1)}, bf16[256,2048]{1,0:T(8,128)(2,1)S(1)}, u32[]{:S(2)}, u32[]{:S(2)}) %collective-permute-start.1) | collective-permute-done | bytes 1048608 | tf_op jit(solution)/shard_map/ppermute | solution.py:325
  28.5 4.7 %collective-permute-start.6 = (bf16[2,256,256]{2,1,0:T(8,128)(2,1)S(1)}, bf16[2,256,256]{2,1,0:T(8,128)(2,1)S(1)}, u32[]{:S(2)}, u32[]{:S(2)}) collective-permute-start(bf16[2,256,256]{2,1,0:T(8,128)(2,1)S(1)} %shard_map.75.refs_2_), channel_id=1, source_target_pairs={{0,1},{1,0},{2,3},{3,2},{4,5},{5,4},{6,7},{7,6},{8,9},{9,8},{10,11... | collective-permute-start | bytes 786440 | tf_op jit(solution)/shard_map/ppermute | solution.py:325
  34.1 7.6 %collective-permute-start.4 = (bf16[2,256,256]{2,1,0:T(8,128)(2,1)S(1)}, bf16[2,256,256]{2,1,0:T(8,128)(2,1)S(1)}, u32[]{:S(2)}, u32[]{:S(2)}) collective-permute-start(bf16[2,256,256]{2,1,0:T(8,128)(2,1)S(1)} %shard_map.75.refs_2_), channel_id=1, source_target_pairs={{0,2},{1,3},{2,0},{3,1},{4,6},{5,7},{6,4},{7,5},{8,10},{9,11},{10,... | collective-permute-start | bytes 786440 | tf_op jit(solution)/shard_map/ppermute | solution.py:325
  42.6 10.4 %collective-permute-done.4.refs_3_ = bf16[2,256,256]{2,1,0:T(8,128)(2,1)S(1)} collective-permute-done((bf16[2,256,256]{2,1,0:T(8,128)(2,1)S(1)}, bf16[2,256,256]{2,1,0:T(8,128)(2,1)S(1)}, u32[]{:S(2)}, u32[]{:S(2)}) %collective-permute-start.4) | collective-permute-done | bytes 262176 | tf_op jit(solution)/shard_map/ppermute | solution.py:325
  53.7 1.3 %collective-permute-start.10 = (bf16[2,256,256]{2,1,0:T(8,128)(2,1)S(1)}, bf16[2,256,256]{2,1,0:T(8,128)(2,1)S(1)}, u32[]{:S(2)}, u32[]{:S(2)}) collective-permute-start(bf16[2,256,256]{2,1,0:T(8,128)(2,1)S(1)} %collective-permute-done.4.refs_3_), channel_id=1, source_target_pairs={{1,0},{2,3},{5,4},{6,7},{9,8},{10,11},{13,12},{14,15},{17,16},{18,... | collective-permute-start | bytes 786440 | tf_op jit(solution)/shard_map/ppermute | solution.py:325
  55.9 1.6 %collective-permute-start.7 = (bf16[2,256,256]{2,1,0:T(8,128)(2,1)S(1)}, bf16[2,256,256]{2,1,0:T(8,128)(2,1)S(1)}, u32[]{:S(2)}, u32[]{:S(2)}) collective-permute-start(bf16[2,256,256]{2,1,0:T(8,128)(2,1)S(1)} %collective-permute-done.6.refs_4_), channel_id=1, source_target_pairs={{0,16},{1,17},{2,18},{3,19},{4,20},{5,21},{6,22},{7,23},{8,24},{9,... | collective-permute-start | bytes 786440 | tf_op jit(solution)/shard_map/ppermute | solution.py:325
  57.5 9.6 %collective-permute-done.10.refs_6_ = bf16[2,256,256]{2,1,0:T(8,128)(2,1)S(1)} collective-permute-done((bf16[2,256,256]{2,1,0:T(8,128)(2,1)S(1)}, bf16[2,256,256]{2,1,0:T(8,128)(2,1)S(1)}, u32[]{:S(2)}, u32[]{:S(2)}) %collective-permute-start.10) | collective-permute-done | bytes 262176 | tf_op jit(solution)/shard_map/ppermute | solution.py:325
  67.6 3.4 %collective-permute-start.11 = (bf16[2,256,256]{2,1,0:T(8,128)(2,1)S(1)}, bf16[2,256,256]{2,1,0:T(8,128)(2,1)S(1)}, u32[]{:S(2)}, u32[]{:S(2)}) collective-permute-start(bf16[2,256,256]{2,1,0:T(8,128)(2,1)S(1)} %collective-permute-done.10.refs_6_), channel_id=1, source_target_pairs={{0,16},{3,19},{4,20},{7,23},{8,24},{11,27},{12,28},{15,31},{16,0},... | collective-permute-start | bytes 786440 | tf_op jit(solution)/shard_map/ppermute | solution.py:325
  71.9 0.8 shard_map.80
  72.7 0.7 shard_map.81
  73.5 1.6 %collective-permute-start.18 = (bf16[256,256]{1,0:T(8,128)(2,1)S(1)}, bf16[256,256]{1,0:T(8,128)(2,1)S(1)}, u32[]{:S(2)}, u32[]{:S(2)}) collective-permute-start(bf16[256,256]{1,0:T(8,128)(2,1)S(1)} %get-tuple-element.41), channel_id=1, source_target_pairs={{0,8},{1,9},{2,10},{3,11},{4,12},{5,13},{6,14},{7,15},{8,0},{9,1},... | collective-permute-start | bytes 393224 | tf_op jit(solution)/shard_map/ppermute | solution.py:325
  75.0 1.3 %collective-permute-done.5.refs_4_ = bf16[2,256,256]{2,1,0:T(8,128)(2,1)S(1)} collective-permute-done((bf16[2,256,256]{2,1,0:T(8,128)(2,1)S(1)}, bf16[2,256,256]{2,1,0:T(8,128)(2,1)S(1)}, u32[]{:S(2)}, u32[]{:S(2)}) %collective-permute-start.5) | collective-permute-done | bytes 262176 | tf_op jit(solution)/shard_map/ppermute | solution.py:325
  76.3 3.0 %collective-permute-done.11.refs_7_ = bf16[2,256,256]{2,1,0:T(8,128)(2,1)S(1)} collective-permute-done((bf16[2,256,256]{2,1,0:T(8,128)(2,1)S(1)}, bf16[2,256,256]{2,1,0:T(8,128)(2,1)S(1)}, u32[]{:S(2)}, u32[]{:S(2)}) %collective-permute-start.11) | collective-permute-done | bytes 262176 | tf_op jit(solution)/shard_map/ppermute | solution.py:325
  79.3 0.8 shard_map.76
  81.4 1.5 %collective-permute-start.12 = (bf16[256,256]{1,0:T(8,128)(2,1)S(1)}, bf16[256,256]{1,0:T(8,128)(2,1)S(1)}, u32[]{:S(2)}, u32[]{:S(2)}) collective-permute-start(bf16[256,256]{1,0:T(8,128)(2,1)S(1)} %get-tuple-element.33), channel_id=1, source_target_pairs={{0,8},{1,9},{2,10},{3,11},{4,12},{5,13},{6,14},{7,15},{8,0},{9,1},... | collective-permute-start | bytes 393224 | tf_op jit(solution)/shard_map/ppermute | solution.py:325
  82.9 1.8 %shard_map.84.refs_12_ = bf16[256,512]{1,0:T(8,128)(2,1)S(1)} custom-call(f32[256,256]{1,0:T(8,128)S(1)} %get-tuple-element.40.refs_0_, bf16[256,256]{1,0:T(8,128)(2,1)S(1)} %collective-permute-done.18.refs_1_, f32[256,256]{1,0:T(8,128)S(1)} %collective-permute-done.19.refs_2_, bf16[256,256]{1,0:T(8,128)(2,1)S(1)} %collective-permute-done.20.refs_3_, ...), custom_call_target="tpu_custom_call" | custom-call | tf_op jit(solution)/shard_map/pallas_call | solution.py:332
  84.7 3.0 %collective-permute-done.12.refs_1_ = bf16[256,256]{1,0:T(8,128)(2,1)S(1)} collective-permute-done((bf16[256,256]{1,0:T(8,128)(2,1)S(1)}, bf16[256,256]{1,0:T(8,128)(2,1)S(1)}, u32[]{:S(2)}, u32[]{:S(2)}) %collective-permute-start.12) | collective-permute-done | bytes 131104 | tf_op jit(solution)/shard_map/ppermute | solution.py:325
  87.8 1.0 %collective-permute-done.14.refs_3_ = bf16[256,256]{1,0:T(8,128)(2,1)S(1)} collective-permute-done((bf16[256,256]{1,0:T(8,128)(2,1)S(1)}, bf16[256,256]{1,0:T(8,128)(2,1)S(1)}, u32[]{:S(2)}, u32[]{:S(2)}) %collective-permute-start.14) | collective-permute-done | bytes 131104 | tf_op jit(solution)/shard_map/ppermute | solution.py:325
  88.8 2.6 %shard_map.85 = bf16[256,1024]{1,0:T(8,128)(2,1)} custom-call(f32[256,256]{1,0:T(8,128)S(1)} %get-tuple-element.32.refs_0_, bf16[256,256]{1,0:T(8,128)(2,1)S(1)} %collective-permute-done.12.refs_1_, f32[256,256]{1,0:T(8,128)S(1)} %collective-permute-done.13.refs_2_, bf16[256,256]{1,0:T(8,128)(2,1)S(1)} %collective-permute-done.14.refs_3_, ...), custom_call_target="tpu_custom_call" | custom-call | tf_op jit(solution)/shard_map/pallas_call | solution.py:332
  (47 shorter events, 7.1 us)
Async XLA Ops:
  1.6 26.2 %collective-permute-start.1 = (bf16[256,2048]{1,0:T(8,128)(2,1)S(1)}, bf16[256,2048]{1,0:T(8,128)(2,1)S(1)}, u32[]{:S(2)}, u32[]{:S(2)}) collective-permute-start(bf16[256,2048]{1,0:T(8,128)(2,1)S(1)} %get-tuple-element.27), channel_id=1, source_target_pairs={{0,8},{1,9},{2,10},{3,11},{4,12},{5,13},{6,14},{7,15},{8,0},{9,1},... | collective-permute-start | bytes 3145736 | tf_op jit(solution)/shard_map/ppermute | solution.py:325
  4.6 23.2 %collective-permute-start.3 = (bf16[256,512]{1,0:T(8,128)(2,1)S(1)}, bf16[256,512]{1,0:T(8,128)(2,1)S(1)}, u32[]{:S(2)}, u32[]{:S(2)}) collective-permute-start(bf16[256,512]{1,0:T(8,128)(2,1)S(1)} %get-tuple-element.29), channel_id=1, source_target_pairs={{0,4},{1,5},{2,6},{3,7},{4,0},{5,1},{6,2},{7,3},{8,12},{9,13},{10,... | collective-permute-start | bytes 786440 | tf_op jit(solution)/shard_map/ppermute | solution.py:325
  7.3 60.3 %collective-permute-start = (bf16[256,2048]{1,0:T(8,128)(2,1)S(1)}, bf16[256,2048]{1,0:T(8,128)(2,1)S(1)}, u32[]{:S(2)}, u32[]{:S(2)}) collective-permute-start(bf16[256,2048]{1,0:T(8,128)(2,1)S(1)} %get-tuple-element.26.refs_0_), channel_id=1, source_target_pairs={{0,4},{1,5},{2,6},{3,7},{4,0},{5,1},{6,2},{7,3},{8,12},{9,13},{10,... | collective-permute-start | bytes 3145736 | tf_op jit(solution)/shard_map/ppermute | solution.py:325
  7.9 20.7 %collective-permute-start.21 = (bf16[544,256]{1,0:T(8,128)(2,1)S(1)}, bf16[544,256]{1,0:T(8,128)(2,1)S(1)}, u32[]{:S(2)}, u32[]{:S(2)}) collective-permute-start(bf16[544,256]{1,0:T(8,128)(2,1)S(1)} %get-tuple-element.44), channel_id=1, source_target_pairs={{0,1},{4,5},{8,9},{12,13},{16,17},{20,21},{24,25},{28,29}} | collective-permute-start | bytes 835592 | tf_op jit(solution)/shard_map/ppermute | solution.py:325
  11.4 22.0 %collective-permute-start.15 = (bf16[544,256]{1,0:T(8,128)(2,1)S(1)}, bf16[544,256]{1,0:T(8,128)(2,1)S(1)}, u32[]{:S(2)}, u32[]{:S(2)}) collective-permute-start(bf16[544,256]{1,0:T(8,128)(2,1)S(1)} %get-tuple-element.36), channel_id=1, source_target_pairs={{0,1},{4,5},{8,9},{12,13},{16,17},{20,21},{24,25},{28,29}} | collective-permute-start | bytes 835592 | tf_op jit(solution)/shard_map/ppermute | solution.py:325
  27.8 43.4 %collective-permute-start.2 = (bf16[256,2048]{1,0:T(8,128)(2,1)S(1)}, bf16[256,2048]{1,0:T(8,128)(2,1)S(1)}, u32[]{:S(2)}, u32[]{:S(2)}) collective-permute-start(bf16[256,2048]{1,0:T(8,128)(2,1)S(1)} %collective-permute-done.1.refs_0_), channel_id=1, source_target_pairs={{0,4},{1,5},{2,6},{3,7},{4,0},{5,1},{6,2},{7,3},{8,12},{9,13},{10,... | collective-permute-start | bytes 3145736 | tf_op jit(solution)/shard_map/ppermute | solution.py:325
  27.8 6.3 %collective-permute-start.8 = (bf16[2,256,256]{2,1,0:T(8,128)(2,1)S(1)}, bf16[2,256,256]{2,1,0:T(8,128)(2,1)S(1)}, u32[]{:S(2)}, u32[]{:S(2)}) collective-permute-start(bf16[2,256,256]{2,1,0:T(8,128)(2,1)S(1)} %shard_map.75.refs_2_), channel_id=1, source_target_pairs={{1,2},{2,1},{5,6},{6,5},{9,10},{10,9},{13,14},{14,13},{17,18},{18,... | collective-permute-start | bytes 786440 | tf_op jit(solution)/shard_map/ppermute | solution.py:325
  28.5 13.4 %collective-permute-start.6 = (bf16[2,256,256]{2,1,0:T(8,128)(2,1)S(1)}, bf16[2,256,256]{2,1,0:T(8,128)(2,1)S(1)}, u32[]{:S(2)}, u32[]{:S(2)}) collective-permute-start(bf16[2,256,256]{2,1,0:T(8,128)(2,1)S(1)} %shard_map.75.refs_2_), channel_id=1, source_target_pairs={{0,1},{1,0},{2,3},{3,2},{4,5},{5,4},{6,7},{7,6},{8,9},{9,8},{10,11... | collective-permute-start | bytes 786440 | tf_op jit(solution)/shard_map/ppermute | solution.py:325
  33.4 20.3 %collective-permute-start.22 = (bf16[544,256]{1,0:T(8,128)(2,1)S(1)}, bf16[544,256]{1,0:T(8,128)(2,1)S(1)}, u32[]{:S(2)}, u32[]{:S(2)}) collective-permute-start(bf16[544,256]{1,0:T(8,128)(2,1)S(1)} %shard_map.82), channel_id=1, source_target_pairs={{1,2},{5,6},{9,10},{13,14},{17,18},{21,22},{25,26},{29,30}} | collective-permute-start | bytes 835592 | tf_op jit(solution)/shard_map/ppermute | solution.py:325
  34.1 18.9 %collective-permute-start.4 = (bf16[2,256,256]{2,1,0:T(8,128)(2,1)S(1)}, bf16[2,256,256]{2,1,0:T(8,128)(2,1)S(1)}, u32[]{:S(2)}, u32[]{:S(2)}) collective-permute-start(bf16[2,256,256]{2,1,0:T(8,128)(2,1)S(1)} %shard_map.75.refs_2_), channel_id=1, source_target_pairs={{0,2},{1,3},{2,0},{3,1},{4,6},{5,7},{6,4},{7,5},{8,10},{9,11},{10,... | collective-permute-start | bytes 786440 | tf_op jit(solution)/shard_map/ppermute | solution.py:325
  41.9 13.3 %collective-permute-start.16 = (bf16[544,256]{1,0:T(8,128)(2,1)S(1)}, bf16[544,256]{1,0:T(8,128)(2,1)S(1)}, u32[]{:S(2)}, u32[]{:S(2)}) collective-permute-start(bf16[544,256]{1,0:T(8,128)(2,1)S(1)} %shard_map.78), channel_id=1, source_target_pairs={{1,2},{5,6},{9,10},{13,14},{17,18},{21,22},{25,26},{29,30}} | collective-permute-start | bytes 835592 | tf_op jit(solution)/shard_map/ppermute | solution.py:325
  53.0 2.9 %collective-permute-start.9 = (bf16[2,256,256]{2,1,0:T(8,128)(2,1)S(1)}, bf16[2,256,256]{2,1,0:T(8,128)(2,1)S(1)}, u32[]{:S(2)}, u32[]{:S(2)}) collective-permute-start(bf16[2,256,256]{2,1,0:T(8,128)(2,1)S(1)} %collective-permute-done.8.refs_5_), channel_id=1, source_target_pairs={{1,17},{2,18},{5,21},{6,22},{9,25},{10,26},{13,29},{14,30},{17,1},... | collective-permute-start | bytes 786440 | tf_op jit(solution)/shard_map/ppermute | solution.py:325
  53.7 13.4 %collective-permute-start.10 = (bf16[2,256,256]{2,1,0:T(8,128)(2,1)S(1)}, bf16[2,256,256]{2,1,0:T(8,128)(2,1)S(1)}, u32[]{:S(2)}, u32[]{:S(2)}) collective-permute-start(bf16[2,256,256]{2,1,0:T(8,128)(2,1)S(1)} %collective-permute-done.4.refs_3_), channel_id=1, source_target_pairs={{1,0},{2,3},{5,4},{6,7},{9,8},{10,11},{13,12},{14,15},{17,16},{18,... | collective-permute-start | bytes 786440 | tf_op jit(solution)/shard_map/ppermute | solution.py:325
  55.2 25.6 %collective-permute-start.23 = (bf16[544,256]{1,0:T(8,128)(2,1)S(1)}, bf16[544,256]{1,0:T(8,128)(2,1)S(1)}, u32[]{:S(2)}, u32[]{:S(2)}) collective-permute-start(bf16[544,256]{1,0:T(8,128)(2,1)S(1)} %shard_map.83), channel_id=1, source_target_pairs={{2,3},{6,7},{10,11},{14,15},{18,19},{22,23},{26,27},{30,31}} | collective-permute-start | bytes 835592 | tf_op jit(solution)/shard_map/ppermute | solution.py:325
  55.9 17.6 %collective-permute-start.7 = (bf16[2,256,256]{2,1,0:T(8,128)(2,1)S(1)}, bf16[2,256,256]{2,1,0:T(8,128)(2,1)S(1)}, u32[]{:S(2)}, u32[]{:S(2)}) collective-permute-start(bf16[2,256,256]{2,1,0:T(8,128)(2,1)S(1)} %collective-permute-done.6.refs_4_), channel_id=1, source_target_pairs={{0,16},{1,17},{2,18},{3,19},{4,20},{5,21},{6,22},{7,23},{8,24},{9,... | collective-permute-start | bytes 786440 | tf_op jit(solution)/shard_map/ppermute | solution.py:325
  67.1 9.2 %collective-permute-start.5 = (bf16[2,256,256]{2,1,0:T(8,128)(2,1)S(1)}, bf16[2,256,256]{2,1,0:T(8,128)(2,1)S(1)}, u32[]{:S(2)}, u32[]{:S(2)}) collective-permute-start(bf16[2,256,256]{2,1,0:T(8,128)(2,1)S(1)} %collective-permute-done.4.refs_3_), channel_id=1, source_target_pairs={{0,16},{1,17},{2,18},{3,19},{4,20},{5,21},{6,22},{7,23},{8,24},{9,... | collective-permute-start | bytes 786440 | tf_op jit(solution)/shard_map/ppermute | solution.py:325
  67.6 11.7 %collective-permute-start.11 = (bf16[2,256,256]{2,1,0:T(8,128)(2,1)S(1)}, bf16[2,256,256]{2,1,0:T(8,128)(2,1)S(1)}, u32[]{:S(2)}, u32[]{:S(2)}) collective-permute-start(bf16[2,256,256]{2,1,0:T(8,128)(2,1)S(1)} %collective-permute-done.10.refs_6_), channel_id=1, source_target_pairs={{0,16},{3,19},{4,20},{7,23},{8,24},{11,27},{12,28},{15,31},{16,0},... | collective-permute-start | bytes 786440 | tf_op jit(solution)/shard_map/ppermute | solution.py:325
  71.2 13.5 %collective-permute-start.17 = (bf16[544,256]{1,0:T(8,128)(2,1)S(1)}, bf16[544,256]{1,0:T(8,128)(2,1)S(1)}, u32[]{:S(2)}, u32[]{:S(2)}) collective-permute-start(bf16[544,256]{1,0:T(8,128)(2,1)S(1)} %shard_map.79), channel_id=1, source_target_pairs={{2,3},{6,7},{10,11},{14,15},{18,19},{22,23},{26,27},{30,31}} | collective-permute-start | bytes 835592 | tf_op jit(solution)/shard_map/ppermute | solution.py:325
  73.5 7.9 %collective-permute-start.18 = (bf16[256,256]{1,0:T(8,128)(2,1)S(1)}, bf16[256,256]{1,0:T(8,128)(2,1)S(1)}, u32[]{:S(2)}, u32[]{:S(2)}) collective-permute-start(bf16[256,256]{1,0:T(8,128)(2,1)S(1)} %get-tuple-element.41), channel_id=1, source_target_pairs={{0,8},{1,9},{2,10},{3,11},{4,12},{5,13},{6,14},{7,15},{8,0},{9,1},... | collective-permute-start | bytes 393224 | tf_op jit(solution)/shard_map/ppermute | solution.py:325
  76.3 6.6 %collective-permute-start.20 = (bf16[256,256]{1,0:T(8,128)(2,1)S(1)}, bf16[256,256]{1,0:T(8,128)(2,1)S(1)}, u32[]{:S(2)}, u32[]{:S(2)}) collective-permute-start(bf16[256,256]{1,0:T(8,128)(2,1)S(1)} %get-tuple-element.43), channel_id=1, source_target_pairs={{0,12},{1,13},{2,14},{3,15},{4,8},{5,9},{6,10},{7,11},{8,4},{9,5},... | collective-permute-start | bytes 393224 | tf_op jit(solution)/shard_map/ppermute | solution.py:325
  79.3 3.6 %collective-permute-start.19 = (f32[256,256]{1,0:T(8,128)S(1)}, f32[256,256]{1,0:T(8,128)S(1)}, u32[]{:S(2)}, u32[]{:S(2)}) collective-permute-start(f32[256,256]{1,0:T(8,128)S(1)} %get-tuple-element.42), channel_id=1, source_target_pairs={{0,4},{1,5},{2,6},{3,7},{4,0},{5,1},{6,2},{7,3},{8,12},{9,13},{10,... | collective-permute-start | bytes 786440 | tf_op jit(solution)/shard_map/ppermute | solution.py:325
  80.8 8.0 %collective-permute-start.13 = (f32[256,256]{1,0:T(8,128)S(1)}, f32[256,256]{1,0:T(8,128)S(1)}, u32[]{:S(2)}, u32[]{:S(2)}) collective-permute-start(f32[256,256]{1,0:T(8,128)S(1)} %get-tuple-element.34), channel_id=1, source_target_pairs={{0,4},{1,5},{2,6},{3,7},{4,0},{5,1},{6,2},{7,3},{8,12},{9,13},{10,... | collective-permute-start | bytes 786440 | tf_op jit(solution)/shard_map/ppermute | solution.py:325
  81.4 6.4 %collective-permute-start.12 = (bf16[256,256]{1,0:T(8,128)(2,1)S(1)}, bf16[256,256]{1,0:T(8,128)(2,1)S(1)}, u32[]{:S(2)}, u32[]{:S(2)}) collective-permute-start(bf16[256,256]{1,0:T(8,128)(2,1)S(1)} %get-tuple-element.33), channel_id=1, source_target_pairs={{0,8},{1,9},{2,10},{3,11},{4,12},{5,13},{6,14},{7,15},{8,0},{9,1},... | collective-permute-start | bytes 393224 | tf_op jit(solution)/shard_map/ppermute | solution.py:325
  82.9 5.9 %collective-permute-start.14 = (bf16[256,256]{1,0:T(8,128)(2,1)S(1)}, bf16[256,256]{1,0:T(8,128)(2,1)S(1)}, u32[]{:S(2)}, u32[]{:S(2)}) collective-permute-start(bf16[256,256]{1,0:T(8,128)(2,1)S(1)} %get-tuple-element.35), channel_id=1, source_target_pairs={{0,12},{1,13},{2,14},{3,15},{4,8},{5,9},{6,10},{7,11},{8,4},{9,5},... | collective-permute-start | bytes 393224 | tf_op jit(solution)/shard_map/ppermute | solution.py:325
  (5 other events, 23.3 us)

commit v3 on v2

--- a/solution.py
+++ b/solution.py
@@ -156,10 +156,10 @@
     copy.wait()
 
 
-def combine_kernel(heads, prev_ref, own_ref, side_ref, msg_ref):
-    size = own_ref.shape[0] // heads
+def join(slots, prev_ref, own_ref, side_ref, out_ref):
+    size = own_ref.shape[0] // slots
     stride = size + EXTRA
-    for h in range(heads):
+    for h in range(slots):
         memory, normer, top = load_message(prev_ref, h * stride, size)
         own_normer = side_ref[h * 8 : h * 8 + 1, :]
         own_top = side_ref[h * 8 + 1 : h * 8 + 2, 0:1]
@@ -169,13 +169,56 @@
         early = jnp.exp(shifted - both)
         late = jnp.exp(own_top - both)
         joined = early * memory.astype(f32) + late * own_ref[h * size : (h + 1) * size, :]
-        store_message(msg_ref, h * stride, size, joined, early * normer + late * own_normer, both)
+        normers = early * normer + late * own_normer
+        store_message(out_ref, h * stride, size, joined, normers, both)
+
+
+def combine_kernel(slots, sender, prev_ref, own_ref, side_ref, out_ref):
+    place = lax.axis_index("ctx")
+
+    @pl.when(place == sender)
+    def _():
+        join(slots, prev_ref, own_ref, side_ref, out_ref)
+
+    @pl.when(place != sender)
+    def _():
+        out_ref[...] = prev_ref[...]
+
+
+def mix_kernel(message_ref, piece_ref, out_ref):
+    place = lax.axis_index("ctx")
+    rows = piece_ref.shape[1]
+
+    @pl.when(place == 0)
+    def _():
+        out_ref[...] = message_ref[...]
+
+    @pl.when(place != 0)
+    def _():
+        for j in range(CORES):
+            out_ref[j * rows : (j + 1) * rows, :] = piece_ref[j]
+        rest = out_ref.shape[0] - CORES * rows
+        out_ref[CORES * rows :, :] = jnp.zeros((rest, out_ref.shape[1]), out_ref.dtype)
+
+
+def pick_kernel(inner_ref, outer_ref, out_ref):
+    place = lax.axis_index("ctx")
+    rows = out_ref.shape[1]
+    inner = jnp.logical_or(place == 1, place == 2)
+
+    @pl.when(inner)
+    def _():
+        out_ref[...] = inner_ref[...]
+
+    @pl.when(jnp.logical_not(inner))
+    def _():
+        for j in range(CORES):
+            out_ref[j] = outer_ref[j * rows : (j + 1) * rows, :]
 
 
 def away_kernel(nz, ng, phase, count, *refs):
-    split = nz == 4
     first = 2 if phase else 1
-    tokens, parts = refs[:count], refs[count : count + first + nz - 1 + split]
+    tokens, parts = refs[:count], refs[count : count + first + nz - 1]
     outs, whole = refs[count + len(parts) : -1], refs[-1]
     rows, width = parts[-1].shape[1:]
     place, group = lax.axis_index("ctx"), lax.axis_index("groups")
@@ -185,19 +228,13 @@
         values = [(parts[0][...], parts[1][:, pl.ds(column, width)])]
     else:
         values = [(parts[0][0], parts[0][1])]
-    steps = list(range(nz))
     for part in parts[first:]:
         values.append((part[0], part[1]))
-    if split:
-        inner = jnp.logical_or(place == 1, place == 2)
-        outer = values.pop()
-        values[-1] = tuple(jnp.where(inner, a, b) for a, b in zip(values[-1], outer))
-        steps = [0, 2, 1, 3]
-    for at, s in enumerate(steps):
+    for s in range(nz):
         for j in range(CORES):
             owner = lax.rem(core + j, CORES)
             row = pl.multiple_of((owner * nz + (place ^ s)) * rows, rows)
-            whole[pl.ds(row, rows), :] = values[at][j]
+            whole[pl.ds(row, rows), :] = values[s][j]
     for token, out in zip(tokens, outs):
         value = jnp.dot(token[...], whole[...], preferred_element_type=f32)
         out[...] = value.astype(out.dtype)
@@ -306,15 +343,12 @@
 ANY = pl.BlockSpec(memory_space=pl.ANY)
 
 
-def gather_plan(nz):
-    if nz != 4:
-        return [(s, None, lambda z, s=s: z ^ s) for s in range(1, nz)]
-    return [
-        ("2", None, lambda z: z ^ 2),
-        ("1", None, lambda z: z ^ 1),
-        ("in", None, lambda z: z ^ 3 if z in (1, 2) else None),
-        ("out", "2", lambda z: {1: 0, 2: 3}.get(z)),
-    ]
+def links(z):
+    return {z: z + 1, z + 1: z}
+
+
+def compact(mesh):
+    return mesh.shape["ctx"] == 4 and mesh.shape["groups"] == CORES == 2
 
 
 def make_body(mesh):
@@ -399,35 +433,60 @@
         for rel, value in enumerate(arrived):
             tokens.extend([value, over_core(value)])
         pieces = [[packed]] + [[own_parts[r], swapped] for r in range(1, ng)]
-        gathered = {}
-        for name, origin, where in gather_plan(nz):
-            value = packed if origin is None else gathered[origin]
-            mine = send(value, lambda g, x, k, z: None if where(z) is None else (g, x, k, where(z)))
-            gathered[name] = mine
-            pieces[0].append(mine)
+
+        def over_ctx(value, targets):
+            return send(
+                value,
+                lambda g, x, k, z: (g, x, k, targets[z]) if z in targets else (g, x, 1 - k, z),
+            )
+
+        own = [prepared[1 + 3 * r] for r in range(ng)]
+        first = [prepared[2 + 3 * r] for r in range(ng)]
+        side = [prepared[3 + 3 * r] for r in range(ng)]
+        states = [[over_ctx(first[0], links(0))]] + [[] for _ in range(1, ng)]
+
+        def extend(hop, r):
+            message_out = call(
+                functools.partial(combine_kernel, slots, hop - 1),
+                states[r][-1], own[r], side[r],
+                out_shape=message,
+                in_specs=[VMEM] * 3,
+                out_specs=VMEM,
+            )
+            states[r].append(over_ctx(message_out, links(hop - 1)))
+
+        gathered = {
+            s: over_ctx(packed, {z: z ^ s for z in range(nz)})
+            for s in (range(1, nz) if not compact(mesh) else (2, 1))
+        }
+        if compact(mesh):
+            inside = over_ctx(packed, links(1))
+            mixed = call(
+                mix_kernel,
+                first[1], gathered[2],
+                out_shape=message,
+                in_specs=[VMEM] * 2,
+                out_specs=VMEM,
+            )
+            outside = over_ctx(mixed, {**links(0), **links(2)})
+            states[1].append(outside)
+            gathered[3] = call(
+                pick_kernel,
+                inside, outside,
+                out_shape=jax.ShapeDtypeStruct(packed.shape, bf16),
+                in_specs=[VMEM] * 2,
+                out_specs=VMEM,
+            )
+        else:
             for r in range(1, ng):
-                pieces[r].append(
-                    send(
-                        mine,
-                        lambda g, x, k, z: (
-                            ((g - r) % ng, x, k, z) if z in map(where, range(nz)) else None
-                        ),
-                    )
-                )
-        states = [[] for _ in range(ng)]
-        for r in range(ng):
-            own, current, side = prepared[1 + 3 * r : 4 + 3 * r]
-            for hop in range(1, nz):
-                state = send(current, lambda g, x, k, z: (g, x, k, z + 1) if z == hop - 1 else None)
-                states[r].append(state)
-                if hop < nz - 1:
-                    current = call(
-                        functools.partial(combine_kernel, slots),
-                        state, own, side,
-                        out_shape=message,
-                        in_specs=[VMEM] * 3,
-                        out_specs=VMEM,
-                    )
+                states[r].append(over_ctx(first[r], links(0)))
+        for hop in range(2, nz):
+            for r in range(ng):
+                extend(hop, r)
+        for s in range(1, nz):
+            pieces[0].append(gathered[s])
+            for r in range(1, ng):
+                pieces[r].append(send(gathered[s], lambda g, x, k, z: ((g - r) % ng, x, k, z)))
         results = []
         for r in range(ng):
             piece = jax.ShapeDtypeStruct((length, width), f32)

time: 92.4 us -> 83 us (0.90)
  the two profiles are of different devices: /device:TPU:0 before, /device:TPU:11 now
where the time goes in v3:
time: 83 us; the launch traced here: 82.8 us
  waiting for transfers between devices  50.5 us (61%)
  starting transfers between devices  20 us (24%)
  Pallas kernels  12.1 us (15%)
    ppermute x22, waiting for transfers between devices, send(): return lax.ppermute(value, AXES, moves(mesh, where))  50.5 us
    ppermute x22, starting transfers between devices, send(): return lax.ppermute(value, AXES, moves(mesh, where))  20 us
    pallas_call x15, Pallas kernels, call(): return pl.pallas_call(kernel, compiler_params=params, **options)(*args)  12.1 us
  transfers between devices with their start and end apart: 22, of which 8 were waited for; matrix products, arithmetic and copies ran while one was open for 0% of the time, Pallas kernels for 10%

profile of v3, /device:TPU:11, one launch (start us, length us, event | category | flops | bytes accessed | tf_op | source)
XLA Modules:
  0.0 82.8 jit_solution(10233850647850191007)
XLA Ops:
  0.0 1.6 %shard_map.74 = (bf16[256,512]{1,0:T(8,128)(2,1)S(1)}, bf16[256,256]{1,0:T(8,128)(2,1)S(1)}, bf16[256,256]{1,0:T(8,128)(2,1)S(1)}, bf16[256,2048]{1,0:T(8,128)(2,1)S(1)}) custom-call(bf16[256,4096]{1,0:T(8,128)(2,1)} %bitcast.18, bf16[256,1024]{1,0:T(8,128)(2,1)} %w_ref.1), custom_call_target="tpu_custom_call" | custom-call | tf_op jit(solution)/shard_map/pallas_call | solution.py:366
  1.9 1.0 %collective-permute-start.3 = (bf16[256,512]{1,0:T(8,128)(2,1)S(1)}, bf16[256,512]{1,0:T(8,128)(2,1)S(1)}, u32[]{:S(2)}, u32[]{:S(2)}) collective-permute-start(bf16[256,512]{1,0:T(8,128)(2,1)S(1)} %get-tuple-element.29), channel_id=1, source_target_pairs={{0,4},{1,5},{2,6},{3,7},{4,0},{5,1},{6,2},{7,3},{8,12},{9,13},{10,... | collective-permute-start | bytes 786440 | tf_op jit(solution)/shard_map/ppermute | solution.py:359
  2.9 2.6 %shard_map.73 = (bf16[256,2048]{1,0:T(8,128)(2,1)S(1)}, f32[512,256]{1,0:T(8,128)S(1)}, bf16[544,256]{1,0:T(8,128)(2,1)S(1)}, f32[16,256]{1,0:T(8,128)S(1)}, f32...) custom-call(bf16[256,1024]{1,0:T(8,128)(2,1)S(1)} %bitcast.6, ...), custom_call_target="tpu_custom_call" | custom-call | tf_op jit(solution)/shard_map/pallas_call | solution.py:366
  5.7 2.8 %collective-permute-start.6 = (bf16[2,256,256]{2,1,0:T(8,128)(2,1)S(1)}, bf16[2,256,256]{2,1,0:T(8,128)(2,1)S(1)}, u32[]{:S(2)}, u32[]{:S(2)}) collective-permute-start(bf16[2,256,256]{2,1,0:T(8,128)(2,1)S(1)} %shard_map.75.refs_2_), channel_id=1, source_target_pairs={{0,2},{1,3},{2,0},{3,1},{4,6},{5,7},{6,4},{7,5},{8,10},{9,11},{10,... | collective-permute-start | bytes 786440 | tf_op jit(solution)/shard_map/ppermute | solution.py:359
  8.5 17.2 %collective-permute-done.1.refs_0_ = bf16[256,2048]{1,0:T(8,128)(2,1)S(1)} collective-permute-done((bf16[256,2048]{1,0:T(8,128)(2,1)S(1)}, bf16[256,2048]{1,0:T(8,128)(2,1)S(1)}, u32[]{:S(2)}, u32[]{:S(2)}) %collective-permute-start.1) | collective-permute-done | bytes 1048608 | tf_op jit(solution)/shard_map/ppermute | solution.py:359
  25.7 1.5 %collective-permute-start.2 = (bf16[256,2048]{1,0:T(8,128)(2,1)S(1)}, bf16[256,2048]{1,0:T(8,128)(2,1)S(1)}, u32[]{:S(2)}, u32[]{:S(2)}) collective-permute-start(bf16[256,2048]{1,0:T(8,128)(2,1)S(1)} %collective-permute-done.1.refs_0_), channel_id=1, source_target_pairs={{0,4},{1,5},{2,6},{3,7},{4,0},{5,1},{6,2},{7,3},{8,12},{9,13},{10,... | collective-permute-start | bytes 3145736 | tf_op jit(solution)/shard_map/ppermute | solution.py:359
  27.7 2.3 %collective-permute-start.20 = (bf16[544,256]{1,0:T(8,128)(2,1)S(1)}, bf16[544,256]{1,0:T(8,128)(2,1)S(1)}, u32[]{:S(2)}, u32[]{:S(2)}) collective-permute-start(bf16[544,256]{1,0:T(8,128)(2,1)S(1)} %shard_map.84), channel_id=1, source_target_pairs={{0,4},{1,2},{2,1},{3,7},{4,0},{5,6},{6,5},{7,3},{8,12},{9,10},{10,... | collective-permute-start | bytes 835592 | tf_op jit(solution)/shard_map/ppermute | solution.py:359
  30.0 5.5 %collective-permute-done.9.outer_ref.prev_ref.refs_9_ = bf16[544,256]{1,0:T(8,128)(2,1)S(1)} collective-permute-done((bf16[544,256]{1,0:T(8,128)(2,1)S(1)}, bf16[544,256]{1,0:T(8,128)(2,1)S(1)}, u32[]{:S(2)}, u32[]{:S(2)}) %collective-permute-start.9) | collective-permute-done | bytes 278560 | tf_op jit(solution)/shard_map/ppermute | solution.py:359
  35.7 1.2 %collective-permute-start.14 = (bf16[544,256]{1,0:T(8,128)(2,1)S(1)}, bf16[544,256]{1,0:T(8,128)(2,1)S(1)}, u32[]{:S(2)}, u32[]{:S(2)}) collective-permute-start(bf16[544,256]{1,0:T(8,128)(2,1)S(1)} %shard_map.80), channel_id=1, source_target_pairs={{0,4},{1,2},{2,1},{3,7},{4,0},{5,6},{6,5},{7,3},{8,12},{9,10},{10,... | collective-permute-start | bytes 835592 | tf_op jit(solution)/shard_map/ppermute | solution.py:359
  37.3 11.5 %collective-permute-done.8.inner_ref = bf16[2,256,256]{2,1,0:T(8,128)(2,1)S(1)} collective-permute-done((bf16[2,256,256]{2,1,0:T(8,128)(2,1)S(1)}, bf16[2,256,256]{2,1,0:T(8,128)(2,1)S(1)}, u32[]{:S(2)}, u32[]{:S(2)}) %collective-permute-start.8) | collective-permute-done | bytes 262176 | tf_op jit(solution)/shard_map/ppermute | solution.py:359
  48.8 1.7 %collective-permute-start.21 = (bf16[544,256]{1,0:T(8,128)(2,1)S(1)}, bf16[544,256]{1,0:T(8,128)(2,1)S(1)}, u32[]{:S(2)}, u32[]{:S(2)}) collective-permute-start(bf16[544,256]{1,0:T(8,128)(2,1)S(1)} %shard_map.85), channel_id=1, source_target_pairs={{0,4},{1,5},{2,3},{3,2},{4,0},{5,1},{6,7},{7,6},{8,12},{9,13},{10,... | collective-permute-start | bytes 835592 | tf_op jit(solution)/shard_map/ppermute | solution.py:359
  50.5 1.2 %collective-permute-start.7 = (bf16[2,256,256]{2,1,0:T(8,128)(2,1)S(1)}, bf16[2,256,256]{2,1,0:T(8,128)(2,1)S(1)}, u32[]{:S(2)}, u32[]{:S(2)}) collective-permute-start(bf16[2,256,256]{2,1,0:T(8,128)(2,1)S(1)} %collective-permute-done.6.piece_ref.refs_4_), channel_id=1, source_target_pairs={{0,16},{1,17},{2,18},{3,19},{4,20},{5,21},{6,22},{7,23},{8,24},{9,... | collective-permute-start | bytes 786440 | tf_op jit(solution)/shard_map/ppermute | solution.py:359
  52.0 1.3 %collective-permute-start.10 = (bf16[2,256,256]{2,1,0:T(8,128)(2,1)S(1)}, bf16[2,256,256]{2,1,0:T(8,128)(2,1)S(1)}, u32[]{:S(2)}, u32[]{:S(2)}) collective-permute-start(bf16[2,256,256]{2,1,0:T(8,128)(2,1)S(1)} %shard_map.77.refs_5_), channel_id=1, source_target_pairs={{0,16},{1,17},{2,18},{3,19},{4,20},{5,21},{6,22},{7,23},{8,24},{9,... | collective-permute-start | bytes 786440 | tf_op jit(solution)/shard_map/ppermute | solution.py:359
  53.3 0.9 %collective-permute-start.15 = (bf16[544,256]{1,0:T(8,128)(2,1)S(1)}, bf16[544,256]{1,0:T(8,128)(2,1)S(1)}, u32[]{:S(2)}, u32[]{:S(2)}) collective-permute-start(bf16[544,256]{1,0:T(8,128)(2,1)S(1)} %shard_map.81), channel_id=1, source_target_pairs={{0,4},{1,5},{2,3},{3,2},{4,0},{5,1},{6,7},{7,6},{8,12},{9,13},{10,... | collective-permute-start | bytes 835592 | tf_op jit(solution)/shard_map/ppermute | solution.py:359
  55.8 2.6 %collective-permute-done.7.refs_5_ = bf16[2,256,256]{2,1,0:T(8,128)(2,1)S(1)} collective-permute-done((bf16[2,256,256]{2,1,0:T(8,128)(2,1)S(1)}, bf16[2,256,256]{2,1,0:T(8,128)(2,1)S(1)}, u32[]{:S(2)}, u32[]{:S(2)}) %collective-permute-start.7) | collective-permute-done | bytes 262176 | tf_op jit(solution)/shard_map/ppermute | solution.py:359
  58.6 5.4 %collective-permute-done.5.refs_4_ = bf16[2,256,256]{2,1,0:T(8,128)(2,1)S(1)} collective-permute-done((bf16[2,256,256]{2,1,0:T(8,128)(2,1)S(1)}, bf16[2,256,256]{2,1,0:T(8,128)(2,1)S(1)}, u32[]{:S(2)}, u32[]{:S(2)}) %collective-permute-start.5) | collective-permute-done | bytes 262176 | tf_op jit(solution)/shard_map/ppermute | solution.py:359
  64.0 1.5 %collective-permute-start.18 = (bf16[256,256]{1,0:T(8,128)(2,1)S(1)}, bf16[256,256]{1,0:T(8,128)(2,1)S(1)}, u32[]{:S(2)}, u32[]{:S(2)}) collective-permute-start(bf16[256,256]{1,0:T(8,128)(2,1)S(1)} %get-tuple-element.43), channel_id=1, source_target_pairs={{0,12},{1,13},{2,14},{3,15},{4,8},{5,9},{6,10},{7,11},{8,4},{9,5},... | collective-permute-start | bytes 393224 | tf_op jit(solution)/shard_map/ppermute | solution.py:359
  65.4 4.2 %collective-permute-done.10.refs_6_ = bf16[2,256,256]{2,1,0:T(8,128)(2,1)S(1)} collective-permute-done((bf16[2,256,256]{2,1,0:T(8,128)(2,1)S(1)}, bf16[2,256,256]{2,1,0:T(8,128)(2,1)S(1)}, u32[]{:S(2)}, u32[]{:S(2)}) %collective-permute-start.10) | collective-permute-done | bytes 262176 | tf_op jit(solution)/shard_map/ppermute | solution.py:359
  69.6 0.9 %collective-permute-start.17 = (f32[256,256]{1,0:T(8,128)S(1)}, f32[256,256]{1,0:T(8,128)S(1)}, u32[]{:S(2)}, u32[]{:S(2)}) collective-permute-start(f32[256,256]{1,0:T(8,128)S(1)} %get-tuple-element.42), channel_id=1, source_target_pairs={{0,4},{1,5},{2,6},{3,7},{4,0},{5,1},{6,2},{7,3},{8,12},{9,13},{10,... | collective-permute-start | bytes 786440 | tf_op jit(solution)/shard_map/ppermute | solution.py:359
  70.5 0.8 shard_map.78
  72.4 1.8 %collective-permute-start.13 = (bf16[256,256]{1,0:T(8,128)(2,1)S(1)}, bf16[256,256]{1,0:T(8,128)(2,1)S(1)}, u32[]{:S(2)}, u32[]{:S(2)}) collective-permute-start(bf16[256,256]{1,0:T(8,128)(2,1)S(1)} %get-tuple-element.36), channel_id=1, source_target_pairs={{0,12},{1,13},{2,14},{3,15},{4,8},{5,9},{6,10},{7,11},{8,4},{9,5},... | collective-permute-start | bytes 393224 | tf_op jit(solution)/shard_map/ppermute | solution.py:359
  74.2 1.8 %shard_map.86.refs_12_ = bf16[256,512]{1,0:T(8,128)(2,1)S(1)} custom-call(f32[256,256]{1,0:T(8,128)S(1)} %get-tuple-element.40.refs_0_, bf16[256,256]{1,0:T(8,128)(2,1)S(1)} %collective-permute-done.16.refs_1_, f32[256,256]{1,0:T(8,128)S(1)} %collective-permute-done.17.refs_2_, bf16[256,256]{1,0:T(8,128)(2,1)S(1)} %collective-permute-done.18.refs_3_, ...), custom_call_target="tpu_custom_call" | custom-call | tf_op jit(solution)/shard_map/pallas_call | solution.py:366
  76.8 3.4 %collective-permute-done.13.refs_3_ = bf16[256,256]{1,0:T(8,128)(2,1)S(1)} collective-permute-done((bf16[256,256]{1,0:T(8,128)(2,1)S(1)}, bf16[256,256]{1,0:T(8,128)(2,1)S(1)}, u32[]{:S(2)}, u32[]{:S(2)}) %collective-permute-start.13) | collective-permute-done | bytes 131104 | tf_op jit(solution)/shard_map/ppermute | solution.py:359
  80.2 2.6 %shard_map.87 = bf16[256,1024]{1,0:T(8,128)(2,1)} custom-call(f32[256,256]{1,0:T(8,128)S(1)} %get-tuple-element.33.refs_0_, bf16[256,256]{1,0:T(8,128)(2,1)S(1)} %collective-permute-done.11.refs_1_, f32[256,256]{1,0:T(8,128)S(1)} %collective-permute-done.12.refs_2_, bf16[256,256]{1,0:T(8,128)(2,1)S(1)} %collective-permute-done.13.refs_3_, ...), custom_call_target="tpu_custom_call" | custom-call | tf_op jit(solution)/shard_map/pallas_call | solution.py:366
  (45 shorter events, 5.3 us)
Async XLA Ops:
  0.0 2.9 %copy-start.3 = (f32[1,4,256]{2,1,0:T(4,128)S(1)}, f32[1,4,256]{2,1,0:T(4,128)}, u32[]{:S(2)}) copy-start(f32[1,4,256]{2,1,0:T(4,128)} %param.12) | copy-start | bytes 12292
  0.0 2.9 %copy-start.2 = (f32[1,4,256]{2,1,0:T(4,128)S(1)}, f32[1,4,256]{2,1,0:T(4,128)}, u32[]{:S(2)}) copy-start(f32[1,4,256]{2,1,0:T(4,128)} %param.11) | copy-start | bytes 12292
  1.6 24.1 %collective-permute-start.1 = (bf16[256,2048]{1,0:T(8,128)(2,1)S(1)}, bf16[256,2048]{1,0:T(8,128)(2,1)S(1)}, u32[]{:S(2)}, u32[]{:S(2)}) collective-permute-start(bf16[256,2048]{1,0:T(8,128)(2,1)S(1)} %get-tuple-element.27), channel_id=1, source_target_pairs={{0,8},{1,9},{2,10},{3,11},{4,12},{5,13},{6,14},{7,15},{8,0},{9,1},... | collective-permute-start | bytes 3145736 | tf_op jit(solution)/shard_map/ppermute | solution.py:359
  1.9 3.8 %collective-permute-start.3 = (bf16[256,512]{1,0:T(8,128)(2,1)S(1)}, bf16[256,512]{1,0:T(8,128)(2,1)S(1)}, u32[]{:S(2)}, u32[]{:S(2)}) collective-permute-start(bf16[256,512]{1,0:T(8,128)(2,1)S(1)} %get-tuple-element.29), channel_id=1, source_target_pairs={{0,4},{1,5},{2,6},{3,7},{4,0},{5,1},{6,2},{7,3},{8,12},{9,13},{10,... | collective-permute-start | bytes 786440 | tf_op jit(solution)/shard_map/ppermute | solution.py:359
  5.5 46.2 %collective-permute-start = (bf16[256,2048]{1,0:T(8,128)(2,1)S(1)}, bf16[256,2048]{1,0:T(8,128)(2,1)S(1)}, u32[]{:S(2)}, u32[]{:S(2)}) collective-permute-start(bf16[256,2048]{1,0:T(8,128)(2,1)S(1)} %get-tuple-element.26.refs_0_), channel_id=1, source_target_pairs={{0,4},{1,5},{2,6},{3,7},{4,0},{5,1},{6,2},{7,3},{8,12},{9,13},{10,... | collective-permute-start | bytes 3145736 | tf_op jit(solution)/shard_map/ppermute | solution.py:359
  5.6 21.9 %collective-permute-start.19 = (bf16[544,256]{1,0:T(8,128)(2,1)S(1)}, bf16[544,256]{1,0:T(8,128)(2,1)S(1)}, u32[]{:S(2)}, u32[]{:S(2)}) collective-permute-start(bf16[544,256]{1,0:T(8,128)(2,1)S(1)} %get-tuple-element.44), channel_id=1, source_target_pairs={{0,1},{1,0},{2,6},{3,7},{4,5},{5,4},{6,2},{7,3},{8,9},{9,8},{10,14... | collective-permute-start | bytes 835592 | tf_op jit(solution)/shard_map/ppermute | solution.py:359
  5.7 21.5 %collective-permute-start.6 = (bf16[2,256,256]{2,1,0:T(8,128)(2,1)S(1)}, bf16[2,256,256]{2,1,0:T(8,128)(2,1)S(1)}, u32[]{:S(2)}, u32[]{:S(2)}) collective-permute-start(bf16[2,256,256]{2,1,0:T(8,128)(2,1)S(1)} %shard_map.75.refs_2_), channel_id=1, source_target_pairs={{0,2},{1,3},{2,0},{3,1},{4,6},{5,7},{6,4},{7,5},{8,10},{9,11},{10,... | collective-permute-start | bytes 786440 | tf_op jit(solution)/shard_map/ppermute | solution.py:359
  25.7 27.6 %collective-permute-start.2 = (bf16[256,2048]{1,0:T(8,128)(2,1)S(1)}, bf16[256,2048]{1,0:T(8,128)(2,1)S(1)}, u32[]{:S(2)}, u32[]{:S(2)}) collective-permute-start(bf16[256,2048]{1,0:T(8,128)(2,1)S(1)} %collective-permute-done.1.refs_0_), channel_id=1, source_target_pairs={{0,4},{1,5},{2,6},{3,7},{4,0},{5,1},{6,2},{7,3},{8,12},{9,13},{10,... | collective-permute-start | bytes 3145736 | tf_op jit(solution)/shard_map/ppermute | solution.py:359
  27.3 8.3 %collective-permute-start.9 = (bf16[544,256]{1,0:T(8,128)(2,1)S(1)}, bf16[544,256]{1,0:T(8,128)(2,1)S(1)}, u32[]{:S(2)}, u32[]{:S(2)}) collective-permute-start(bf16[544,256]{1,0:T(8,128)(2,1)S(1)} %shard_map.76), channel_id=1, source_target_pairs={{0,1},{1,0},{2,3},{3,2},{4,5},{5,4},{6,7},{7,6},{8,9},{9,8},{10,11... | collective-permute-start | bytes 835592 | tf_op jit(solution)/shard_map/ppermute | solution.py:359
  27.7 9.6 %collective-permute-start.20 = (bf16[544,256]{1,0:T(8,128)(2,1)S(1)}, bf16[544,256]{1,0:T(8,128)(2,1)S(1)}, u32[]{:S(2)}, u32[]{:S(2)}) collective-permute-start(bf16[544,256]{1,0:T(8,128)(2,1)S(1)} %shard_map.84), channel_id=1, source_target_pairs={{0,4},{1,2},{2,1},{3,7},{4,0},{5,6},{6,5},{7,3},{8,12},{9,10},{10,... | collective-permute-start | bytes 835592 | tf_op jit(solution)/shard_map/ppermute | solution.py:359
  35.7 16.3 %collective-permute-start.14 = (bf16[544,256]{1,0:T(8,128)(2,1)S(1)}, bf16[544,256]{1,0:T(8,128)(2,1)S(1)}, u32[]{:S(2)}, u32[]{:S(2)}) collective-permute-start(bf16[544,256]{1,0:T(8,128)(2,1)S(1)} %shard_map.80), channel_id=1, source_target_pairs={{0,4},{1,2},{2,1},{3,7},{4,0},{5,6},{6,5},{7,3},{8,12},{9,10},{10,... | collective-permute-start | bytes 835592 | tf_op jit(solution)/shard_map/ppermute | solution.py:359
  36.9 11.8 %collective-permute-start.8 = (bf16[2,256,256]{2,1,0:T(8,128)(2,1)S(1)}, bf16[2,256,256]{2,1,0:T(8,128)(2,1)S(1)}, u32[]{:S(2)}, u32[]{:S(2)}) collective-permute-start(bf16[2,256,256]{2,1,0:T(8,128)(2,1)S(1)} %shard_map.75.refs_2_), channel_id=1, source_target_pairs={{0,4},{1,2},{2,1},{3,7},{4,0},{5,6},{6,5},{7,3},{8,12},{9,10},{10,... | collective-permute-start | bytes 786440 | tf_op jit(solution)/shard_map/ppermute | solution.py:359
  37.3 13.2 %collective-permute-start.4 = (bf16[2,256,256]{2,1,0:T(8,128)(2,1)S(1)}, bf16[2,256,256]{2,1,0:T(8,128)(2,1)S(1)}, u32[]{:S(2)}, u32[]{:S(2)}) collective-permute-start(bf16[2,256,256]{2,1,0:T(8,128)(2,1)S(1)} %shard_map.75.refs_2_), channel_id=1, source_target_pairs={{0,1},{1,0},{2,3},{3,2},{4,5},{5,4},{6,7},{7,6},{8,9},{9,8},{10,11... | collective-permute-start | bytes 786440 | tf_op jit(solution)/shard_map/ppermute | solution.py:359
  48.8 23.2 %collective-permute-start.21 = (bf16[544,256]{1,0:T(8,128)(2,1)S(1)}, bf16[544,256]{1,0:T(8,128)(2,1)S(1)}, u32[]{:S(2)}, u32[]{:S(2)}) collective-permute-start(bf16[544,256]{1,0:T(8,128)(2,1)S(1)} %shard_map.85), channel_id=1, source_target_pairs={{0,4},{1,5},{2,3},{3,2},{4,0},{5,1},{6,7},{7,6},{8,12},{9,13},{10,... | collective-permute-start | bytes 835592 | tf_op jit(solution)/shard_map/ppermute | solution.py:359
  50.5 7.9 %collective-permute-start.7 = (bf16[2,256,256]{2,1,0:T(8,128)(2,1)S(1)}, bf16[2,256,256]{2,1,0:T(8,128)(2,1)S(1)}, u32[]{:S(2)}, u32[]{:S(2)}) collective-permute-start(bf16[2,256,256]{2,1,0:T(8,128)(2,1)S(1)} %collective-permute-done.6.piece_ref.refs_4_), channel_id=1, source_target_pairs={{0,16},{1,17},{2,18},{3,19},{4,20},{5,21},{6,22},{7,23},{8,24},{9,... | collective-permute-start | bytes 786440 | tf_op jit(solution)/shard_map/ppermute | solution.py:359
  51.7 12.2 %collective-permute-start.5 = (bf16[2,256,256]{2,1,0:T(8,128)(2,1)S(1)}, bf16[2,256,256]{2,1,0:T(8,128)(2,1)S(1)}, u32[]{:S(2)}, u32[]{:S(2)}) collective-permute-start(bf16[2,256,256]{2,1,0:T(8,128)(2,1)S(1)} %collective-permute-done.4.refs_3_), channel_id=1, source_target_pairs={{0,16},{1,17},{2,18},{3,19},{4,20},{5,21},{6,22},{7,23},{8,24},{9,... | collective-permute-start | bytes 786440 | tf_op jit(solution)/shard_map/ppermute | solution.py:359
  52.0 17.6 %collective-permute-start.10 = (bf16[2,256,256]{2,1,0:T(8,128)(2,1)S(1)}, bf16[2,256,256]{2,1,0:T(8,128)(2,1)S(1)}, u32[]{:S(2)}, u32[]{:S(2)}) collective-permute-start(bf16[2,256,256]{2,1,0:T(8,128)(2,1)S(1)} %shard_map.77.refs_5_), channel_id=1, source_target_pairs={{0,16},{1,17},{2,18},{3,19},{4,20},{5,21},{6,22},{7,23},{8,24},{9,... | collective-permute-start | bytes 786440 | tf_op jit(solution)/shard_map/ppermute | solution.py:359
  53.3 22.7 %collective-permute-start.15 = (bf16[544,256]{1,0:T(8,128)(2,1)S(1)}, bf16[544,256]{1,0:T(8,128)(2,1)S(1)}, u32[]{:S(2)}, u32[]{:S(2)}) collective-permute-start(bf16[544,256]{1,0:T(8,128)(2,1)S(1)} %shard_map.81), channel_id=1, source_target_pairs={{0,4},{1,5},{2,3},{3,2},{4,0},{5,1},{6,7},{7,6},{8,12},{9,13},{10,... | collective-permute-start | bytes 835592 | tf_op jit(solution)/shard_map/ppermute | solution.py:359
  58.4 13.7 %collective-permute-start.16 = (bf16[256,256]{1,0:T(8,128)(2,1)S(1)}, bf16[256,256]{1,0:T(8,128)(2,1)S(1)}, u32[]{:S(2)}, u32[]{:S(2)}) collective-permute-start(bf16[256,256]{1,0:T(8,128)(2,1)S(1)} %get-tuple-element.41), channel_id=1, source_target_pairs={{0,8},{1,9},{2,10},{3,11},{4,12},{5,13},{6,14},{7,15},{8,0},{9,1},... | collective-permute-start | bytes 393224 | tf_op jit(solution)/shard_map/ppermute | solution.py:359
  64.0 8.4 %collective-permute-start.18 = (bf16[256,256]{1,0:T(8,128)(2,1)S(1)}, bf16[256,256]{1,0:T(8,128)(2,1)S(1)}, u32[]{:S(2)}, u32[]{:S(2)}) collective-permute-start(bf16[256,256]{1,0:T(8,128)(2,1)S(1)} %get-tuple-element.43), channel_id=1, source_target_pairs={{0,12},{1,13},{2,14},{3,15},{4,8},{5,9},{6,10},{7,11},{8,4},{9,5},... | collective-permute-start | bytes 393224 | tf_op jit(solution)/shard_map/ppermute | solution.py:359
  69.6 4.6 %collective-permute-start.17 = (f32[256,256]{1,0:T(8,128)S(1)}, f32[256,256]{1,0:T(8,128)S(1)}, u32[]{:S(2)}, u32[]{:S(2)}) collective-permute-start(f32[256,256]{1,0:T(8,128)S(1)} %get-tuple-element.42), channel_id=1, source_target_pairs={{0,4},{1,5},{2,6},{3,7},{4,0},{5,1},{6,2},{7,3},{8,12},{9,13},{10,... | collective-permute-start | bytes 786440 | tf_op jit(solution)/shard_map/ppermute | solution.py:359
  72.0 8.2 %collective-permute-start.12 = (f32[256,256]{1,0:T(8,128)S(1)}, f32[256,256]{1,0:T(8,128)S(1)}, u32[]{:S(2)}, u32[]{:S(2)}) collective-permute-start(f32[256,256]{1,0:T(8,128)S(1)} %get-tuple-element.35), channel_id=1, source_target_pairs={{0,4},{1,5},{2,6},{3,7},{4,0},{5,1},{6,2},{7,3},{8,12},{9,13},{10,... | collective-permute-start | bytes 786440 | tf_op jit(solution)/shard_map/ppermute | solution.py:359
  72.1 4.7 %collective-permute-start.11 = (bf16[256,256]{1,0:T(8,128)(2,1)S(1)}, bf16[256,256]{1,0:T(8,128)(2,1)S(1)}, u32[]{:S(2)}, u32[]{:S(2)}) collective-permute-start(bf16[256,256]{1,0:T(8,128)(2,1)S(1)} %get-tuple-element.34), channel_id=1, source_target_pairs={{0,8},{1,9},{2,10},{3,11},{4,12},{5,13},{6,14},{7,15},{8,0},{9,1},... | collective-permute-start | bytes 393224 | tf_op jit(solution)/shard_map/ppermute | solution.py:359
  72.4 7.8 %collective-permute-start.13 = (bf16[256,256]{1,0:T(8,128)(2,1)S(1)}, bf16[256,256]{1,0:T(8,128)(2,1)S(1)}, u32[]{:S(2)}, u32[]{:S(2)}) collective-permute-start(bf16[256,256]{1,0:T(8,128)(2,1)S(1)} %get-tuple-element.36), channel_id=1, source_target_pairs={{0,12},{1,13},{2,14},{3,15},{4,8},{5,9},{6,10},{7,11},{8,4},{9,5},... | collective-permute-start | bytes 393224 | tf_op jit(solution)/shard_map/ppermute | solution.py:359
  (3 other events, 8.7 us)

commit v4 on v3

--- a/solution.py
+++ b/solution.py
@@ -216,7 +216,7 @@
             out_ref[j] = outer_ref[j * rows : (j + 1) * rows, :]
 
 
-def away_kernel(nz, ng, phase, count, *refs):
+def away_kernel(nz, ng, phase, swapped, count, *refs):
     first = 2 if phase else 1
     tokens, parts = refs[:count], refs[count : count + first + nz - 1]
     outs, whole = refs[count + len(parts) : -1], refs[-1]
@@ -231,9 +231,13 @@
     for part in parts[first:]:
         values.append((part[0], part[1]))
     for s in range(nz):
+        source = place ^ s
+        if swapped and s >= 2:
+            inner = jnp.logical_or(place == 1, place == 2)
+            source = jnp.where(inner, place ^ (5 - s), source)
         for j in range(CORES):
             owner = lax.rem(core + j, CORES)
-            row = pl.multiple_of((owner * nz + (place ^ s)) * rows, rows)
+            row = pl.multiple_of((owner * nz + source) * rows, rows)
             whole[pl.ds(row, rows), :] = values[s][j]
     for token, out in zip(tokens, outs):
         value = jnp.dot(token[...], whole[...], preferred_element_type=f32)
@@ -443,7 +447,7 @@
         own = [prepared[1 + 3 * r] for r in range(ng)]
         first = [prepared[2 + 3 * r] for r in range(ng)]
         side = [prepared[3 + 3 * r] for r in range(ng)]
-        states = [[over_ctx(first[0], links(0))]] + [[] for _ in range(1, ng)]
+        states = [[] for _ in range(ng)]
 
         def extend(hop, r):
             message_out = call(
@@ -455,30 +459,31 @@
             )
             states[r].append(over_ctx(message_out, links(hop - 1)))
 
-        gathered = {
-            s: over_ctx(packed, {z: z ^ s for z in range(nz)})
-            for s in (range(1, nz) if not compact(mesh) else (2, 1))
-        }
         if compact(mesh):
-            inside = over_ctx(packed, links(1))
-            mixed = call(
-                mix_kernel,
-                first[1], gathered[2],
-                out_shape=message,
-                in_specs=[VMEM] * 2,
-                out_specs=VMEM,
-            )
-            outside = over_ctx(mixed, {**links(0), **links(2)})
-            states[1].append(outside)
-            gathered[3] = call(
-                pick_kernel,
-                inside, outside,
-                out_shape=jax.ShapeDtypeStruct(packed.shape, bf16),
-                in_specs=[VMEM] * 2,
-                out_specs=VMEM,
-            )
+            near = over_ctx(packed, {z: z ^ 1 for z in range(nz)})
+            middle = over_ctx(packed, links(1))
+            across = over_ctx(near, links(1))
+            gathered = {1: near}
+            for r, inside in enumerate((middle, across)):
+                mixed = call(
+                    mix_kernel,
+                    first[r], inside,
+                    out_shape=message,
+                    in_specs=[VMEM] * 2,
+                    out_specs=VMEM,
+                )
+                outside = over_ctx(mixed, {**links(0), **links(2)})
+                states[r].append(outside)
+                gathered[r + 2] = call(
+                    pick_kernel,
+                    inside, outside,
+                    out_shape=jax.ShapeDtypeStruct(packed.shape, bf16),
+                    in_specs=[VMEM] * 2,
+                    out_specs=VMEM,
+                )
         else:
-            for r in range(1, ng):
+            gathered = {s: over_ctx(packed, {z: z ^ s for z in range(nz)}) for s in range(1, nz)}
+            for r in range(ng):
                 states[r].append(over_ctx(first[r], links(0)))
         for hop in range(2, nz):
             for r in range(ng):
@@ -493,7 +498,7 @@
             small = jax.ShapeDtypeStruct((length, width), bf16)
             count = CORES * (nx - 1)
             sent = call(
-                functools.partial(away_kernel, nz, ng, r, count),
+                functools.partial(away_kernel, nz, ng, r, compact(mesh), count),
                 *tokens[CORES:], *pieces[r],
                 out_shape=(small,) * count + (jax.ShapeDtypeStruct((depth, width), bf16),),
                 in_specs=[VMEM] * (count + len(pieces[r])),

time: 83 us -> 77.5 us (0.934)
  waiting for transfers between devices: 50.5 us -> 41.5 us
  starting transfers between devices: 20 us -> 23.4 us
    ppermute x22, waiting for transfers between devices: 50.5 us -> 41.5 us  [send(): return lax.ppermute(value, AXES, moves(mesh, where))]
    ppermute x22, starting transfers between devices: 20 us -> 23.4 us  [send(): return lax.ppermute(value, AXES, moves(mesh, where))]
    pallas_call x15 -> x17, Pallas kernels: 12.1 us -> 12.1 us  [call(): return pl.pallas_call(kernel, compiler_params=params, **options)(*args)]
  transfers between devices with their start and end apart: 22 -> 22, of which waited for: 8 -> 10; matrix products, arithmetic and copies ran while one was open for 0% -> 0% of each run, Pallas kernels for 10% -> 10%
where the time goes in v4:
time: 77.5 us; the launch traced here: 77.3 us
  waiting for transfers between devices  41.5 us (54%)
  starting transfers between devices  23.4 us (30%)
  Pallas kernels  12.1 us (16%)
    ppermute x22, waiting for transfers between devices, send(): return lax.ppermute(value, AXES, moves(mesh, where))  41.5 us
    ppermute x22, starting transfers between devices, send(): return lax.ppermute(value, AXES, moves(mesh, where))  23.4 us
    pallas_call x17, Pallas kernels, call(): return pl.pallas_call(kernel, compiler_params=params, **options)(*args)  12.1 us
  transfers between devices with their start and end apart: 22, of which 10 were waited for; matrix products, arithmetic and copies ran while one was open for 0% of the time, Pallas kernels for 10%

profile of v4, /device:TPU:11, one launch (start us, length us, event | category | flops | bytes accessed | tf_op | source)
XLA Modules:
  0.0 77.3 jit_solution(16761906564939823850)
XLA Ops:
  0.0 1.6 %shard_map.74 = (bf16[256,512]{1,0:T(8,128)(2,1)S(1)}, bf16[256,256]{1,0:T(8,128)(2,1)S(1)}, bf16[256,256]{1,0:T(8,128)(2,1)S(1)}, bf16[256,2048]{1,0:T(8,128)(2,1)S(1)}) custom-call(bf16[256,4096]{1,0:T(8,128)(2,1)} %bitcast.18, bf16[256,1024]{1,0:T(8,128)(2,1)} %w_ref.1), custom_call_target="tpu_custom_call" | custom-call | tf_op jit(solution)/shard_map/pallas_call | solution.py:370
  4.2 2.6 %shard_map.73 = (bf16[256,2048]{1,0:T(8,128)(2,1)S(1)}, f32[512,256]{1,0:T(8,128)S(1)}, bf16[544,256]{1,0:T(8,128)(2,1)S(1)}, f32[16,256]{1,0:T(8,128)S(1)}, f32...) custom-call(bf16[256,1024]{1,0:T(8,128)(2,1)S(1)} %bitcast.6, ...), custom_call_target="tpu_custom_call" | custom-call | tf_op jit(solution)/shard_map/pallas_call | solution.py:370
  7.3 2.8 %collective-permute-start.6 = (bf16[2,256,256]{2,1,0:T(8,128)(2,1)S(1)}, bf16[2,256,256]{2,1,0:T(8,128)(2,1)S(1)}, u32[]{:S(2)}, u32[]{:S(2)}) collective-permute-start(bf16[2,256,256]{2,1,0:T(8,128)(2,1)S(1)} %shard_map.75.refs_2_), channel_id=1, source_target_pairs={{0,4},{1,2},{2,1},{3,7},{4,0},{5,6},{6,5},{7,3},{8,12},{9,10},{10,... | collective-permute-start | bytes 786440 | tf_op jit(solution)/shard_map/ppermute | solution.py:363
  10.1 1.5 %collective-permute-done.4.refs_3_ = bf16[2,256,256]{2,1,0:T(8,128)(2,1)S(1)} collective-permute-done((bf16[2,256,256]{2,1,0:T(8,128)(2,1)S(1)}, bf16[2,256,256]{2,1,0:T(8,128)(2,1)S(1)}, u32[]{:S(2)}, u32[]{:S(2)}) %collective-permute-start.4) | collective-permute-done | bytes 262176 | tf_op jit(solution)/shard_map/ppermute | solution.py:363
  11.6 1.3 %collective-permute-start.9 = (bf16[2,256,256]{2,1,0:T(8,128)(2,1)S(1)}, bf16[2,256,256]{2,1,0:T(8,128)(2,1)S(1)}, u32[]{:S(2)}, u32[]{:S(2)}) collective-permute-start(bf16[2,256,256]{2,1,0:T(8,128)(2,1)S(1)} %collective-permute-done.4.refs_3_), channel_id=1, source_target_pairs={{0,4},{1,2},{2,1},{3,7},{4,0},{5,6},{6,5},{7,3},{8,12},{9,10},{10,... | collective-permute-start | bytes 786440 | tf_op jit(solution)/shard_map/ppermute | solution.py:363
  12.9 12.8 %collective-permute-done.1.refs_0_ = bf16[256,2048]{1,0:T(8,128)(2,1)S(1)} collective-permute-done((bf16[256,2048]{1,0:T(8,128)(2,1)S(1)}, bf16[256,2048]{1,0:T(8,128)(2,1)S(1)}, u32[]{:S(2)}, u32[]{:S(2)}) %collective-permute-start.1) | collective-permute-done | bytes 1048608 | tf_op jit(solution)/shard_map/ppermute | solution.py:363
  25.7 1.5 %collective-permute-start.2 = (bf16[256,2048]{1,0:T(8,128)(2,1)S(1)}, bf16[256,2048]{1,0:T(8,128)(2,1)S(1)}, u32[]{:S(2)}, u32[]{:S(2)}) collective-permute-start(bf16[256,2048]{1,0:T(8,128)(2,1)S(1)} %collective-permute-done.1.refs_0_), channel_id=1, source_target_pairs={{0,4},{1,5},{2,6},{3,7},{4,0},{5,1},{6,2},{7,3},{8,12},{9,13},{10,... | collective-permute-start | bytes 3145736 | tf_op jit(solution)/shard_map/ppermute | solution.py:363
  27.5 1.4 %collective-permute-start.10 = (bf16[544,256]{1,0:T(8,128)(2,1)S(1)}, bf16[544,256]{1,0:T(8,128)(2,1)S(1)}, u32[]{:S(2)}, u32[]{:S(2)}) collective-permute-start(bf16[544,256]{1,0:T(8,128)(2,1)S(1)} %shard_map.78), channel_id=1, source_target_pairs={{0,1},{1,0},{2,3},{3,2},{4,5},{5,4},{6,7},{7,6},{8,9},{9,8},{10,11... | collective-permute-start | bytes 835592 | tf_op jit(solution)/shard_map/ppermute | solution.py:363
  28.9 6.6 %collective-permute-done.7.outer_ref.prev_ref.refs_9_ = bf16[544,256]{1,0:T(8,128)(2,1)S(1)} collective-permute-done((bf16[544,256]{1,0:T(8,128)(2,1)S(1)}, bf16[544,256]{1,0:T(8,128)(2,1)S(1)}, u32[]{:S(2)}, u32[]{:S(2)}) %collective-permute-start.7) | collective-permute-done | bytes 278560 | tf_op jit(solution)/shard_map/ppermute | solution.py:363
  35.7 1.2 %collective-permute-start.20 = (bf16[544,256]{1,0:T(8,128)(2,1)S(1)}, bf16[544,256]{1,0:T(8,128)(2,1)S(1)}, u32[]{:S(2)}, u32[]{:S(2)}) collective-permute-start(bf16[544,256]{1,0:T(8,128)(2,1)S(1)} %shard_map.86), channel_id=1, source_target_pairs={{0,4},{1,2},{2,1},{3,7},{4,0},{5,6},{6,5},{7,3},{8,12},{9,10},{10,... | collective-permute-start | bytes 835592 | tf_op jit(solution)/shard_map/ppermute | solution.py:363
  36.9 4.6 %collective-permute-done.10.outer_ref.prev_ref.refs_9_ = bf16[544,256]{1,0:T(8,128)(2,1)S(1)} collective-permute-done((bf16[544,256]{1,0:T(8,128)(2,1)S(1)}, bf16[544,256]{1,0:T(8,128)(2,1)S(1)}, u32[]{:S(2)}, u32[]{:S(2)}) %collective-permute-start.10) | collective-permute-done | bytes 278560 | tf_op jit(solution)/shard_map/ppermute | solution.py:363
  41.7 1.2 %collective-permute-start.15 = (bf16[544,256]{1,0:T(8,128)(2,1)S(1)}, bf16[544,256]{1,0:T(8,128)(2,1)S(1)}, u32[]{:S(2)}, u32[]{:S(2)}) collective-permute-start(bf16[544,256]{1,0:T(8,128)(2,1)S(1)} %shard_map.82), channel_id=1, source_target_pairs={{0,4},{1,2},{2,1},{3,7},{4,0},{5,6},{6,5},{7,3},{8,12},{9,10},{10,... | collective-permute-start | bytes 835592 | tf_op jit(solution)/shard_map/ppermute | solution.py:363
  42.9 2.0 %collective-permute-start.21 = (bf16[544,256]{1,0:T(8,128)(2,1)S(1)}, bf16[544,256]{1,0:T(8,128)(2,1)S(1)}, u32[]{:S(2)}, u32[]{:S(2)}) collective-permute-start(bf16[544,256]{1,0:T(8,128)(2,1)S(1)} %shard_map.87), channel_id=1, source_target_pairs={{0,4},{1,5},{2,3},{3,2},{4,0},{5,1},{6,7},{7,6},{8,12},{9,13},{10,... | collective-permute-start | bytes 835592 | tf_op jit(solution)/shard_map/ppermute | solution.py:363
  45.0 1.2 %collective-permute-start.5 = (bf16[2,256,256]{2,1,0:T(8,128)(2,1)S(1)}, bf16[2,256,256]{2,1,0:T(8,128)(2,1)S(1)}, u32[]{:S(2)}, u32[]{:S(2)}) collective-permute-start(bf16[2,256,256]{2,1,0:T(8,128)(2,1)S(1)} %collective-permute-done.4.refs_3_), channel_id=1, source_target_pairs={{0,16},{1,17},{2,18},{3,19},{4,20},{5,21},{6,22},{7,23},{8,24},{9,... | collective-permute-start | bytes 786440 | tf_op jit(solution)/shard_map/ppermute | solution.py:363
  46.6 2.6 %collective-permute-done.15.prev_ref.refs_10_ = bf16[544,256]{1,0:T(8,128)(2,1)S(1)} collective-permute-done((bf16[544,256]{1,0:T(8,128)(2,1)S(1)}, bf16[544,256]{1,0:T(8,128)(2,1)S(1)}, u32[]{:S(2)}, u32[]{:S(2)}) %collective-permute-start.15) | collective-permute-done | bytes 278560 | tf_op jit(solution)/shard_map/ppermute | solution.py:363
  49.1 1.2 %collective-permute-start.11 = (bf16[2,256,256]{2,1,0:T(8,128)(2,1)S(1)}, bf16[2,256,256]{2,1,0:T(8,128)(2,1)S(1)}, u32[]{:S(2)}, u32[]{:S(2)}) collective-permute-start(bf16[2,256,256]{2,1,0:T(8,128)(2,1)S(1)} %shard_map.79.refs_5_), channel_id=1, source_target_pairs={{0,16},{1,17},{2,18},{3,19},{4,20},{5,21},{6,22},{7,23},{8,24},{9,... | collective-permute-start | bytes 786440 | tf_op jit(solution)/shard_map/ppermute | solution.py:363
  50.4 2.1 %collective-permute-start.16 = (bf16[544,256]{1,0:T(8,128)(2,1)S(1)}, bf16[544,256]{1,0:T(8,128)(2,1)S(1)}, u32[]{:S(2)}, u32[]{:S(2)}) collective-permute-start(bf16[544,256]{1,0:T(8,128)(2,1)S(1)} %shard_map.83), channel_id=1, source_target_pairs={{0,4},{1,5},{2,3},{3,2},{4,0},{5,1},{6,7},{7,6},{8,12},{9,13},{10,... | collective-permute-start | bytes 835592 | tf_op jit(solution)/shard_map/ppermute | solution.py:363
  54.3 4.1 %collective-permute-done.8.refs_5_ = bf16[2,256,256]{2,1,0:T(8,128)(2,1)S(1)} collective-permute-done((bf16[2,256,256]{2,1,0:T(8,128)(2,1)S(1)}, bf16[2,256,256]{2,1,0:T(8,128)(2,1)S(1)}, u32[]{:S(2)}, u32[]{:S(2)}) %collective-permute-start.8) | collective-permute-done | bytes 262176 | tf_op jit(solution)/shard_map/ppermute | solution.py:363
  58.4 1.6 %collective-permute-start.19 = (bf16[256,256]{1,0:T(8,128)(2,1)S(1)}, bf16[256,256]{1,0:T(8,128)(2,1)S(1)}, u32[]{:S(2)}, u32[]{:S(2)}) collective-permute-start(bf16[256,256]{1,0:T(8,128)(2,1)S(1)} %get-tuple-element.44), channel_id=1, source_target_pairs={{0,12},{1,13},{2,14},{3,15},{4,8},{5,9},{6,10},{7,11},{8,4},{9,5},... | collective-permute-start | bytes 393224 | tf_op jit(solution)/shard_map/ppermute | solution.py:363
  60.0 4.0 %collective-permute-done.11.refs_6_ = bf16[2,256,256]{2,1,0:T(8,128)(2,1)S(1)} collective-permute-done((bf16[2,256,256]{2,1,0:T(8,128)(2,1)S(1)}, bf16[2,256,256]{2,1,0:T(8,128)(2,1)S(1)}, u32[]{:S(2)}, u32[]{:S(2)}) %collective-permute-start.11) | collective-permute-done | bytes 262176 | tf_op jit(solution)/shard_map/ppermute | solution.py:363
  66.9 1.8 %collective-permute-start.14 = (bf16[256,256]{1,0:T(8,128)(2,1)S(1)}, bf16[256,256]{1,0:T(8,128)(2,1)S(1)}, u32[]{:S(2)}, u32[]{:S(2)}) collective-permute-start(bf16[256,256]{1,0:T(8,128)(2,1)S(1)} %get-tuple-element.37), channel_id=1, source_target_pairs={{0,12},{1,13},{2,14},{3,15},{4,8},{5,9},{6,10},{7,11},{8,4},{9,5},... | collective-permute-start | bytes 393224 | tf_op jit(solution)/shard_map/ppermute | solution.py:363
  68.7 1.8 %shard_map.88.refs_12_ = bf16[256,512]{1,0:T(8,128)(2,1)S(1)} custom-call(f32[256,256]{1,0:T(8,128)S(1)} %get-tuple-element.41.refs_0_, bf16[256,256]{1,0:T(8,128)(2,1)S(1)} %collective-permute-done.17.refs_1_, f32[256,256]{1,0:T(8,128)S(1)} %collective-permute-done.18.refs_2_, bf16[256,256]{1,0:T(8,128)(2,1)S(1)} %collective-permute-done.19.refs_3_, ...), custom_call_target="tpu_custom_call" | custom-call | tf_op jit(solution)/shard_map/pallas_call | solution.py:370
  71.2 3.4 %collective-permute-done.14.refs_3_ = bf16[256,256]{1,0:T(8,128)(2,1)S(1)} collective-permute-done((bf16[256,256]{1,0:T(8,128)(2,1)S(1)}, bf16[256,256]{1,0:T(8,128)(2,1)S(1)}, u32[]{:S(2)}, u32[]{:S(2)}) %collective-permute-start.14) | collective-permute-done | bytes 131104 | tf_op jit(solution)/shard_map/ppermute | solution.py:363
  74.6 2.6 %shard_map.89 = bf16[256,1024]{1,0:T(8,128)(2,1)} custom-call(f32[256,256]{1,0:T(8,128)S(1)} %get-tuple-element.34.refs_0_, bf16[256,256]{1,0:T(8,128)(2,1)S(1)} %collective-permute-done.12.refs_1_, f32[256,256]{1,0:T(8,128)S(1)} %collective-permute-done.13.refs_2_, bf16[256,256]{1,0:T(8,128)(2,1)S(1)} %collective-permute-done.14.refs_3_, ...), custom_call_target="tpu_custom_call" | custom-call | tf_op jit(solution)/shard_map/pallas_call | solution.py:370
  (47 shorter events, 9.3 us)
Async XLA Ops:
  0.0 4.2 %copy-start.1 = (bf16[1,256,1024]{2,1,0:T(8,128)(2,1)S(1)}, bf16[1,256,1024]{2,1,0:T(8,128)(2,1)}, u32[]{:S(2)}) copy-start(bf16[1,256,1024]{2,1,0:T(8,128)(2,1)} %param.10) | copy-start | bytes 1572868
  0.0 4.2 %copy-start = (bf16[1,256,1024]{2,1,0:T(8,128)(2,1)S(1)}, bf16[1,256,1024]{2,1,0:T(8,128)(2,1)}, u32[]{:S(2)}) copy-start(bf16[1,256,1024]{2,1,0:T(8,128)(2,1)} %param.9) | copy-start | bytes 1572868
  1.6 24.1 %collective-permute-start.1 = (bf16[256,2048]{1,0:T(8,128)(2,1)S(1)}, bf16[256,2048]{1,0:T(8,128)(2,1)S(1)}, u32[]{:S(2)}, u32[]{:S(2)}) collective-permute-start(bf16[256,2048]{1,0:T(8,128)(2,1)S(1)} %get-tuple-element.27), channel_id=1, source_target_pairs={{0,8},{1,9},{2,10},{3,11},{4,12},{5,13},{6,14},{7,15},{8,0},{9,1},... | collective-permute-start | bytes 3145736 | tf_op jit(solution)/shard_map/ppermute | solution.py:363
  1.9 2.1 %collective-permute-start.3 = (bf16[256,512]{1,0:T(8,128)(2,1)S(1)}, bf16[256,512]{1,0:T(8,128)(2,1)S(1)}, u32[]{:S(2)}, u32[]{:S(2)}) collective-permute-start(bf16[256,512]{1,0:T(8,128)(2,1)S(1)} %get-tuple-element.29), channel_id=1, source_target_pairs={{0,4},{1,5},{2,6},{3,7},{4,0},{5,1},{6,2},{7,3},{8,12},{9,13},{10,... | collective-permute-start | bytes 786440 | tf_op jit(solution)/shard_map/ppermute | solution.py:363
  4.1 7.6 %collective-permute-start.4 = (bf16[2,256,256]{2,1,0:T(8,128)(2,1)S(1)}, bf16[2,256,256]{2,1,0:T(8,128)(2,1)S(1)}, u32[]{:S(2)}, u32[]{:S(2)}) collective-permute-start(bf16[2,256,256]{2,1,0:T(8,128)(2,1)S(1)} %shard_map.75.refs_2_), channel_id=1, source_target_pairs={{0,1},{1,0},{2,3},{3,2},{4,5},{5,4},{6,7},{7,6},{8,9},{9,8},{10,11... | collective-permute-start | bytes 786440 | tf_op jit(solution)/shard_map/ppermute | solution.py:363
  6.8 39.4 %collective-permute-start = (bf16[256,2048]{1,0:T(8,128)(2,1)S(1)}, bf16[256,2048]{1,0:T(8,128)(2,1)S(1)}, u32[]{:S(2)}, u32[]{:S(2)}) collective-permute-start(bf16[256,2048]{1,0:T(8,128)(2,1)S(1)} %get-tuple-element.26.refs_0_), channel_id=1, source_target_pairs={{0,4},{1,5},{2,6},{3,7},{4,0},{5,1},{6,2},{7,3},{8,12},{9,13},{10,... | collective-permute-start | bytes 3145736 | tf_op jit(solution)/shard_map/ppermute | solution.py:363
  7.3 20.0 %collective-permute-start.6 = (bf16[2,256,256]{2,1,0:T(8,128)(2,1)S(1)}, bf16[2,256,256]{2,1,0:T(8,128)(2,1)S(1)}, u32[]{:S(2)}, u32[]{:S(2)}) collective-permute-start(bf16[2,256,256]{2,1,0:T(8,128)(2,1)S(1)} %shard_map.75.refs_2_), channel_id=1, source_target_pairs={{0,4},{1,2},{2,1},{3,7},{4,0},{5,6},{6,5},{7,3},{8,12},{9,10},{10,... | collective-permute-start | bytes 786440 | tf_op jit(solution)/shard_map/ppermute | solution.py:363
  11.6 15.9 %collective-permute-start.9 = (bf16[2,256,256]{2,1,0:T(8,128)(2,1)S(1)}, bf16[2,256,256]{2,1,0:T(8,128)(2,1)S(1)}, u32[]{:S(2)}, u32[]{:S(2)}) collective-permute-start(bf16[2,256,256]{2,1,0:T(8,128)(2,1)S(1)} %collective-permute-done.4.refs_3_), channel_id=1, source_target_pairs={{0,4},{1,2},{2,1},{3,7},{4,0},{5,6},{6,5},{7,3},{8,12},{9,10},{10,... | collective-permute-start | bytes 786440 | tf_op jit(solution)/shard_map/ppermute | solution.py:363
  25.7 24.7 %collective-permute-start.2 = (bf16[256,2048]{1,0:T(8,128)(2,1)S(1)}, bf16[256,2048]{1,0:T(8,128)(2,1)S(1)}, u32[]{:S(2)}, u32[]{:S(2)}) collective-permute-start(bf16[256,2048]{1,0:T(8,128)(2,1)S(1)} %collective-permute-done.1.refs_0_), channel_id=1, source_target_pairs={{0,4},{1,5},{2,6},{3,7},{4,0},{5,1},{6,2},{7,3},{8,12},{9,13},{10,... | collective-permute-start | bytes 3145736 | tf_op jit(solution)/shard_map/ppermute | solution.py:363
  27.3 8.3 %collective-permute-start.7 = (bf16[544,256]{1,0:T(8,128)(2,1)S(1)}, bf16[544,256]{1,0:T(8,128)(2,1)S(1)}, u32[]{:S(2)}, u32[]{:S(2)}) collective-permute-start(bf16[544,256]{1,0:T(8,128)(2,1)S(1)} %shard_map.76), channel_id=1, source_target_pairs={{0,1},{1,0},{2,3},{3,2},{4,5},{5,4},{6,7},{7,6},{8,9},{9,8},{10,11... | collective-permute-start | bytes 835592 | tf_op jit(solution)/shard_map/ppermute | solution.py:363
  27.5 14.0 %collective-permute-start.10 = (bf16[544,256]{1,0:T(8,128)(2,1)S(1)}, bf16[544,256]{1,0:T(8,128)(2,1)S(1)}, u32[]{:S(2)}, u32[]{:S(2)}) collective-permute-start(bf16[544,256]{1,0:T(8,128)(2,1)S(1)} %shard_map.78), channel_id=1, source_target_pairs={{0,1},{1,0},{2,3},{3,2},{4,5},{5,4},{6,7},{7,6},{8,9},{9,8},{10,11... | collective-permute-start | bytes 835592 | tf_op jit(solution)/shard_map/ppermute | solution.py:363
  35.7 7.2 %collective-permute-start.20 = (bf16[544,256]{1,0:T(8,128)(2,1)S(1)}, bf16[544,256]{1,0:T(8,128)(2,1)S(1)}, u32[]{:S(2)}, u32[]{:S(2)}) collective-permute-start(bf16[544,256]{1,0:T(8,128)(2,1)S(1)} %shard_map.86), channel_id=1, source_target_pairs={{0,4},{1,2},{2,1},{3,7},{4,0},{5,6},{6,5},{7,3},{8,12},{9,10},{10,... | collective-permute-start | bytes 835592 | tf_op jit(solution)/shard_map/ppermute | solution.py:363
  41.7 7.4 %collective-permute-start.15 = (bf16[544,256]{1,0:T(8,128)(2,1)S(1)}, bf16[544,256]{1,0:T(8,128)(2,1)S(1)}, u32[]{:S(2)}, u32[]{:S(2)}) collective-permute-start(bf16[544,256]{1,0:T(8,128)(2,1)S(1)} %shard_map.82), channel_id=1, source_target_pairs={{0,4},{1,2},{2,1},{3,7},{4,0},{5,6},{6,5},{7,3},{8,12},{9,10},{10,... | collective-permute-start | bytes 835592 | tf_op jit(solution)/shard_map/ppermute | solution.py:363
  42.9 23.5 %collective-permute-start.21 = (bf16[544,256]{1,0:T(8,128)(2,1)S(1)}, bf16[544,256]{1,0:T(8,128)(2,1)S(1)}, u32[]{:S(2)}, u32[]{:S(2)}) collective-permute-start(bf16[544,256]{1,0:T(8,128)(2,1)S(1)} %shard_map.87), channel_id=1, source_target_pairs={{0,4},{1,5},{2,3},{3,2},{4,0},{5,1},{6,7},{7,6},{8,12},{9,13},{10,... | collective-permute-start | bytes 835592 | tf_op jit(solution)/shard_map/ppermute | solution.py:363
  45.0 9.0 %collective-permute-start.5 = (bf16[2,256,256]{2,1,0:T(8,128)(2,1)S(1)}, bf16[2,256,256]{2,1,0:T(8,128)(2,1)S(1)}, u32[]{:S(2)}, u32[]{:S(2)}) collective-permute-start(bf16[2,256,256]{2,1,0:T(8,128)(2,1)S(1)} %collective-permute-done.4.refs_3_), channel_id=1, source_target_pairs={{0,16},{1,17},{2,18},{3,19},{4,20},{5,21},{6,22},{7,23},{8,24},{9,... | collective-permute-start | bytes 786440 | tf_op jit(solution)/shard_map/ppermute | solution.py:363
  46.2 12.1 %collective-permute-start.8 = (bf16[2,256,256]{2,1,0:T(8,128)(2,1)S(1)}, bf16[2,256,256]{2,1,0:T(8,128)(2,1)S(1)}, u32[]{:S(2)}, u32[]{:S(2)}) collective-permute-start(bf16[2,256,256]{2,1,0:T(8,128)(2,1)S(1)} %shard_map.77.refs_4_), channel_id=1, source_target_pairs={{0,16},{1,17},{2,18},{3,19},{4,20},{5,21},{6,22},{7,23},{8,24},{9,... | collective-permute-start | bytes 786440 | tf_op jit(solution)/shard_map/ppermute | solution.py:363
  49.1 14.9 %collective-permute-start.11 = (bf16[2,256,256]{2,1,0:T(8,128)(2,1)S(1)}, bf16[2,256,256]{2,1,0:T(8,128)(2,1)S(1)}, u32[]{:S(2)}, u32[]{:S(2)}) collective-permute-start(bf16[2,256,256]{2,1,0:T(8,128)(2,1)S(1)} %shard_map.79.refs_5_), channel_id=1, source_target_pairs={{0,16},{1,17},{2,18},{3,19},{4,20},{5,21},{6,22},{7,23},{8,24},{9,... | collective-permute-start | bytes 786440 | tf_op jit(solution)/shard_map/ppermute | solution.py:363
  50.4 20.1 %collective-permute-start.16 = (bf16[544,256]{1,0:T(8,128)(2,1)S(1)}, bf16[544,256]{1,0:T(8,128)(2,1)S(1)}, u32[]{:S(2)}, u32[]{:S(2)}) collective-permute-start(bf16[544,256]{1,0:T(8,128)(2,1)S(1)} %shard_map.83), channel_id=1, source_target_pairs={{0,4},{1,5},{2,3},{3,2},{4,0},{5,1},{6,7},{7,6},{8,12},{9,13},{10,... | collective-permute-start | bytes 835592 | tf_op jit(solution)/shard_map/ppermute | solution.py:363
  54.0 12.5 %collective-permute-start.17 = (bf16[256,256]{1,0:T(8,128)(2,1)S(1)}, bf16[256,256]{1,0:T(8,128)(2,1)S(1)}, u32[]{:S(2)}, u32[]{:S(2)}) collective-permute-start(bf16[256,256]{1,0:T(8,128)(2,1)S(1)} %get-tuple-element.42), channel_id=1, source_target_pairs={{0,8},{1,9},{2,10},{3,11},{4,12},{5,13},{6,14},{7,15},{8,0},{9,1},... | collective-permute-start | bytes 393224 | tf_op jit(solution)/shard_map/ppermute | solution.py:363
  58.4 8.5 %collective-permute-start.19 = (bf16[256,256]{1,0:T(8,128)(2,1)S(1)}, bf16[256,256]{1,0:T(8,128)(2,1)S(1)}, u32[]{:S(2)}, u32[]{:S(2)}) collective-permute-start(bf16[256,256]{1,0:T(8,128)(2,1)S(1)} %get-tuple-element.44), channel_id=1, source_target_pairs={{0,12},{1,13},{2,14},{3,15},{4,8},{5,9},{6,10},{7,11},{8,4},{9,5},... | collective-permute-start | bytes 393224 | tf_op jit(solution)/shard_map/ppermute | solution.py:363
  64.0 4.7 %collective-permute-start.18 = (f32[256,256]{1,0:T(8,128)S(1)}, f32[256,256]{1,0:T(8,128)S(1)}, u32[]{:S(2)}, u32[]{:S(2)}) collective-permute-start(f32[256,256]{1,0:T(8,128)S(1)} %get-tuple-element.43), channel_id=1, source_target_pairs={{0,4},{1,5},{2,6},{3,7},{4,0},{5,1},{6,2},{7,3},{8,12},{9,13},{10,... | collective-permute-start | bytes 786440 | tf_op jit(solution)/shard_map/ppermute | solution.py:363
  66.4 8.2 %collective-permute-start.13 = (f32[256,256]{1,0:T(8,128)S(1)}, f32[256,256]{1,0:T(8,128)S(1)}, u32[]{:S(2)}, u32[]{:S(2)}) collective-permute-start(f32[256,256]{1,0:T(8,128)S(1)} %get-tuple-element.36), channel_id=1, source_target_pairs={{0,4},{1,5},{2,6},{3,7},{4,0},{5,1},{6,2},{7,3},{8,12},{9,13},{10,... | collective-permute-start | bytes 786440 | tf_op jit(solution)/shard_map/ppermute | solution.py:363
  66.5 4.7 %collective-permute-start.12 = (bf16[256,256]{1,0:T(8,128)(2,1)S(1)}, bf16[256,256]{1,0:T(8,128)(2,1)S(1)}, u32[]{:S(2)}, u32[]{:S(2)}) collective-permute-start(bf16[256,256]{1,0:T(8,128)(2,1)S(1)} %get-tuple-element.35), channel_id=1, source_target_pairs={{0,8},{1,9},{2,10},{3,11},{4,12},{5,13},{6,14},{7,15},{8,0},{9,1},... | collective-permute-start | bytes 393224 | tf_op jit(solution)/shard_map/ppermute | solution.py:363
  66.9 7.8 %collective-permute-start.14 = (bf16[256,256]{1,0:T(8,128)(2,1)S(1)}, bf16[256,256]{1,0:T(8,128)(2,1)S(1)}, u32[]{:S(2)}, u32[]{:S(2)}) collective-permute-start(bf16[256,256]{1,0:T(8,128)(2,1)S(1)} %get-tuple-element.37), channel_id=1, source_target_pairs={{0,12},{1,13},{2,14},{3,15},{4,8},{5,9},{6,10},{7,11},{8,4},{9,5},... | collective-permute-start | bytes 393224 | tf_op jit(solution)/shard_map/ppermute | solution.py:363
  (3 other events, 12.5 us)

commit v5 on v4

--- a/solution.py
+++ b/solution.py
@@ -250,97 +250,110 @@
         out[...] = jnp.dot(token[...], whole[...], preferred_element_type=f32)
 
 
-def read_kernel(heads, ng, nx, hops, phase, *refs):
-    partials = [refs[j * nx : (j + 1) * nx] for j in range(CORES)]
-    k_ref, v_ref, gate_ref, forget_ref, reset_ref = refs[CORES * nx : CORES * nx + 5]
-    at = CORES * nx + 5
-    done = phase if phase == ng - 1 else 0
-    states, earlier = refs[at : at + hops], refs[at + hops : at + hops + done]
-    out_ref, state, sem = refs[at + hops + done :]
-    length = k_ref.shape[0]
-    size, vsize = k_ref.shape[1] // heads, v_ref.shape[1] // heads
-    factor = size ** (-0.5)
-    stride = size + EXTRA
-    group, dp, place = (lax.axis_index(a) for a in AXES)
-    core = lax.rem(dp, CORES)
-
-    def slot_of(j):
-        return lax.rem(core + j, CORES)
-
-    def head_of(j, r):
-        return slot_of(j) * ng + lax.rem(group + r, ng)
-
-    for h in range(hops):
-
-        @pl.when(place == h + 1)
-        def _():
-            pltpu.make_async_copy(states[h], state, sem).start()
-
-    @pl.when(place == 0)
-    def _():
-        state[...] = jnp.zeros_like(state)
-
+def head_of(j, r, ng):
+    slot = lax.rem(lax.rem(lax.axis_index("dp"), CORES) + j, CORES)
+    return slot * ng + lax.rem(lax.axis_index("groups") + r, ng)
+
+
+def decay_kernel(ng, gate_ref, forget_ref, reset_ref, *outs):
+    length = reset_ref.shape[1]
     t_at = lax.broadcasted_iota(jnp.int32, (length, length), 0)
     s_at = lax.broadcasted_iota(jnp.int32, (length, length), 1)
-    forget = [log_sigmoid(forget_ref[pl.ds(head_of(j, phase), 1), :]) for j in range(CORES)]
+    pairs = [(j, r) for r in range(ng) for j in range(CORES)]
+    forget = [log_sigmoid(forget_ref[pl.ds(head_of(j, r, ng), 1), :]) for j, r in pairs]
     running = lane_scan(padded(jnp.concatenate([reset_ref[...].astype(f32)] + forget, axis=0)))
     running_rows = running.T
     count, count_rows = running[0:1], running_rows[:, 0:1]
     linked = jnp.logical_and(count_rows == count, t_at >= s_at)
-    exponents = []
+    for at, (j, r) in enumerate(pairs):
+        decay_ref, column_ref = outs[2 * r], outs[2 * r + 1]
+        cum_t = running_rows[:, 1 + at : 2 + at]
+        exponent = jnp.where(
+            linked,
+            cum_t - running[1 + at : 2 + at] + gate_ref[pl.ds(head_of(j, r, ng), 1), :],
+            very_low,
+        )
+        top = jnp.max(exponent, axis=1, keepdims=True)
+        decay_ref[j] = jnp.exp(exponent - top)
+        lane = lax.broadcasted_iota(jnp.int32, (length, 128), 1)
+        columns = jnp.where(lane == 0, top, jnp.where(lane == 1, cum_t, count_rows))
+        column_ref[j] = columns
+
+
+def read_kernel(heads, ng, nx, hops, phase, *refs):
+    partials = [refs[j * nx : (j + 1) * nx] for j in range(CORES)]
+    k_ref, v_ref, decay_ref, column_ref = refs[CORES * nx : CORES * nx + 4]
+    at = CORES * nx + 4
+    states = refs[at : at + hops]
+    out_ref, state, result, sem, out_sems = refs[at + hops + (1 if phase else 0) :]
+    size, vsize = k_ref.shape[1] // heads, v_ref.shape[1] // heads
+    factor = size ** (-0.5)
+    stride = size + EXTRA
+    place = lax.axis_index("ctx")
+    core = lax.rem(lax.axis_index("dp"), CORES)
+    for h in range(hops):
+
+        @pl.when(place == h + 1)
+        def _():
+            pltpu.make_async_copy(states[h], state, sem).start()
+
+    @pl.when(place == 0)
+    def _():
+        state[...] = jnp.zeros_like(state)
+
+    queries, scores = [], []
     for j in range(CORES):
-        exponents.append(
-            jnp.where(
-                linked,
-                running_rows[:, 1 + j : 2 + j]
-                - running[1 + j : 2 + j]
-                + gate_ref[pl.ds(head_of(j, phase), 1), :],
-                very_low,
-            )
-        )
-
-    @pl.when(place > 0)
-    def _():
-        pltpu.make_async_copy(states[0], state, sem).wait()
-
-    for j in range(CORES):
+        head = head_of(j, phase, ng)
         total = partials[j][0][...]
         for other in partials[j][1:]:
             total = total + other[...].astype(f32)
         query = total.astype(bf16)
-        head = head_of(j, phase)
         keys = k_ref[:, pl.ds(pl.multiple_of(head * size, size), size)]
-        values = v_ref[:, pl.ds(pl.multiple_of(head * vsize, vsize), vsize)]
-        base = pl.multiple_of(slot_of(j) * stride, EXTRA)
+        queries.append(query)
+        scores.append(
+            lax.dot_general(query, keys, (((1,), (1,)), ((), ())), preferred_element_type=f32)
+        )
+
+    @pl.when(place > 0)
+    def _():
+        pltpu.make_async_copy(states[0], state, sem).wait()
+
+    copies = []
+    for j in range(CORES):
+        head = head_of(j, phase, ng)
+        query = queries[j]
+        column = pl.multiple_of(head * vsize, vsize)
+        values = v_ref[:, pl.ds(column, vsize)]
+        base = pl.multiple_of(lax.rem(core + j, CORES) * stride, EXTRA)
         memory = state[pl.ds(base, size), :]
         extra = state[pl.ds(pl.multiple_of(base + size, EXTRA), EXTRA), :].astype(f32)
         normer = (extra[0:1] + extra[1:2] + extra[2:3]).astype(bf16).astype(f32)
         top = extra[3:4, 0:1] + extra[4:5, 0:1] + extra[5:6, 0:1]
         top = jnp.where(place == 0, very_low, top)
-        exponent = exponents[j]
-        carried = jnp.where(count_rows == 0.0, running_rows[:, 1 + j : 2 + j] + top, very_low)
-        row_max = jnp.maximum(jnp.max(exponent, axis=1, keepdims=True), carried)
-        scores = lax.dot_general(
-            query, keys, (((1,), (1,)), ((), ())), preferred_element_type=f32
-        )
-        weighted = (jnp.exp(exponent - row_max) * (scores * factor)).astype(bf16)
+        columns = column_ref[j]
+        block_max, cum_t, count_rows = columns[:, 0:1], columns[:, 1:2], columns[:, 2:3]
+        carried = jnp.where(count_rows == 0.0, cum_t + top, very_low)
+        row_max = jnp.maximum(block_max, carried)
+        weighted = (decay_ref[j] * (scores[j] * factor)).astype(bf16)
+        within = jnp.exp(block_max - row_max)
         scale = jnp.exp(carried - row_max) * factor
         cross = jnp.dot(query, memory, preferred_element_type=f32)
         inter = jnp.sum(query.astype(f32) * normer, axis=1, keepdims=True)
-        numerator = jnp.dot(weighted, values, preferred_element_type=f32) + scale * cross
-        denominator = jnp.sum(weighted.astype(f32), axis=1, keepdims=True) + scale * inter
+        numerator = (
+            within * jnp.dot(weighted, values, preferred_element_type=f32) + scale * cross
+        )
+        denominator = (
+            within * jnp.sum(weighted.astype(f32), axis=1, keepdims=True) + scale * inter
+        )
         floor = jnp.exp(jnp.maximum(-row_max, 0.0))
-        hidden = (numerator / jnp.maximum(jnp.abs(denominator), floor)).astype(bf16)
-        if phase < ng - 1:
-            out_ref[:, j * vsize : (j + 1) * vsize] = hidden
-        else:
-            target = pl.multiple_of(head_of(j, phase) * vsize, vsize)
-            out_ref[:, pl.ds(target, vsize)] = hidden
-    if phase == ng - 1:
-        for r in range(phase):
-            for j in range(CORES):
-                target = pl.multiple_of(head_of(j, r) * vsize, vsize)
-                out_ref[:, pl.ds(target, vsize)] = earlier[r][:, j * vsize : (j + 1) * vsize]
+        result[j] = (numerator / jnp.maximum(jnp.abs(denominator), floor)).astype(bf16)
+        copy = pltpu.make_async_copy(
+            result.at[j], out_ref.at[:, pl.ds(column, vsize)], out_sems.at[j]
+        )
+        copy.start()
+        copies.append(copy)
+    for copy in copies:
+        copy.wait()
 
 
 VMEM = pl.BlockSpec(memory_space=pltpu.VMEM)
@@ -492,7 +505,18 @@
             pieces[0].append(gathered[s])
             for r in range(1, ng):
                 pieces[r].append(send(gathered[s], lambda g, x, k, z: ((g - r) % ng, x, k, z)))
-        results = []
+        decays = call(
+            functools.partial(decay_kernel, ng),
+            gate, forget, resets,
+            out_shape=(
+                jax.ShapeDtypeStruct((CORES, length, length), f32),
+                jax.ShapeDtypeStruct((CORES, length, 128), f32),
+            )
+            * ng,
+            in_specs=[VMEM] * 3,
+            out_specs=(VMEM,) * (2 * ng),
+        )
+        hidden = None
         for r in range(ng):
             piece = jax.ShapeDtypeStruct((length, width), f32)
             small = jax.ShapeDtypeStruct((length, width), bf16)
@@ -520,25 +544,22 @@
                             sums[CORES * rel + j], lambda g, x, k, z: (g, (x - rel) % nx, k ^ j, z)
                         )
                     )
-            last = r == ng - 1
-            results.append(
-                call(
-                    functools.partial(read_kernel, heads, ng, nx, nz - 1, r),
-                    *partials[0], *partials[1], keys, values, gate, forget, resets,
-                    *states[r], *(results if last else []),
-                    out_shape=jax.ShapeDtypeStruct(
-                        (length, vwidth if last else CORES * vsize), bf16
-                    ),
-                    in_specs=[VMEM] * (CORES * nx + 5)
-                    + [ANY] * (nz - 1) + [VMEM] * (r if last else 0),
-                    out_specs=VMEM,
-                    scratch_shapes=[
-                        pltpu.VMEM(message.shape, bf16),
-                        pltpu.SemaphoreType.DMA(()),
-                    ],
-                )
-            )
-        hidden = results[-1]
+            count = CORES * nx + 4 + nz - 1
+            hidden = call(
+                functools.partial(read_kernel, heads, ng, nx, nz - 1, r),
+                *partials[0], *partials[1], keys, values, *decays[2 * r : 2 * r + 2],
+                *states[r], *([hidden] if r else []),
+                out_shape=jax.ShapeDtypeStruct((length, vwidth), bf16),
+                in_specs=[VMEM] * (CORES * nx + 4) + [ANY] * (nz - 1 + (1 if r else 0)),
+                out_specs=ANY,
+                input_output_aliases={count: 0} if r else {},
+                scratch_shapes=[
+                    pltpu.VMEM(message.shape, bf16),
+                    pltpu.VMEM((CORES, length, vsize), bf16),
+                    pltpu.SemaphoreType.DMA(()),
+                    pltpu.SemaphoreType.DMA((CORES,)),
+                ],
+            )
         return hidden[None]
 
     return body

time: 77.5 us -> 78 us (level)
  the two profiles are of different devices: /device:TPU:11 before, /device:TPU:0 now
where the time goes in v5:
time: 78 us; the launch traced here: 76.6 us
  waiting for transfers between devices  47.6 us (61%)
  starting transfers between devices  16.3 us (21%)
  Pallas kernels  12.5 us (16%)
    ppermute x22, waiting for transfers between devices, send(): return lax.ppermute(value, AXES, moves(mesh, where))  47.6 us
    ppermute x22, starting transfers between devices, send(): return lax.ppermute(value, AXES, moves(mesh, where))  16.3 us
    pallas_call x18, Pallas kernels, call(): return pl.pallas_call(kernel, compiler_params=params, **options)(*args)  12.5 us
  transfers between devices with their start and end apart: 22, of which 10 were waited for; matrix products, arithmetic and copies ran while one was open for 0% of the time, Pallas kernels for 12%

profile of v5, /device:TPU:0, one launch (start us, length us, event | category | flops | bytes accessed | tf_op | source)
XLA Modules:
  0.0 76.6 jit_solution(11288024105000227495)
XLA Ops:
  0.0 1.6 %shard_map.74 = (bf16[256,512]{1,0:T(8,128)(2,1)S(1)}, bf16[256,256]{1,0:T(8,128)(2,1)S(1)}, bf16[256,256]{1,0:T(8,128)(2,1)S(1)}, bf16[256,2048]{1,0:T(8,128)(2,1)S(1)}) custom-call(bf16[256,4096]{1,0:T(8,128)(2,1)} %bitcast.16, bf16[256,1024]{1,0:T(8,128)(2,1)} %w_ref.1), custom_call_target="tpu_custom_call" | custom-call | tf_op jit(solution)/shard_map/pallas_call | solution.py:383
  1.6 3.0 %collective-permute-start.1 = (bf16[256,2048]{1,0:T(8,128)(2,1)S(1)}, bf16[256,2048]{1,0:T(8,128)(2,1)S(1)}, u32[]{:S(2)}, u32[]{:S(2)}) collective-permute-start(bf16[256,2048]{1,0:T(8,128)(2,1)S(1)} %get-tuple-element.31), channel_id=1, source_target_pairs={{0,8},{1,9},{2,10},{3,11},{4,12},{5,13},{6,14},{7,15},{8,0},{9,1},... | collective-permute-start | bytes 3145736 | tf_op jit(solution)/shard_map/ppermute | solution.py:376
  4.6 1.5 %collective-permute-done.3.swapped_ref.refs_3_ = bf16[256,512]{1,0:T(8,128)(2,1)S(1)} collective-permute-done((bf16[256,512]{1,0:T(8,128)(2,1)S(1)}, bf16[256,512]{1,0:T(8,128)(2,1)S(1)}, u32[]{:S(2)}, u32[]{:S(2)}) %collective-permute-start.3) | collective-permute-done | bytes 262176 | tf_op jit(solution)/shard_map/ppermute | solution.py:376
  6.2 1.6 %collective-permute-start.4 = (bf16[2,256,256]{2,1,0:T(8,128)(2,1)S(1)}, bf16[2,256,256]{2,1,0:T(8,128)(2,1)S(1)}, u32[]{:S(2)}, u32[]{:S(2)}) collective-permute-start(bf16[2,256,256]{2,1,0:T(8,128)(2,1)S(1)} %shard_map.75.refs_2_), channel_id=1, source_target_pairs={{0,1},{1,0},{2,3},{3,2},{4,5},{5,4},{6,7},{7,6},{8,9},{9,8},{10,11... | collective-permute-start | bytes 786440 | tf_op jit(solution)/shard_map/ppermute | solution.py:376
  7.9 2.6 %shard_map.73 = (bf16[256,2048]{1,0:T(8,128)(2,1)S(1)}, f32[512,256]{1,0:T(8,128)S(1)}, bf16[544,256]{1,0:T(8,128)(2,1)S(1)}, f32[16,256]{1,0:T(8,128)S(1)}, f32...) custom-call(bf16[256,1024]{1,0:T(8,128)(2,1)S(1)} %bitcast.6, ...), custom_call_target="tpu_custom_call" | custom-call | tf_op jit(solution)/shard_map/pallas_call | solution.py:383
  11.1 3.5 %collective-permute-done.4.refs_3_ = bf16[2,256,256]{2,1,0:T(8,128)(2,1)S(1)} collective-permute-done((bf16[2,256,256]{2,1,0:T(8,128)(2,1)S(1)}, bf16[2,256,256]{2,1,0:T(8,128)(2,1)S(1)}, u32[]{:S(2)}, u32[]{:S(2)}) %collective-permute-start.4) | collective-permute-done | bytes 262176 | tf_op jit(solution)/shard_map/ppermute | solution.py:376
  14.6 13.2 %collective-permute-done.1.refs_0_ = bf16[256,2048]{1,0:T(8,128)(2,1)S(1)} collective-permute-done((bf16[256,2048]{1,0:T(8,128)(2,1)S(1)}, bf16[256,2048]{1,0:T(8,128)(2,1)S(1)}, u32[]{:S(2)}, u32[]{:S(2)}) %collective-permute-start.1) | collective-permute-done | bytes 1048608 | tf_op jit(solution)/shard_map/ppermute | solution.py:376
  27.8 1.9 %collective-permute-start.7 = (bf16[544,256]{1,0:T(8,128)(2,1)S(1)}, bf16[544,256]{1,0:T(8,128)(2,1)S(1)}, u32[]{:S(2)}, u32[]{:S(2)}) collective-permute-start(bf16[544,256]{1,0:T(8,128)(2,1)S(1)} %shard_map.76), channel_id=1, source_target_pairs={{0,1},{1,0},{2,3},{3,2},{4,5},{5,4},{6,7},{7,6},{8,9},{9,8},{10,11... | collective-permute-start | bytes 835592 | tf_op jit(solution)/shard_map/ppermute | solution.py:376
  30.0 7.4 %collective-permute-done.7.outer_ref.prev_ref.refs_8_ = bf16[544,256]{1,0:T(8,128)(2,1)S(1)} collective-permute-done((bf16[544,256]{1,0:T(8,128)(2,1)S(1)}, bf16[544,256]{1,0:T(8,128)(2,1)S(1)}, u32[]{:S(2)}, u32[]{:S(2)}) %collective-permute-start.7) | collective-permute-done | bytes 278560 | tf_op jit(solution)/shard_map/ppermute | solution.py:376
  37.5 5.5 %collective-permute-done.10.outer_ref.prev_ref.refs_8_ = bf16[544,256]{1,0:T(8,128)(2,1)S(1)} collective-permute-done((bf16[544,256]{1,0:T(8,128)(2,1)S(1)}, bf16[544,256]{1,0:T(8,128)(2,1)S(1)}, u32[]{:S(2)}, u32[]{:S(2)}) %collective-permute-start.10) | collective-permute-done | bytes 278560 | tf_op jit(solution)/shard_map/ppermute | solution.py:376
  43.7 1.7 %collective-permute-start.5 = (bf16[2,256,256]{2,1,0:T(8,128)(2,1)S(1)}, bf16[2,256,256]{2,1,0:T(8,128)(2,1)S(1)}, u32[]{:S(2)}, u32[]{:S(2)}) collective-permute-start(bf16[2,256,256]{2,1,0:T(8,128)(2,1)S(1)} %collective-permute-done.4.refs_3_), channel_id=1, source_target_pairs={{0,16},{1,17},{2,18},{3,19},{4,20},{5,21},{6,22},{7,23},{8,24},{9,... | collective-permute-start | bytes 786440 | tf_op jit(solution)/shard_map/ppermute | solution.py:376
  45.9 1.8 %collective-permute-start.11 = (bf16[2,256,256]{2,1,0:T(8,128)(2,1)S(1)}, bf16[2,256,256]{2,1,0:T(8,128)(2,1)S(1)}, u32[]{:S(2)}, u32[]{:S(2)}) collective-permute-start(bf16[2,256,256]{2,1,0:T(8,128)(2,1)S(1)} %shard_map.79.refs_5_), channel_id=1, source_target_pairs={{0,16},{1,17},{2,18},{3,19},{4,20},{5,21},{6,22},{7,23},{8,24},{9,... | collective-permute-start | bytes 786440 | tf_op jit(solution)/shard_map/ppermute | solution.py:376
  47.7 0.8 %shard_map.85 = (bf16[256,256]{1,0:T(8,128)(2,1)S(1)}, bf16[256,256]{1,0:T(8,128)(2,1)S(1)}, bf16[2048,256]{1,0:T(8,128)(2,1)S(1)}) custom-call(bf16[256,2048]{1,0:T(8,128)(2,1)S(1)} %collective-permute-done.1.refs_0_, bf16[256,2048]{1,0:T(8,128)(2,1)S(1)} %collective-permute-done.2.refs_1_, bf16[2,256,256]{2,1,0:T(8,128)(2,1)S(1)} %shard_map.75.refs_2_, ...), custom_call_target="tpu_custom_call" | custom-call | tf_op jit(solution)/shard_map/pallas_call | solution.py:383
  49.2 3.6 %collective-permute-done.5.refs_4_ = bf16[2,256,256]{2,1,0:T(8,128)(2,1)S(1)} collective-permute-done((bf16[2,256,256]{2,1,0:T(8,128)(2,1)S(1)}, bf16[2,256,256]{2,1,0:T(8,128)(2,1)S(1)}, u32[]{:S(2)}, u32[]{:S(2)}) %collective-permute-start.5) | collective-permute-done | bytes 262176 | tf_op jit(solution)/shard_map/ppermute | solution.py:376
  52.9 5.6 %collective-permute-done.8.refs_5_ = bf16[2,256,256]{2,1,0:T(8,128)(2,1)S(1)} collective-permute-done((bf16[2,256,256]{2,1,0:T(8,128)(2,1)S(1)}, bf16[2,256,256]{2,1,0:T(8,128)(2,1)S(1)}, u32[]{:S(2)}, u32[]{:S(2)}) %collective-permute-start.8) | collective-permute-done | bytes 262176 | tf_op jit(solution)/shard_map/ppermute | solution.py:376
  58.5 1.7 %collective-permute-start.17 = (bf16[256,256]{1,0:T(8,128)(2,1)S(1)}, bf16[256,256]{1,0:T(8,128)(2,1)S(1)}, u32[]{:S(2)}, u32[]{:S(2)}) collective-permute-start(bf16[256,256]{1,0:T(8,128)(2,1)S(1)} %get-tuple-element.48), channel_id=1, source_target_pairs={{0,8},{1,9},{2,10},{3,11},{4,12},{5,13},{6,14},{7,15},{8,0},{9,1},... | collective-permute-start | bytes 393224 | tf_op jit(solution)/shard_map/ppermute | solution.py:376
  60.2 3.1 %collective-permute-done.11.refs_6_ = bf16[2,256,256]{2,1,0:T(8,128)(2,1)S(1)} collective-permute-done((bf16[2,256,256]{2,1,0:T(8,128)(2,1)S(1)}, bf16[2,256,256]{2,1,0:T(8,128)(2,1)S(1)}, u32[]{:S(2)}, u32[]{:S(2)}) %collective-permute-start.11) | collective-permute-done | bytes 262176 | tf_op jit(solution)/shard_map/ppermute | solution.py:376
  63.7 0.8 %shard_map.80 = (bf16[256,256]{1,0:T(8,128)(2,1)S(1)}, bf16[256,256]{1,0:T(8,128)(2,1)S(1)}, bf16[2048,256]{1,0:T(8,128)(2,1)S(1)}) custom-call(bf16[256,2048]{1,0:T(8,128)(2,1)S(1)} %collective-permute-done.1.refs_0_, bf16[256,2048]{1,0:T(8,128)(2,1)S(1)} %collective-permute-done.2.refs_1_, bf16[256,256]{1,0:T(8,128)(2,1)S(1)} %get-tuple-element.32.refs_2_, ...), custom_call_target="tpu_custom_call" | custom-call | tf_op jit(solution)/shard_map/pallas_call | solution.py:383
  65.2 1.4 %collective-permute-start.13 = (f32[256,256]{1,0:T(8,128)S(1)}, f32[256,256]{1,0:T(8,128)S(1)}, u32[]{:S(2)}, u32[]{:S(2)}) collective-permute-start(f32[256,256]{1,0:T(8,128)S(1)} %get-tuple-element.40), channel_id=1, source_target_pairs={{0,4},{1,5},{2,6},{3,7},{4,0},{5,1},{6,2},{7,3},{8,12},{9,13},{10,... | collective-permute-start | bytes 786440 | tf_op jit(solution)/shard_map/ppermute | solution.py:376
  67.0 1.9 %collective-permute-done.19.refs_3_ = bf16[256,256]{1,0:T(8,128)(2,1)S(1)} collective-permute-done((bf16[256,256]{1,0:T(8,128)(2,1)S(1)}, bf16[256,256]{1,0:T(8,128)(2,1)S(1)}, u32[]{:S(2)}, u32[]{:S(2)}) %collective-permute-start.19) | collective-permute-done | bytes 131104 | tf_op jit(solution)/shard_map/ppermute | solution.py:376
  69.2 1.1 %shard_map.82 = (f32[2,256,256]{2,1,0:T(8,128)S(1)}, f32[2,256,128]{2,1,0:T(8,128)S(1)}, f32[2,256,256]{2,1,0:T(8,128)S(1)}, f32[2,256,128]{2,1,0:T(8,128)S(1)}) custom-call(f32[4,256]{1,0:T(4,128)S(1)} %bitcast.13, f32[4,256]{1,0:T(4,128)S(1)} %bitcast.15, s32[1,256]{1,0:T(1,128)S(1)} %copy-done.4), custom_call_target="tpu_custom_call" | custom-call | tf_op jit(solution)/shard_map/pallas_call | solution.py:383
  70.3 2.0 %shard_map.89.refs_11_ = bf16[256,1024]{1,0:T(8,128)(2,1)} custom-call(f32[256,256]{1,0:T(8,128)S(1)} %get-tuple-element.47.refs_0_, bf16[256,256]{1,0:T(8,128)(2,1)S(1)} %collective-permute-done.17.refs_1_, f32[256,256]{1,0:T(8,128)S(1)} %collective-permute-done.18.refs_2_, bf16[256,256]{1,0:T(8,128)(2,1)S(1)} %collective-permute-done.19.refs_3_, ...), custom_call_target="tpu_custom_call" | custom-call | tf_op jit(solution)/shard_map/pallas_call | solution.py:383
  72.4 2.2 %collective-permute-done.14.refs_3_ = bf16[256,256]{1,0:T(8,128)(2,1)S(1)} collective-permute-done((bf16[256,256]{1,0:T(8,128)(2,1)S(1)}, bf16[256,256]{1,0:T(8,128)(2,1)S(1)}, u32[]{:S(2)}, u32[]{:S(2)}) %collective-permute-start.14) | collective-permute-done | bytes 131104 | tf_op jit(solution)/shard_map/ppermute | solution.py:376
  74.6 2.0 %shard_map.90 = bf16[256,1024]{1,0:T(8,128)(2,1)} custom-call(f32[256,256]{1,0:T(8,128)S(1)} %get-tuple-element.38.refs_0_, bf16[256,256]{1,0:T(8,128)(2,1)S(1)} %collective-permute-done.12.refs_1_, f32[256,256]{1,0:T(8,128)S(1)} %collective-permute-done.13.refs_2_, ...), custom_call_target="tpu_custom_call", output_to_operand_aliasing={{}: (11, {})} | custom-call | tf_op jit(solution)/shard_map/pallas_call | solution.py:383
  (48 shorter events, 4.9 us)
Async XLA Ops:
  0.0 7.8 %copy-start.3 = (f32[1,4,256]{2,1,0:T(4,128)S(1)}, f32[1,4,256]{2,1,0:T(4,128)}, u32[]{:S(2)}) copy-start(f32[1,4,256]{2,1,0:T(4,128)} %param.12) | copy-start | bytes 12292
  0.0 7.8 %copy-start.4 = (s32[1,256]{1,0:T(1,128)S(1)}, s32[1,256]{1,0:T(1,128)}, u32[]{:S(2)}) copy-start(s32[1,256]{1,0:T(1,128)} %reset_ref.1) | copy-start | bytes 3076
  1.6 26.2 %collective-permute-start.1 = (bf16[256,2048]{1,0:T(8,128)(2,1)S(1)}, bf16[256,2048]{1,0:T(8,128)(2,1)S(1)}, u32[]{:S(2)}, u32[]{:S(2)}) collective-permute-start(bf16[256,2048]{1,0:T(8,128)(2,1)S(1)} %get-tuple-element.31), channel_id=1, source_target_pairs={{0,8},{1,9},{2,10},{3,11},{4,12},{5,13},{6,14},{7,15},{8,0},{9,1},... | collective-permute-start | bytes 3145736 | tf_op jit(solution)/shard_map/ppermute | solution.py:376
  4.6 1.5 %collective-permute-start.3 = (bf16[256,512]{1,0:T(8,128)(2,1)S(1)}, bf16[256,512]{1,0:T(8,128)(2,1)S(1)}, u32[]{:S(2)}, u32[]{:S(2)}) collective-permute-start(bf16[256,512]{1,0:T(8,128)(2,1)S(1)} %get-tuple-element.33), channel_id=1, source_target_pairs={{0,4},{1,5},{2,6},{3,7},{4,0},{5,1},{6,2},{7,3},{8,12},{9,13},{10,... | collective-permute-start | bytes 786440 | tf_op jit(solution)/shard_map/ppermute | solution.py:376
  6.2 8.4 %collective-permute-start.4 = (bf16[2,256,256]{2,1,0:T(8,128)(2,1)S(1)}, bf16[2,256,256]{2,1,0:T(8,128)(2,1)S(1)}, u32[]{:S(2)}, u32[]{:S(2)}) collective-permute-start(bf16[2,256,256]{2,1,0:T(8,128)(2,1)S(1)} %shard_map.75.refs_2_), channel_id=1, source_target_pairs={{0,1},{1,0},{2,3},{3,2},{4,5},{5,4},{6,7},{7,6},{8,9},{9,8},{10,11... | collective-permute-start | bytes 786440 | tf_op jit(solution)/shard_map/ppermute | solution.py:376
  10.5 34.9 %collective-permute-start = (bf16[256,2048]{1,0:T(8,128)(2,1)S(1)}, bf16[256,2048]{1,0:T(8,128)(2,1)S(1)}, u32[]{:S(2)}, u32[]{:S(2)}) collective-permute-start(bf16[256,2048]{1,0:T(8,128)(2,1)S(1)} %get-tuple-element.30.refs_0_), channel_id=1, source_target_pairs={{0,4},{1,5},{2,6},{3,7},{4,0},{5,1},{6,2},{7,3},{8,12},{9,13},{10,... | collective-permute-start | bytes 3145736 | tf_op jit(solution)/shard_map/ppermute | solution.py:376
  10.6 17.2 %collective-permute-start.6 = (bf16[2,256,256]{2,1,0:T(8,128)(2,1)S(1)}, bf16[2,256,256]{2,1,0:T(8,128)(2,1)S(1)}, u32[]{:S(2)}, u32[]{:S(2)}) collective-permute-start(bf16[2,256,256]{2,1,0:T(8,128)(2,1)S(1)} %shard_map.75.refs_2_), channel_id=1, source_target_pairs={{0,4},{1,2},{2,1},{3,7},{4,0},{5,6},{6,5},{7,3},{8,12},{9,10},{10,... | collective-permute-start | bytes 786440 | tf_op jit(solution)/shard_map/ppermute | solution.py:376
  14.6 15.1 %collective-permute-start.9 = (bf16[2,256,256]{2,1,0:T(8,128)(2,1)S(1)}, bf16[2,256,256]{2,1,0:T(8,128)(2,1)S(1)}, u32[]{:S(2)}, u32[]{:S(2)}) collective-permute-start(bf16[2,256,256]{2,1,0:T(8,128)(2,1)S(1)} %collective-permute-done.4.refs_3_), channel_id=1, source_target_pairs={{0,4},{1,2},{2,1},{3,7},{4,0},{5,6},{6,5},{7,3},{8,12},{9,10},{10,... | collective-permute-start | bytes 786440 | tf_op jit(solution)/shard_map/ppermute | solution.py:376
  27.8 19.8 %collective-permute-start.2 = (bf16[256,2048]{1,0:T(8,128)(2,1)S(1)}, bf16[256,2048]{1,0:T(8,128)(2,1)S(1)}, u32[]{:S(2)}, u32[]{:S(2)}) collective-permute-start(bf16[256,2048]{1,0:T(8,128)(2,1)S(1)} %collective-permute-done.1.refs_0_), channel_id=1, source_target_pairs={{0,4},{1,5},{2,6},{3,7},{4,0},{5,1},{6,2},{7,3},{8,12},{9,13},{10,... | collective-permute-start | bytes 3145736 | tf_op jit(solution)/shard_map/ppermute | solution.py:376
  27.8 9.6 %collective-permute-start.7 = (bf16[544,256]{1,0:T(8,128)(2,1)S(1)}, bf16[544,256]{1,0:T(8,128)(2,1)S(1)}, u32[]{:S(2)}, u32[]{:S(2)}) collective-permute-start(bf16[544,256]{1,0:T(8,128)(2,1)S(1)} %shard_map.76), channel_id=1, source_target_pairs={{0,1},{1,0},{2,3},{3,2},{4,5},{5,4},{6,7},{7,6},{8,9},{9,8},{10,11... | collective-permute-start | bytes 835592 | tf_op jit(solution)/shard_map/ppermute | solution.py:376
  29.7 13.3 %collective-permute-start.10 = (bf16[544,256]{1,0:T(8,128)(2,1)S(1)}, bf16[544,256]{1,0:T(8,128)(2,1)S(1)}, u32[]{:S(2)}, u32[]{:S(2)}) collective-permute-start(bf16[544,256]{1,0:T(8,128)(2,1)S(1)} %shard_map.78), channel_id=1, source_target_pairs={{0,1},{1,0},{2,3},{3,2},{4,5},{5,4},{6,7},{7,6},{8,9},{9,8},{10,11... | collective-permute-start | bytes 835592 | tf_op jit(solution)/shard_map/ppermute | solution.py:376
  37.4 5.7 %collective-permute-start.20 = (bf16[544,256]{1,0:T(8,128)(2,1)S(1)}, bf16[544,256]{1,0:T(8,128)(2,1)S(1)}, u32[]{:S(2)}, u32[]{:S(2)}) collective-permute-start(bf16[544,256]{1,0:T(8,128)(2,1)S(1)} %shard_map.87), channel_id=1, source_target_pairs={{0,4},{1,2},{2,1},{3,7},{4,0},{5,6},{6,5},{7,3},{8,12},{9,10},{10,... | collective-permute-start | bytes 835592 | tf_op jit(solution)/shard_map/ppermute | solution.py:376
  43.0 2.8 %collective-permute-start.15 = (bf16[544,256]{1,0:T(8,128)(2,1)S(1)}, bf16[544,256]{1,0:T(8,128)(2,1)S(1)}, u32[]{:S(2)}, u32[]{:S(2)}) collective-permute-start(bf16[544,256]{1,0:T(8,128)(2,1)S(1)} %shard_map.83), channel_id=1, source_target_pairs={{0,4},{1,2},{2,1},{3,7},{4,0},{5,6},{6,5},{7,3},{8,12},{9,10},{10,... | collective-permute-start | bytes 835592 | tf_op jit(solution)/shard_map/ppermute | solution.py:376
  43.2 22.1 %collective-permute-start.21 = (bf16[544,256]{1,0:T(8,128)(2,1)S(1)}, bf16[544,256]{1,0:T(8,128)(2,1)S(1)}, u32[]{:S(2)}, u32[]{:S(2)}) collective-permute-start(bf16[544,256]{1,0:T(8,128)(2,1)S(1)} %shard_map.88), channel_id=1, source_target_pairs={{0,4},{1,5},{2,3},{3,2},{4,0},{5,1},{6,7},{7,6},{8,12},{9,13},{10,... | collective-permute-start | bytes 835592 | tf_op jit(solution)/shard_map/ppermute | solution.py:376
  43.7 9.2 %collective-permute-start.5 = (bf16[2,256,256]{2,1,0:T(8,128)(2,1)S(1)}, bf16[2,256,256]{2,1,0:T(8,128)(2,1)S(1)}, u32[]{:S(2)}, u32[]{:S(2)}) collective-permute-start(bf16[2,256,256]{2,1,0:T(8,128)(2,1)S(1)} %collective-permute-done.4.refs_3_), channel_id=1, source_target_pairs={{0,16},{1,17},{2,18},{3,19},{4,20},{5,21},{6,22},{7,23},{8,24},{9,... | collective-permute-start | bytes 786440 | tf_op jit(solution)/shard_map/ppermute | solution.py:376
  45.4 13.1 %collective-permute-start.8 = (bf16[2,256,256]{2,1,0:T(8,128)(2,1)S(1)}, bf16[2,256,256]{2,1,0:T(8,128)(2,1)S(1)}, u32[]{:S(2)}, u32[]{:S(2)}) collective-permute-start(bf16[2,256,256]{2,1,0:T(8,128)(2,1)S(1)} %shard_map.77.refs_4_), channel_id=1, source_target_pairs={{0,16},{1,17},{2,18},{3,19},{4,20},{5,21},{6,22},{7,23},{8,24},{9,... | collective-permute-start | bytes 786440 | tf_op jit(solution)/shard_map/ppermute | solution.py:376
  45.9 17.4 %collective-permute-start.11 = (bf16[2,256,256]{2,1,0:T(8,128)(2,1)S(1)}, bf16[2,256,256]{2,1,0:T(8,128)(2,1)S(1)}, u32[]{:S(2)}, u32[]{:S(2)}) collective-permute-start(bf16[2,256,256]{2,1,0:T(8,128)(2,1)S(1)} %shard_map.79.refs_5_), channel_id=1, source_target_pairs={{0,16},{1,17},{2,18},{3,19},{4,20},{5,21},{6,22},{7,23},{8,24},{9,... | collective-permute-start | bytes 786440 | tf_op jit(solution)/shard_map/ppermute | solution.py:376
  47.6 24.7 %collective-permute-start.16 = (bf16[544,256]{1,0:T(8,128)(2,1)S(1)}, bf16[544,256]{1,0:T(8,128)(2,1)S(1)}, u32[]{:S(2)}, u32[]{:S(2)}) collective-permute-start(bf16[544,256]{1,0:T(8,128)(2,1)S(1)} %shard_map.84), channel_id=1, source_target_pairs={{0,4},{1,5},{2,3},{3,2},{4,0},{5,1},{6,7},{7,6},{8,12},{9,13},{10,... | collective-permute-start | bytes 835592 | tf_op jit(solution)/shard_map/ppermute | solution.py:376
  52.9 17.4 %collective-permute-start.18 = (f32[256,256]{1,0:T(8,128)S(1)}, f32[256,256]{1,0:T(8,128)S(1)}, u32[]{:S(2)}, u32[]{:S(2)}) collective-permute-start(f32[256,256]{1,0:T(8,128)S(1)} %get-tuple-element.49), channel_id=1, source_target_pairs={{0,4},{1,5},{2,6},{3,7},{4,0},{5,1},{6,2},{7,3},{8,12},{9,13},{10,... | collective-permute-start | bytes 786440 | tf_op jit(solution)/shard_map/ppermute | solution.py:376
  58.5 8.1 %collective-permute-start.17 = (bf16[256,256]{1,0:T(8,128)(2,1)S(1)}, bf16[256,256]{1,0:T(8,128)(2,1)S(1)}, u32[]{:S(2)}, u32[]{:S(2)}) collective-permute-start(bf16[256,256]{1,0:T(8,128)(2,1)S(1)} %get-tuple-element.48), channel_id=1, source_target_pairs={{0,8},{1,9},{2,10},{3,11},{4,12},{5,13},{6,14},{7,15},{8,0},{9,1},... | collective-permute-start | bytes 393224 | tf_op jit(solution)/shard_map/ppermute | solution.py:376
  63.2 5.6 %collective-permute-start.19 = (bf16[256,256]{1,0:T(8,128)(2,1)S(1)}, bf16[256,256]{1,0:T(8,128)(2,1)S(1)}, u32[]{:S(2)}, u32[]{:S(2)}) collective-permute-start(bf16[256,256]{1,0:T(8,128)(2,1)S(1)} %get-tuple-element.50), channel_id=1, source_target_pairs={{0,12},{1,13},{2,14},{3,15},{4,8},{5,9},{6,10},{7,11},{8,4},{9,5},... | collective-permute-start | bytes 393224 | tf_op jit(solution)/shard_map/ppermute | solution.py:376
  65.2 9.4 %collective-permute-start.13 = (f32[256,256]{1,0:T(8,128)S(1)}, f32[256,256]{1,0:T(8,128)S(1)}, u32[]{:S(2)}, u32[]{:S(2)}) collective-permute-start(f32[256,256]{1,0:T(8,128)S(1)} %get-tuple-element.40), channel_id=1, source_target_pairs={{0,4},{1,5},{2,6},{3,7},{4,0},{5,1},{6,2},{7,3},{8,12},{9,13},{10,... | collective-permute-start | bytes 786440 | tf_op jit(solution)/shard_map/ppermute | solution.py:376
  66.6 5.8 %collective-permute-start.12 = (bf16[256,256]{1,0:T(8,128)(2,1)S(1)}, bf16[256,256]{1,0:T(8,128)(2,1)S(1)}, u32[]{:S(2)}, u32[]{:S(2)}) collective-permute-start(bf16[256,256]{1,0:T(8,128)(2,1)S(1)} %get-tuple-element.39), channel_id=1, source_target_pairs={{0,8},{1,9},{2,10},{3,11},{4,12},{5,13},{6,14},{7,15},{8,0},{9,1},... | collective-permute-start | bytes 393224 | tf_op jit(solution)/shard_map/ppermute | solution.py:376
  68.8 5.8 %collective-permute-start.14 = (bf16[256,256]{1,0:T(8,128)(2,1)S(1)}, bf16[256,256]{1,0:T(8,128)(2,1)S(1)}, u32[]{:S(2)}, u32[]{:S(2)}) collective-permute-start(bf16[256,256]{1,0:T(8,128)(2,1)S(1)} %get-tuple-element.41), channel_id=1, source_target_pairs={{0,12},{1,13},{2,14},{3,15},{4,8},{5,9},{6,10},{7,11},{8,4},{9,5},... | collective-permute-start | bytes 393224 | tf_op jit(solution)/shard_map/ppermute | solution.py:376
  (3 other events, 23.5 us)

commit v6 on v5

--- a/solution.py
+++ b/solution.py
@@ -80,23 +80,31 @@
     return ref[base : base + size, :], normer, top
 
 
-def slice_kernel(ng, nx, x_ref, w_ref, send_ref, *refs):
-    own, away, sems = refs[:ng], refs[ng : ng + nx - 1], refs[ng + nx - 1]
-    group, dp = lax.axis_index("groups"), lax.axis_index("dp")
-    core, x = lax.rem(dp, CORES), lax.div(dp, CORES)
-    half, width, depth = send_ref.shape[1], own[0].shape[1], away[0].shape[1]
+def weight_kernel(ng, w_ref, send_ref, *refs):
+    own, sems = refs[:ng], refs[ng]
+    group = lax.axis_index("groups")
+    core = lax.rem(lax.axis_index("dp"), CORES)
+    half, width = send_ref.shape[1], own[0].shape[1]
+    wanted = [((1 - core) * half, send_ref)]
+    for r in range(ng):
+        wanted.append((core * half + lax.rem(group + r, ng) * width, own[r]))
+    fetch(w_ref, wanted, width, sems)
+
+
+def token_kernel(nx, x_ref, *refs):
+    away, sems = refs[: nx - 1], refs[nx - 1]
+    x = lax.div(lax.axis_index("dp"), CORES)
+    depth = away[0].shape[1]
+    wanted = [(lax.rem(x + rel, nx) * depth, away[rel - 1]) for rel in range(1, nx)]
+    fetch(x_ref, wanted, depth, sems)
+
+
+def fetch(ref, wanted, step, sems):
     copies = []
-
-    def copy(ref, column, target):
-        source = ref.at[:, pl.ds(pl.multiple_of(column, width), target.shape[1])]
-        copies.append(pltpu.make_async_copy(source, target, sems.at[len(copies)]))
+    for i, (column, target) in enumerate(wanted):
+        source = ref.at[:, pl.ds(pl.multiple_of(column, step), target.shape[1])]
+        copies.append(pltpu.make_async_copy(source, target, sems.at[i]))
         copies[-1].start()
-
-    copy(w_ref, (1 - core) * half, send_ref)
-    for r in range(ng):
-        copy(w_ref, core * half + lax.rem(group + r, ng) * width, own[r])
-    for rel in range(1, nx):
-        copy(x_ref, lax.rem(x + rel, nx) * depth, away[rel - 1])
     for each in copies:
         each.wait()
 
@@ -405,21 +413,28 @@
         rows = query_weight.shape[0]
         quarter = jax.ShapeDtypeStruct((rows, width), query_weight.dtype)
         sliced = call(
-            functools.partial(slice_kernel, ng, nx),
-            hbm_tokens, hbm_weight,
+            functools.partial(weight_kernel, ng),
+            hbm_weight,
             out_shape=(
                 jax.ShapeDtypeStruct((rows, half), query_weight.dtype),
                 *[quarter] * ng,
-                *[block] * (nx - 1),
             ),
-            in_specs=[ANY] * 2,
-            out_specs=(VMEM,) * (ng + nx),
-            scratch_shapes=[pltpu.SemaphoreType.DMA((ng + nx,))],
+            in_specs=[ANY],
+            out_specs=(VMEM,) * (1 + ng),
+            scratch_shapes=[pltpu.SemaphoreType.DMA((1 + ng,))],
+        )
+        leaving = call(
+            functools.partial(token_kernel, nx),
+            hbm_tokens,
+            out_shape=(block,) * (nx - 1),
+            in_specs=[ANY],
+            out_specs=(VMEM,) * (nx - 1),
+            scratch_shapes=[pltpu.SemaphoreType.DMA((nx - 1,))],
         )
         swapped = over_core(sliced[0])
         own_parts = sliced[1 : 1 + ng]
         arrived = [
-            send(sliced[ng + rel], lambda g, x, k, z: (g, (x + rel) % nx, k, z))
+            send(leaving[rel - 1], lambda g, x, k, z: (g, (x + rel) % nx, k, z))
             for rel in range(1, nx)
         ]
         packed = call(

time: 78 us -> 77.8 us (level)
  waiting for transfers between devices: 47.6 us -> 46.5 us
  Pallas kernels: 12.5 us -> 13.3 us
    ppermute x22, waiting for transfers between devices: 47.6 us -> 46.5 us  [send(): return lax.ppermute(value, AXES, moves(mesh, where))]
    pallas_call x18 -> x19, Pallas kernels: 12.5 us -> 13.3 us  [call(): return pl.pallas_call(kernel, compiler_params=params, **options)(*args)]
  transfers between devices with their start and end apart: 22 -> 22, of which waited for: 10 -> 10; matrix products, arithmetic and copies ran while one was open for 0% -> 0% of each run, Pallas kernels for 12% -> 13%
where the time goes in v6:
time: 77.8 us; the launch traced here: 76.4 us
  waiting for transfers between devices  46.5 us (60%)
  starting transfers between devices  16.3 us (21%)
  Pallas kernels  13.3 us (17%)
    ppermute x22, waiting for transfers between devices, send(): return lax.ppermute(value, AXES, moves(mesh, where))  46.5 us
    ppermute x22, starting transfers between devices, send(): return lax.ppermute(value, AXES, moves(mesh, where))  16.3 us
    pallas_call x19, Pallas kernels, call(): return pl.pallas_call(kernel, compiler_params=params, **options)(*args)  13.3 us
  transfers between devices with their start and end apart: 22, of which 10 were waited for; matrix products, arithmetic and copies ran while one was open for 0% of the time, Pallas kernels for 13%

profile of v6, /device:TPU:0, one launch (start us, length us, event | category | flops | bytes accessed | tf_op | source)
XLA Modules:
  0.0 76.4 jit_solution(2004823334886828037)
XLA Ops:
  0.0 1.3 %shard_map.74 = bf16[256,2048]{1,0:T(8,128)(2,1)S(1)} custom-call(bf16[256,4096]{1,0:T(8,128)(2,1)} %bitcast.16), custom_call_target="tpu_custom_call" | custom-call | tf_op jit(solution)/shard_map/pallas_call | solution.py:391
  1.4 3.0 %collective-permute-start.1 = (bf16[256,2048]{1,0:T(8,128)(2,1)S(1)}, bf16[256,2048]{1,0:T(8,128)(2,1)S(1)}, u32[]{:S(2)}, u32[]{:S(2)}) collective-permute-start(bf16[256,2048]{1,0:T(8,128)(2,1)S(1)} %shard_map.74), channel_id=1, source_target_pairs={{0,8},{1,9},{2,10},{3,11},{4,12},{5,13},{6,14},{7,15},{8,0},{9,1},... | collective-permute-start | bytes 3145736 | tf_op jit(solution)/shard_map/ppermute | solution.py:384
  4.4 1.1 %shard_map.75 = (bf16[256,512]{1,0:T(8,128)(2,1)S(1)}, bf16[256,256]{1,0:T(8,128)(2,1)S(1)}, bf16[256,256]{1,0:T(8,128)(2,1)S(1)}) custom-call(bf16[256,1024]{1,0:T(8,128)(2,1)} %w_ref.1), custom_call_target="tpu_custom_call" | custom-call | tf_op jit(solution)/shard_map/pallas_call | solution.py:391
  5.6 1.5 %collective-permute-done.3.swapped_ref.refs_3_ = bf16[256,512]{1,0:T(8,128)(2,1)S(1)} collective-permute-done((bf16[256,512]{1,0:T(8,128)(2,1)S(1)}, bf16[256,512]{1,0:T(8,128)(2,1)S(1)}, u32[]{:S(2)}, u32[]{:S(2)}) %collective-permute-start.3) | collective-permute-done | bytes 262176 | tf_op jit(solution)/shard_map/ppermute | solution.py:384
  7.1 1.6 %collective-permute-start.4 = (bf16[2,256,256]{2,1,0:T(8,128)(2,1)S(1)}, bf16[2,256,256]{2,1,0:T(8,128)(2,1)S(1)}, u32[]{:S(2)}, u32[]{:S(2)}) collective-permute-start(bf16[2,256,256]{2,1,0:T(8,128)(2,1)S(1)} %shard_map.76.refs_2_), channel_id=1, source_target_pairs={{0,1},{1,0},{2,3},{3,2},{4,5},{5,4},{6,7},{7,6},{8,9},{9,8},{10,11... | collective-permute-start | bytes 786440 | tf_op jit(solution)/shard_map/ppermute | solution.py:384
  8.8 2.6 %shard_map.73 = (bf16[256,2048]{1,0:T(8,128)(2,1)S(1)}, f32[512,256]{1,0:T(8,128)S(1)}, bf16[544,256]{1,0:T(8,128)(2,1)S(1)}, f32[16,256]{1,0:T(8,128)S(1)}, f32...) custom-call(bf16[256,1024]{1,0:T(8,128)(2,1)S(1)} %bitcast.6, ...), custom_call_target="tpu_custom_call" | custom-call | tf_op jit(solution)/shard_map/pallas_call | solution.py:391
  12.0 3.5 %collective-permute-done.4.refs_3_ = bf16[2,256,256]{2,1,0:T(8,128)(2,1)S(1)} collective-permute-done((bf16[2,256,256]{2,1,0:T(8,128)(2,1)S(1)}, bf16[2,256,256]{2,1,0:T(8,128)(2,1)S(1)}, u32[]{:S(2)}, u32[]{:S(2)}) %collective-permute-start.4) | collective-permute-done | bytes 262176 | tf_op jit(solution)/shard_map/ppermute | solution.py:384
  15.5 12.0 %collective-permute-done.1.refs_0_ = bf16[256,2048]{1,0:T(8,128)(2,1)S(1)} collective-permute-done((bf16[256,2048]{1,0:T(8,128)(2,1)S(1)}, bf16[256,2048]{1,0:T(8,128)(2,1)S(1)}, u32[]{:S(2)}, u32[]{:S(2)}) %collective-permute-start.1) | collective-permute-done | bytes 1048608 | tf_op jit(solution)/shard_map/ppermute | solution.py:384
  27.6 1.9 %collective-permute-start.7 = (bf16[544,256]{1,0:T(8,128)(2,1)S(1)}, bf16[544,256]{1,0:T(8,128)(2,1)S(1)}, u32[]{:S(2)}, u32[]{:S(2)}) collective-permute-start(bf16[544,256]{1,0:T(8,128)(2,1)S(1)} %shard_map.77), channel_id=1, source_target_pairs={{0,1},{1,0},{2,3},{3,2},{4,5},{5,4},{6,7},{7,6},{8,9},{9,8},{10,11... | collective-permute-start | bytes 835592 | tf_op jit(solution)/shard_map/ppermute | solution.py:384
  29.8 7.4 %collective-permute-done.7.outer_ref.prev_ref.refs_8_ = bf16[544,256]{1,0:T(8,128)(2,1)S(1)} collective-permute-done((bf16[544,256]{1,0:T(8,128)(2,1)S(1)}, bf16[544,256]{1,0:T(8,128)(2,1)S(1)}, u32[]{:S(2)}, u32[]{:S(2)}) %collective-permute-start.7) | collective-permute-done | bytes 278560 | tf_op jit(solution)/shard_map/ppermute | solution.py:384
  37.3 5.5 %collective-permute-done.10.outer_ref.prev_ref.refs_8_ = bf16[544,256]{1,0:T(8,128)(2,1)S(1)} collective-permute-done((bf16[544,256]{1,0:T(8,128)(2,1)S(1)}, bf16[544,256]{1,0:T(8,128)(2,1)S(1)}, u32[]{:S(2)}, u32[]{:S(2)}) %collective-permute-start.10) | collective-permute-done | bytes 278560 | tf_op jit(solution)/shard_map/ppermute | solution.py:384
  43.5 1.7 %collective-permute-start.5 = (bf16[2,256,256]{2,1,0:T(8,128)(2,1)S(1)}, bf16[2,256,256]{2,1,0:T(8,128)(2,1)S(1)}, u32[]{:S(2)}, u32[]{:S(2)}) collective-permute-start(bf16[2,256,256]{2,1,0:T(8,128)(2,1)S(1)} %collective-permute-done.4.refs_3_), channel_id=1, source_target_pairs={{0,16},{1,17},{2,18},{3,19},{4,20},{5,21},{6,22},{7,23},{8,24},{9,... | collective-permute-start | bytes 786440 | tf_op jit(solution)/shard_map/ppermute | solution.py:384
  45.6 1.8 %collective-permute-start.11 = (bf16[2,256,256]{2,1,0:T(8,128)(2,1)S(1)}, bf16[2,256,256]{2,1,0:T(8,128)(2,1)S(1)}, u32[]{:S(2)}, u32[]{:S(2)}) collective-permute-start(bf16[2,256,256]{2,1,0:T(8,128)(2,1)S(1)} %shard_map.80.refs_5_), channel_id=1, source_target_pairs={{0,16},{1,17},{2,18},{3,19},{4,20},{5,21},{6,22},{7,23},{8,24},{9,... | collective-permute-start | bytes 786440 | tf_op jit(solution)/shard_map/ppermute | solution.py:384
  47.5 0.8 %shard_map.86 = (bf16[256,256]{1,0:T(8,128)(2,1)S(1)}, bf16[256,256]{1,0:T(8,128)(2,1)S(1)}, bf16[2048,256]{1,0:T(8,128)(2,1)S(1)}) custom-call(bf16[256,2048]{1,0:T(8,128)(2,1)S(1)} %collective-permute-done.1.refs_0_, bf16[256,2048]{1,0:T(8,128)(2,1)S(1)} %collective-permute-done.2.refs_1_, bf16[2,256,256]{2,1,0:T(8,128)(2,1)S(1)} %shard_map.76.refs_2_, ...), custom_call_target="tpu_custom_call" | custom-call | tf_op jit(solution)/shard_map/pallas_call | solution.py:391
  49.0 3.6 %collective-permute-done.5.refs_4_ = bf16[2,256,256]{2,1,0:T(8,128)(2,1)S(1)} collective-permute-done((bf16[2,256,256]{2,1,0:T(8,128)(2,1)S(1)}, bf16[2,256,256]{2,1,0:T(8,128)(2,1)S(1)}, u32[]{:S(2)}, u32[]{:S(2)}) %collective-permute-start.5) | collective-permute-done | bytes 262176 | tf_op jit(solution)/shard_map/ppermute | solution.py:384
  52.7 5.6 %collective-permute-done.8.refs_5_ = bf16[2,256,256]{2,1,0:T(8,128)(2,1)S(1)} collective-permute-done((bf16[2,256,256]{2,1,0:T(8,128)(2,1)S(1)}, bf16[2,256,256]{2,1,0:T(8,128)(2,1)S(1)}, u32[]{:S(2)}, u32[]{:S(2)}) %collective-permute-start.8) | collective-permute-done | bytes 262176 | tf_op jit(solution)/shard_map/ppermute | solution.py:384
  58.3 1.7 %collective-permute-start.17 = (bf16[256,256]{1,0:T(8,128)(2,1)S(1)}, bf16[256,256]{1,0:T(8,128)(2,1)S(1)}, u32[]{:S(2)}, u32[]{:S(2)}) collective-permute-start(bf16[256,256]{1,0:T(8,128)(2,1)S(1)} %get-tuple-element.46), channel_id=1, source_target_pairs={{0,8},{1,9},{2,10},{3,11},{4,12},{5,13},{6,14},{7,15},{8,0},{9,1},... | collective-permute-start | bytes 393224 | tf_op jit(solution)/shard_map/ppermute | solution.py:384
  59.9 3.1 %collective-permute-done.11.refs_6_ = bf16[2,256,256]{2,1,0:T(8,128)(2,1)S(1)} collective-permute-done((bf16[2,256,256]{2,1,0:T(8,128)(2,1)S(1)}, bf16[2,256,256]{2,1,0:T(8,128)(2,1)S(1)}, u32[]{:S(2)}, u32[]{:S(2)}) %collective-permute-start.11) | collective-permute-done | bytes 262176 | tf_op jit(solution)/shard_map/ppermute | solution.py:384
  65.0 1.4 %collective-permute-start.13 = (f32[256,256]{1,0:T(8,128)S(1)}, f32[256,256]{1,0:T(8,128)S(1)}, u32[]{:S(2)}, u32[]{:S(2)}) collective-permute-start(f32[256,256]{1,0:T(8,128)S(1)} %get-tuple-element.38), channel_id=1, source_target_pairs={{0,4},{1,5},{2,6},{3,7},{4,0},{5,1},{6,2},{7,3},{8,12},{9,13},{10,... | collective-permute-start | bytes 786440 | tf_op jit(solution)/shard_map/ppermute | solution.py:384
  66.7 1.9 %collective-permute-done.19.refs_3_ = bf16[256,256]{1,0:T(8,128)(2,1)S(1)} collective-permute-done((bf16[256,256]{1,0:T(8,128)(2,1)S(1)}, bf16[256,256]{1,0:T(8,128)(2,1)S(1)}, u32[]{:S(2)}, u32[]{:S(2)}) %collective-permute-start.19) | collective-permute-done | bytes 131104 | tf_op jit(solution)/shard_map/ppermute | solution.py:384
  69.0 1.1 %shard_map.83 = (f32[2,256,256]{2,1,0:T(8,128)S(1)}, f32[2,256,128]{2,1,0:T(8,128)S(1)}, f32[2,256,256]{2,1,0:T(8,128)S(1)}, f32[2,256,128]{2,1,0:T(8,128)S(1)}) custom-call(f32[4,256]{1,0:T(4,128)S(1)} %bitcast.13, f32[4,256]{1,0:T(4,128)S(1)} %bitcast.15, s32[1,256]{1,0:T(1,128)S(1)} %copy-done.4), custom_call_target="tpu_custom_call" | custom-call | tf_op jit(solution)/shard_map/pallas_call | solution.py:391
  70.1 2.0 %shard_map.90.refs_11_ = bf16[256,1024]{1,0:T(8,128)(2,1)} custom-call(f32[256,256]{1,0:T(8,128)S(1)} %get-tuple-element.45.refs_0_, bf16[256,256]{1,0:T(8,128)(2,1)S(1)} %collective-permute-done.17.refs_1_, f32[256,256]{1,0:T(8,128)S(1)} %collective-permute-done.18.refs_2_, bf16[256,256]{1,0:T(8,128)(2,1)S(1)} %collective-permute-done.19.refs_3_, ...), custom_call_target="tpu_custom_call" | custom-call | tf_op jit(solution)/shard_map/pallas_call | solution.py:391
  72.1 2.2 %collective-permute-done.14.refs_3_ = bf16[256,256]{1,0:T(8,128)(2,1)S(1)} collective-permute-done((bf16[256,256]{1,0:T(8,128)(2,1)S(1)}, bf16[256,256]{1,0:T(8,128)(2,1)S(1)}, u32[]{:S(2)}, u32[]{:S(2)}) %collective-permute-start.14) | collective-permute-done | bytes 131104 | tf_op jit(solution)/shard_map/ppermute | solution.py:384
  74.4 2.0 %shard_map.91 = bf16[256,1024]{1,0:T(8,128)(2,1)} custom-call(f32[256,256]{1,0:T(8,128)S(1)} %get-tuple-element.36.refs_0_, bf16[256,256]{1,0:T(8,128)(2,1)S(1)} %collective-permute-done.12.refs_1_, f32[256,256]{1,0:T(8,128)S(1)} %collective-permute-done.13.refs_2_, ...), custom_call_target="tpu_custom_call", output_to_operand_aliasing={{}: (11, {})} | custom-call | tf_op jit(solution)/shard_map/pallas_call | solution.py:391
  (49 shorter events, 5.7 us)
Async XLA Ops:
  0.0 8.8 %copy-start.3 = (f32[1,4,256]{2,1,0:T(4,128)S(1)}, f32[1,4,256]{2,1,0:T(4,128)}, u32[]{:S(2)}) copy-start(f32[1,4,256]{2,1,0:T(4,128)} %param.12) | copy-start | bytes 12292
  0.0 8.8 %copy-start.4 = (s32[1,256]{1,0:T(1,128)S(1)}, s32[1,256]{1,0:T(1,128)}, u32[]{:S(2)}) copy-start(s32[1,256]{1,0:T(1,128)} %reset_ref.1) | copy-start | bytes 3076
  1.4 26.2 %collective-permute-start.1 = (bf16[256,2048]{1,0:T(8,128)(2,1)S(1)}, bf16[256,2048]{1,0:T(8,128)(2,1)S(1)}, u32[]{:S(2)}, u32[]{:S(2)}) collective-permute-start(bf16[256,2048]{1,0:T(8,128)(2,1)S(1)} %shard_map.74), channel_id=1, source_target_pairs={{0,8},{1,9},{2,10},{3,11},{4,12},{5,13},{6,14},{7,15},{8,0},{9,1},... | collective-permute-start | bytes 3145736 | tf_op jit(solution)/shard_map/ppermute | solution.py:384
  5.5 1.6 %collective-permute-start.3 = (bf16[256,512]{1,0:T(8,128)(2,1)S(1)}, bf16[256,512]{1,0:T(8,128)(2,1)S(1)}, u32[]{:S(2)}, u32[]{:S(2)}) collective-permute-start(bf16[256,512]{1,0:T(8,128)(2,1)S(1)} %get-tuple-element.31), channel_id=1, source_target_pairs={{0,4},{1,5},{2,6},{3,7},{4,0},{5,1},{6,2},{7,3},{8,12},{9,13},{10,... | collective-permute-start | bytes 786440 | tf_op jit(solution)/shard_map/ppermute | solution.py:384
  7.1 8.4 %collective-permute-start.4 = (bf16[2,256,256]{2,1,0:T(8,128)(2,1)S(1)}, bf16[2,256,256]{2,1,0:T(8,128)(2,1)S(1)}, u32[]{:S(2)}, u32[]{:S(2)}) collective-permute-start(bf16[2,256,256]{2,1,0:T(8,128)(2,1)S(1)} %shard_map.76.refs_2_), channel_id=1, source_target_pairs={{0,1},{1,0},{2,3},{3,2},{4,5},{5,4},{6,7},{7,6},{8,9},{9,8},{10,11... | collective-permute-start | bytes 786440 | tf_op jit(solution)/shard_map/ppermute | solution.py:384
  11.4 33.8 %collective-permute-start = (bf16[256,2048]{1,0:T(8,128)(2,1)S(1)}, bf16[256,2048]{1,0:T(8,128)(2,1)S(1)}, u32[]{:S(2)}, u32[]{:S(2)}) collective-permute-start(bf16[256,2048]{1,0:T(8,128)(2,1)S(1)} %get-tuple-element.29.refs_0_), channel_id=1, source_target_pairs={{0,4},{1,5},{2,6},{3,7},{4,0},{5,1},{6,2},{7,3},{8,12},{9,13},{10,... | collective-permute-start | bytes 3145736 | tf_op jit(solution)/shard_map/ppermute | solution.py:384
  11.5 16.1 %collective-permute-start.6 = (bf16[2,256,256]{2,1,0:T(8,128)(2,1)S(1)}, bf16[2,256,256]{2,1,0:T(8,128)(2,1)S(1)}, u32[]{:S(2)}, u32[]{:S(2)}) collective-permute-start(bf16[2,256,256]{2,1,0:T(8,128)(2,1)S(1)} %shard_map.76.refs_2_), channel_id=1, source_target_pairs={{0,4},{1,2},{2,1},{3,7},{4,0},{5,6},{6,5},{7,3},{8,12},{9,10},{10,... | collective-permute-start | bytes 786440 | tf_op jit(solution)/shard_map/ppermute | solution.py:384
  15.5 14.0 %collective-permute-start.9 = (bf16[2,256,256]{2,1,0:T(8,128)(2,1)S(1)}, bf16[2,256,256]{2,1,0:T(8,128)(2,1)S(1)}, u32[]{:S(2)}, u32[]{:S(2)}) collective-permute-start(bf16[2,256,256]{2,1,0:T(8,128)(2,1)S(1)} %collective-permute-done.4.refs_3_), channel_id=1, source_target_pairs={{0,4},{1,2},{2,1},{3,7},{4,0},{5,6},{6,5},{7,3},{8,12},{9,10},{10,... | collective-permute-start | bytes 786440 | tf_op jit(solution)/shard_map/ppermute | solution.py:384
  27.6 19.8 %collective-permute-start.2 = (bf16[256,2048]{1,0:T(8,128)(2,1)S(1)}, bf16[256,2048]{1,0:T(8,128)(2,1)S(1)}, u32[]{:S(2)}, u32[]{:S(2)}) collective-permute-start(bf16[256,2048]{1,0:T(8,128)(2,1)S(1)} %collective-permute-done.1.refs_0_), channel_id=1, source_target_pairs={{0,4},{1,5},{2,6},{3,7},{4,0},{5,1},{6,2},{7,3},{8,12},{9,13},{10,... | collective-permute-start | bytes 3145736 | tf_op jit(solution)/shard_map/ppermute | solution.py:384
  27.6 9.6 %collective-permute-start.7 = (bf16[544,256]{1,0:T(8,128)(2,1)S(1)}, bf16[544,256]{1,0:T(8,128)(2,1)S(1)}, u32[]{:S(2)}, u32[]{:S(2)}) collective-permute-start(bf16[544,256]{1,0:T(8,128)(2,1)S(1)} %shard_map.77), channel_id=1, source_target_pairs={{0,1},{1,0},{2,3},{3,2},{4,5},{5,4},{6,7},{7,6},{8,9},{9,8},{10,11... | collective-permute-start | bytes 835592 | tf_op jit(solution)/shard_map/ppermute | solution.py:384
  29.5 13.3 %collective-permute-start.10 = (bf16[544,256]{1,0:T(8,128)(2,1)S(1)}, bf16[544,256]{1,0:T(8,128)(2,1)S(1)}, u32[]{:S(2)}, u32[]{:S(2)}) collective-permute-start(bf16[544,256]{1,0:T(8,128)(2,1)S(1)} %shard_map.79), channel_id=1, source_target_pairs={{0,1},{1,0},{2,3},{3,2},{4,5},{5,4},{6,7},{7,6},{8,9},{9,8},{10,11... | collective-permute-start | bytes 835592 | tf_op jit(solution)/shard_map/ppermute | solution.py:384
  37.2 5.7 %collective-permute-start.20 = (bf16[544,256]{1,0:T(8,128)(2,1)S(1)}, bf16[544,256]{1,0:T(8,128)(2,1)S(1)}, u32[]{:S(2)}, u32[]{:S(2)}) collective-permute-start(bf16[544,256]{1,0:T(8,128)(2,1)S(1)} %shard_map.88), channel_id=1, source_target_pairs={{0,4},{1,2},{2,1},{3,7},{4,0},{5,6},{6,5},{7,3},{8,12},{9,10},{10,... | collective-permute-start | bytes 835592 | tf_op jit(solution)/shard_map/ppermute | solution.py:384
  42.8 2.8 %collective-permute-start.15 = (bf16[544,256]{1,0:T(8,128)(2,1)S(1)}, bf16[544,256]{1,0:T(8,128)(2,1)S(1)}, u32[]{:S(2)}, u32[]{:S(2)}) collective-permute-start(bf16[544,256]{1,0:T(8,128)(2,1)S(1)} %shard_map.84), channel_id=1, source_target_pairs={{0,4},{1,2},{2,1},{3,7},{4,0},{5,6},{6,5},{7,3},{8,12},{9,10},{10,... | collective-permute-start | bytes 835592 | tf_op jit(solution)/shard_map/ppermute | solution.py:384
  42.9 22.1 %collective-permute-start.21 = (bf16[544,256]{1,0:T(8,128)(2,1)S(1)}, bf16[544,256]{1,0:T(8,128)(2,1)S(1)}, u32[]{:S(2)}, u32[]{:S(2)}) collective-permute-start(bf16[544,256]{1,0:T(8,128)(2,1)S(1)} %shard_map.89), channel_id=1, source_target_pairs={{0,4},{1,5},{2,3},{3,2},{4,0},{5,1},{6,7},{7,6},{8,12},{9,13},{10,... | collective-permute-start | bytes 835592 | tf_op jit(solution)/shard_map/ppermute | solution.py:384
  43.5 9.2 %collective-permute-start.5 = (bf16[2,256,256]{2,1,0:T(8,128)(2,1)S(1)}, bf16[2,256,256]{2,1,0:T(8,128)(2,1)S(1)}, u32[]{:S(2)}, u32[]{:S(2)}) collective-permute-start(bf16[2,256,256]{2,1,0:T(8,128)(2,1)S(1)} %collective-permute-done.4.refs_3_), channel_id=1, source_target_pairs={{0,16},{1,17},{2,18},{3,19},{4,20},{5,21},{6,22},{7,23},{8,24},{9,... | collective-permute-start | bytes 786440 | tf_op jit(solution)/shard_map/ppermute | solution.py:384
  45.2 13.1 %collective-permute-start.8 = (bf16[2,256,256]{2,1,0:T(8,128)(2,1)S(1)}, bf16[2,256,256]{2,1,0:T(8,128)(2,1)S(1)}, u32[]{:S(2)}, u32[]{:S(2)}) collective-permute-start(bf16[2,256,256]{2,1,0:T(8,128)(2,1)S(1)} %shard_map.78.refs_4_), channel_id=1, source_target_pairs={{0,16},{1,17},{2,18},{3,19},{4,20},{5,21},{6,22},{7,23},{8,24},{9,... | collective-permute-start | bytes 786440 | tf_op jit(solution)/shard_map/ppermute | solution.py:384
  45.6 17.4 %collective-permute-start.11 = (bf16[2,256,256]{2,1,0:T(8,128)(2,1)S(1)}, bf16[2,256,256]{2,1,0:T(8,128)(2,1)S(1)}, u32[]{:S(2)}, u32[]{:S(2)}) collective-permute-start(bf16[2,256,256]{2,1,0:T(8,128)(2,1)S(1)} %shard_map.80.refs_5_), channel_id=1, source_target_pairs={{0,16},{1,17},{2,18},{3,19},{4,20},{5,21},{6,22},{7,23},{8,24},{9,... | collective-permute-start | bytes 786440 | tf_op jit(solution)/shard_map/ppermute | solution.py:384
  47.4 24.7 %collective-permute-start.16 = (bf16[544,256]{1,0:T(8,128)(2,1)S(1)}, bf16[544,256]{1,0:T(8,128)(2,1)S(1)}, u32[]{:S(2)}, u32[]{:S(2)}) collective-permute-start(bf16[544,256]{1,0:T(8,128)(2,1)S(1)} %shard_map.85), channel_id=1, source_target_pairs={{0,4},{1,5},{2,3},{3,2},{4,0},{5,1},{6,7},{7,6},{8,12},{9,13},{10,... | collective-permute-start | bytes 835592 | tf_op jit(solution)/shard_map/ppermute | solution.py:384
  52.6 17.4 %collective-permute-start.18 = (f32[256,256]{1,0:T(8,128)S(1)}, f32[256,256]{1,0:T(8,128)S(1)}, u32[]{:S(2)}, u32[]{:S(2)}) collective-permute-start(f32[256,256]{1,0:T(8,128)S(1)} %get-tuple-element.47), channel_id=1, source_target_pairs={{0,4},{1,5},{2,6},{3,7},{4,0},{5,1},{6,2},{7,3},{8,12},{9,13},{10,... | collective-permute-start | bytes 786440 | tf_op jit(solution)/shard_map/ppermute | solution.py:384
  58.3 8.1 %collective-permute-start.17 = (bf16[256,256]{1,0:T(8,128)(2,1)S(1)}, bf16[256,256]{1,0:T(8,128)(2,1)S(1)}, u32[]{:S(2)}, u32[]{:S(2)}) collective-permute-start(bf16[256,256]{1,0:T(8,128)(2,1)S(1)} %get-tuple-element.46), channel_id=1, source_target_pairs={{0,8},{1,9},{2,10},{3,11},{4,12},{5,13},{6,14},{7,15},{8,0},{9,1},... | collective-permute-start | bytes 393224 | tf_op jit(solution)/shard_map/ppermute | solution.py:384
  63.0 5.6 %collective-permute-start.19 = (bf16[256,256]{1,0:T(8,128)(2,1)S(1)}, bf16[256,256]{1,0:T(8,128)(2,1)S(1)}, u32[]{:S(2)}, u32[]{:S(2)}) collective-permute-start(bf16[256,256]{1,0:T(8,128)(2,1)S(1)} %get-tuple-element.48), channel_id=1, source_target_pairs={{0,12},{1,13},{2,14},{3,15},{4,8},{5,9},{6,10},{7,11},{8,4},{9,5},... | collective-permute-start | bytes 393224 | tf_op jit(solution)/shard_map/ppermute | solution.py:384
  65.0 9.4 %collective-permute-start.13 = (f32[256,256]{1,0:T(8,128)S(1)}, f32[256,256]{1,0:T(8,128)S(1)}, u32[]{:S(2)}, u32[]{:S(2)}) collective-permute-start(f32[256,256]{1,0:T(8,128)S(1)} %get-tuple-element.38), channel_id=1, source_target_pairs={{0,4},{1,5},{2,6},{3,7},{4,0},{5,1},{6,2},{7,3},{8,12},{9,13},{10,... | collective-permute-start | bytes 786440 | tf_op jit(solution)/shard_map/ppermute | solution.py:384
  66.4 5.8 %collective-permute-start.12 = (bf16[256,256]{1,0:T(8,128)(2,1)S(1)}, bf16[256,256]{1,0:T(8,128)(2,1)S(1)}, u32[]{:S(2)}, u32[]{:S(2)}) collective-permute-start(bf16[256,256]{1,0:T(8,128)(2,1)S(1)} %get-tuple-element.37), channel_id=1, source_target_pairs={{0,8},{1,9},{2,10},{3,11},{4,12},{5,13},{6,14},{7,15},{8,0},{9,1},... | collective-permute-start | bytes 393224 | tf_op jit(solution)/shard_map/ppermute | solution.py:384
  68.6 5.8 %collective-permute-start.14 = (bf16[256,256]{1,0:T(8,128)(2,1)S(1)}, bf16[256,256]{1,0:T(8,128)(2,1)S(1)}, u32[]{:S(2)}, u32[]{:S(2)}) collective-permute-start(bf16[256,256]{1,0:T(8,128)(2,1)S(1)} %get-tuple-element.39), channel_id=1, source_target_pairs={{0,12},{1,13},{2,14},{3,15},{4,8},{5,9},{6,10},{7,11},{8,4},{9,5},... | collective-permute-start | bytes 393224 | tf_op jit(solution)/shard_map/ppermute | solution.py:384
  (3 other events, 26.3 us)
